TPU v7x, 32 devices: a whole 2x2x4 slice. The times are simulated.
32 devices in a mesh: dp: 4 (over y, x), tm: 4 (over z), rows: 2 (over core).
Axes of the slice: x: 2, y: 2, z: 4, core: 2. Of those that a mesh axis runs over, the one named last changes fastest.
Arguments:
- latents: bfloat16 [4, 8, 8, 32, 384], P('dp', 'tm', 'rows'), may hold values from -6 to 6
- hidden: bfloat16 [4, 8, 8, 32, 384], P('dp', 'tm', 'rows'), may hold values from -8 to 8
- cotangent: bfloat16 [4, 8, 8, 32, 384], P('dp', 'tm', 'rows'), may hold values from -6 to 6
- conv_one: bfloat16 [3, 3, 3, 384, 384], replicated, may hold values from -0.0625 to 0.0625
- conv_two: bfloat16 [3, 3, 3, 384, 384], replicated, may hold values from -0.0625 to 0.0625
- lengths: int32 [4], P('dp'), may hold values from 3 to 8, as said below
Outputs:
- latent_grad: float32 [4, 8, 8, 32, 384], P('dp', None, None, ('tm', 'rows'))
Inputs may be any that keep to these rules, and one draw needn't show every extreme that they name: `lengths`: at least one clip has all 8 frames valid.
All inputs are finite; a program needn't handle non-finite values.
Results may differ from a plain program's by a relative error of at most 0.00092.
Values may be sent and summed in bfloat16 or wider, within the bound.
No kernel may reach another device: no remote copies, remote signals or barrier semaphores. Data moves between devices by JAX's collectives and lax.ppermute only.
A program may use at most 64 MiB of HBM per device.

v0:
```python
import jax
import jax.numpy as jnp
from jax import lax
from jax.sharding import PartitionSpec as P


def with_halo(block, sides, width):
    for axis, dim in sides:
        count = lax.axis_size(axis)
        forward = [(i, i + 1) for i in range(count - 1)]
        backward = [(target, source) for source, target in forward]
        low = lax.ppermute(
            lax.slice_in_dim(block, block.shape[dim] - width, None, axis=dim), axis, forward
        )
        high = lax.ppermute(lax.slice_in_dim(block, 0, width, axis=dim), axis, backward)
        block = jnp.concatenate([low, block, high], axis=dim)
    return block


def shifted(value, axis, by):
    devices = lax.axis_size(axis)
    pairs = [(i, i + by) for i in range(devices) if 0 <= i + by < devices]
    return lax.ppermute(value, axis, pairs)


def silu_slope(values):
    sigmoid_of = jax.nn.sigmoid(values)
    return sigmoid_of * (1.0 + values * (1.0 - sigmoid_of))


def extended(row_band, next_frames):
    joined = jnp.concatenate([row_band, next_frames], axis=0)
    return jnp.pad(joined, ((0, 0), (0, 0), (1, 1), (0, 0)))


def transposed_conv(padded, kernel, frame_count, row_count, col_count):
    summed = jnp.zeros((frame_count, row_count, col_count, kernel.shape[4]), jnp.float32)
    for time_tap in range(3):
        for row_tap in range(3):
            slab_rows = padded[time_tap : time_tap + frame_count, row_tap : row_tap + row_count]
            stacked = jnp.stack(
                [slab_rows[:, :, col_tap : col_tap + col_count] for col_tap in range(3)], axis=3
            )
            kernel_slice = kernel[2 - time_tap, 2 - row_tap, ::-1]
            summed = summed + jnp.einsum(
                "frwkc,kdc->frwd", stacked, kernel_slice, preferred_element_type=jnp.float32
            )
    return summed


def on_device(latents, hidden, cotangent, conv_one, conv_two, lengths):
    frame_dev = latents.shape[1]
    row_dev = latents.shape[2]
    col_count = latents.shape[3]
    channels = latents.shape[4]
    first_frame = lax.axis_index("tm") * frame_dev
    frames = first_frame + jnp.arange(frame_dev, dtype=jnp.int32)
    live_frames = frames < lengths[0]
    masked = jnp.where(live_frames[:, None, None, None], cotangent[0], jnp.zeros_like(cotangent[0]))
    cot_band = with_halo(masked, (("rows", 1),), 1)
    cot_next = shifted(cot_band, "tm", -1)
    grad_act = transposed_conv(
        extended(cot_band, cot_next), conv_two, frame_dev, row_dev, col_count
    )
    grad_hidden = (grad_act * silu_slope(hidden[0].astype(jnp.float32))).astype(jnp.bfloat16)
    hidden_band = with_halo(grad_hidden, (("rows", 1),), 1)
    hidden_next = shifted(hidden_band, "tm", -1)
    grad_input = transposed_conv(
        extended(hidden_band, hidden_next), conv_one, frame_dev, row_dev, col_count
    )
    result = masked.astype(jnp.float32) + grad_input * silu_slope(latents[0].astype(jnp.float32))
    result = result[None]
    time_devs = lax.axis_size("tm")
    row_devs = lax.axis_size("rows")
    arrived = lax.all_to_all(
        result[:, None], ("tm", "rows"), split_axis=4, concat_axis=1, tiled=True
    )
    col_dev = arrived.shape[4]
    arranged = arrived.reshape(1, time_devs, row_devs, frame_dev, row_dev, col_dev, channels)
    arranged = arranged.transpose(0, 1, 3, 2, 4, 5, 6)
    return arranged.reshape(1, time_devs * frame_dev, row_devs * row_dev, col_dev, channels)


def solution(mesh):
    in_specs = (
        P("dp", "tm", "rows", None, None),
        P("dp", "tm", "rows", None, None),
        P("dp", "tm", "rows", None, None),
        P(),
        P(),
        P("dp"),
    )
    out_specs = P("dp", None, None, ("tm", "rows"), None)
    return jax.shard_map(
        on_device, mesh=mesh, in_specs=in_specs, out_specs=out_specs, check_vma=False
    )
```

profile of v0, /device:TPU:0, one launch (start us, length us, event | category | flops | bytes accessed | tf_op | source)
XLA Modules:
  0.0 96.8 jit_solution(17803353701645760821)
XLA Ops:
  0.7 1.0 %bitcast_select_fusion.1 = bf16[2,4,32,384]{3,2,1,0:T(8,128)(2,1)S(1)} fusion(bf16[1,2,4,32,384]{4,3,2,1,0:T(8,128)(2,1)} %param.8, pred[2]{0:T(512)(128)(4,1)S(1)} %add_compare_fusion), kind=kLoop, calls=%fused_computation.207 | loop fusion | flops 98304 | bytes 393218 | tf_op jit(solution)/shard_map/jit(_where)/select_n | solution.py:59
  1.7 2.4 %collective-permute-start = (bf16[2,1,32,384]{3,2,1,0:T(8,128)(2,1)S(1)}, bf16[2,1,32,384]{3,2,1,0:T(8,128)(2,1)S(1)}, u32[]{:S(2)}, u32[]{:S(2)}) collective-permute-start(bf16[2,1,32,384]{3,2,1,0:T(8,128)(2,1)S(1)} %get-tuple-element.77), channel_id=1, source_target_pairs={{0,1},{2,3},{4,5},{6,7},{8,9},{10,11},{12,13},{14,15},{16,17},{18,... | collective-permute-start | bytes 147464 | tf_op jit(solution)/shard_map/ppermute | solution.py:12
  4.1 1.3 %collective-permute-start.1 = (bf16[2,1,32,384]{3,2,1,0:T(8,128)(2,1)S(1)}, bf16[2,1,32,384]{3,2,1,0:T(8,128)(2,1)S(1)}, u32[]{:S(2)}, u32[]{:S(2)}) collective-permute-start(bf16[2,1,32,384]{3,2,1,0:T(8,128)(2,1)S(1)} %get-tuple-element.78), channel_id=1, source_target_pairs={{1,0},{3,2},{5,4},{7,6},{9,8},{11,10},{13,12},{15,14},{17,16},{19,... | collective-permute-start | bytes 147464 | tf_op jit(solution)/shard_map/ppermute | solution.py:15
  5.4 5.3 %fusion.122 = (bf16[1,1,3,384,384]{4,3,2,1,0:T(8,128)(2,1)}, bf16[1,1,3,384,384]{4,3,2,1,0:T(8,128)(2,1)S(1)}, bf16[1,1,3,384,384]{4,3,2,1,0:T(8,128)(2,1)S(1)},...) fusion(bf16[3,3,3,384,384]{4,3,2,1,0:T(8,128)(2,1)} %param.10), kind=kLoop, calls=%fused_computation.211 | loop fusion | bytes 15925248 | tf_op jit(solution)/shard_map/slice | solution.py:44
  10.7 2.2 %rev.55 = bf16[1,1,3,384,384]{4,3,2,1,0:T(8,128)(2,1)} reverse(bf16[1,1,3,384,384]{4,3,2,1,0:T(8,128)(2,1)} %get-tuple-element.14), dimensions={2} | reverse | bytes 1769472 | tf_op jit(solution)/shard_map/rev | solution.py:44
  12.9 2.2 %rev.56 = bf16[1,1,3,384,384]{4,3,2,1,0:T(8,128)(2,1)} reverse(bf16[1,1,3,384,384]{4,3,2,1,0:T(8,128)(2,1)} %get-tuple-element.19), dimensions={2} | reverse | bytes 1769472 | tf_op jit(solution)/shard_map/rev | solution.py:44
  15.1 2.2 %rev.57 = bf16[1,1,3,384,384]{4,3,2,1,0:T(8,128)(2,1)} reverse(bf16[1,1,3,384,384]{4,3,2,1,0:T(8,128)(2,1)} %get-tuple-element.18), dimensions={2} | reverse | bytes 1769472 | tf_op jit(solution)/shard_map/rev | solution.py:44
  17.3 2.2 %rev.58 = bf16[1,1,3,384,384]{4,3,2,1,0:T(8,128)(2,1)} reverse(bf16[1,1,3,384,384]{4,3,2,1,0:T(8,128)(2,1)} %get-tuple-element.17), dimensions={2} | reverse | bytes 1769472 | tf_op jit(solution)/shard_map/rev | solution.py:44
  19.5 1.0 %rev.59 = bf16[1,1,3,384,384]{4,3,2,1,0:T(8,128)(2,1)} reverse(bf16[1,1,3,384,384]{4,3,2,1,0:T(8,128)(2,1)S(1)} %get-tuple-element.16), dimensions={2} | reverse | bytes 1769472 | tf_op jit(solution)/shard_map/rev | solution.py:44
  20.5 0.1 rev.60
  20.6 0.1 rev.61
  20.7 1.3 %rev.62 = bf16[1,1,3,384,384]{4,3,2,1,0:T(8,128)(2,1)S(1)} reverse(bf16[1,1,3,384,384]{4,3,2,1,0:T(8,128)(2,1)} %get-tuple-element.21), dimensions={2} | reverse | bytes 1769472 | tf_op jit(solution)/shard_map/rev | solution.py:44
  22.0 2.2 %rev.54 = bf16[1,1,3,384,384]{4,3,2,1,0:T(8,128)(2,1)} reverse(bf16[1,1,3,384,384]{4,3,2,1,0:T(8,128)(2,1)} %get-tuple-element.20), dimensions={2} | reverse | bytes 1769472 | tf_op jit(solution)/shard_map/rev | solution.py:44
  24.2 1.4 %collective-permute-start.2 = (bf16[2,6,32,384]{3,2,1,0:T(8,128)(2,1)S(1)}, bf16[2,6,32,384]{3,2,1,0:T(8,128)(2,1)S(1)}, u32[]{:S(2)}, u32[]{:S(2)}) collective-permute-start(bf16[2,6,32,384]{3,2,1,0:T(8,128)(2,1)S(1)} %pad_maximum_fusion.19), channel_id=1, source_target_pairs={{2,0},{4,2},{6,4},{3,1},{5,3},{7,5},{10,8},{12,10},{14,12},{11,9},... | collective-permute-start | bytes 884744 | tf_op jit(solution)/shard_map/ppermute | solution.py:23
  25.7 0.1 bitcast_select_fusion
  25.8 10.3 %collective-permute-done.2 = bf16[2,6,32,384]{3,2,1,0:T(8,128)(2,1)S(1)} collective-permute-done((bf16[2,6,32,384]{3,2,1,0:T(8,128)(2,1)S(1)}, bf16[2,6,32,384]{3,2,1,0:T(8,128)(2,1)S(1)}, u32[]{:S(2)}, u32[]{:S(2)}) %collective-permute-start.2) | collective-permute-done | bytes 294944 | tf_op jit(solution)/shard_map/ppermute | solution.py:23
  36.1 0.1 pad_maximum_fusion
  36.2 0.7 fusion.82
  36.9 0.2 pad_maximum_fusion.1
  37.1 0.5 fusion.42
  37.6 0.5 fusion.40
  38.1 0.2 pad_maximum_fusion.3
  38.3 0.5 fusion.38
  38.8 0.5 fusion.36
  39.3 0.1 slice_bitcast_fusion.8
  39.4 0.2 pad_maximum_fusion.5
  39.5 0.5 fusion.34
  40.0 0.5 fusion.32
  40.5 0.2 pad_maximum_fusion.7
  40.7 0.5 fusion.30
  41.2 0.5 fusion.28
  41.7 0.7 fusion.9
  42.4 2.2 %collective-permute-start.3 = (bf16[2,1,32,384]{3,2,1,0:T(8,128)(2,1)S(1)}, bf16[2,1,32,384]{3,2,1,0:T(8,128)(2,1)S(1)}, u32[]{:S(2)}, u32[]{:S(2)}) collective-permute-start(bf16[2,1,32,384]{3,2,1,0:T(8,128)(2,1)S(1)} %get-tuple-element.73), channel_id=1, source_target_pairs={{0,1},{2,3},{4,5},{6,7},{8,9},{10,11},{12,13},{14,15},{16,17},{18,... | collective-permute-start | bytes 147464 | tf_op jit(solution)/shard_map/ppermute | solution.py:12
  44.6 1.3 %collective-permute-start.4 = (bf16[2,1,32,384]{3,2,1,0:T(8,128)(2,1)S(1)}, bf16[2,1,32,384]{3,2,1,0:T(8,128)(2,1)S(1)}, u32[]{:S(2)}, u32[]{:S(2)}) collective-permute-start(bf16[2,1,32,384]{3,2,1,0:T(8,128)(2,1)S(1)} %get-tuple-element.74), channel_id=1, source_target_pairs={{1,0},{3,2},{5,4},{7,6},{9,8},{11,10},{13,12},{15,14},{17,16},{19,... | collective-permute-start | bytes 147464 | tf_op jit(solution)/shard_map/ppermute | solution.py:15
  45.9 1.8 %collective-permute-done.4 = bf16[2,1,32,384]{3,2,1,0:T(8,128)(2,1)S(1)} collective-permute-done((bf16[2,1,32,384]{3,2,1,0:T(8,128)(2,1)S(1)}, bf16[2,1,32,384]{3,2,1,0:T(8,128)(2,1)S(1)}, u32[]{:S(2)}, u32[]{:S(2)}) %collective-permute-start.4) | collective-permute-done | bytes 49184 | tf_op jit(solution)/shard_map/ppermute | solution.py:15
  47.7 0.8 pad_maximum_fusion.20
  48.5 1.5 %collective-permute-start.5 = (bf16[2,6,32,384]{3,2,1,0:T(8,128)(2,1)}, bf16[2,6,32,384]{3,2,1,0:T(8,128)(2,1)}, u32[]{:S(2)}, u32[]{:S(2)}) collective-permute-start(bf16[2,6,32,384]{3,2,1,0:T(8,128)(2,1)} %pad_maximum_fusion.20), channel_id=1, source_target_pairs={{2,0},{4,2},{6,4},{3,1},{5,3},{7,5},{10,8},{12,10},{14,12},{11,9},... | collective-permute-start | bytes 884744 | tf_op jit(solution)/shard_map/ppermute | solution.py:23
  50.0 2.7 %fusion.121 = (bf16[1,1,3,384,384]{4,3,2,1,0:T(8,128)(2,1)}, bf16[1,1,3,384,384]{4,3,2,1,0:T(8,128)(2,1)S(1)}, bf16[1,1,3,384,384]{4,3,2,1,0:T(8,128)(2,1)S(1)},...) fusion(bf16[3,3,3,384,384]{4,3,2,1,0:T(8,128)(2,1)S(1)} %bitcas, ...), kind=kLoop, calls=%fused_computation.210 | loop fusion | bytes 15925248 | tf_op jit(solution)/shard_map/slice | solution.py:44
  52.7 2.2 %rev.63 = bf16[1,1,3,384,384]{4,3,2,1,0:T(8,128)(2,1)} reverse(bf16[1,1,3,384,384]{4,3,2,1,0:T(8,128)(2,1)} %get-tuple-element.5), dimensions={2} | reverse | bytes 1769472 | tf_op jit(solution)/shard_map/rev | solution.py:44
  54.9 2.2 %rev.64 = bf16[1,1,3,384,384]{4,3,2,1,0:T(8,128)(2,1)} reverse(bf16[1,1,3,384,384]{4,3,2,1,0:T(8,128)(2,1)} %get-tuple-element.11), dimensions={2} | reverse | bytes 1769472 | tf_op jit(solution)/shard_map/rev | solution.py:44
  57.1 2.2 %rev.65 = bf16[1,1,3,384,384]{4,3,2,1,0:T(8,128)(2,1)} reverse(bf16[1,1,3,384,384]{4,3,2,1,0:T(8,128)(2,1)} %get-tuple-element.10), dimensions={2} | reverse | bytes 1769472 | tf_op jit(solution)/shard_map/rev | solution.py:44
  59.3 2.2 %rev.66 = bf16[1,1,3,384,384]{4,3,2,1,0:T(8,128)(2,1)} reverse(bf16[1,1,3,384,384]{4,3,2,1,0:T(8,128)(2,1)} %get-tuple-element.9), dimensions={2} | reverse | bytes 1769472 | tf_op jit(solution)/shard_map/rev | solution.py:44
  61.4 2.2 %rev.67 = bf16[1,1,3,384,384]{4,3,2,1,0:T(8,128)(2,1)} reverse(bf16[1,1,3,384,384]{4,3,2,1,0:T(8,128)(2,1)} %get-tuple-element.8), dimensions={2} | reverse | bytes 1769472 | tf_op jit(solution)/shard_map/rev | solution.py:44
  63.6 1.0 %rev.68 = bf16[1,1,3,384,384]{4,3,2,1,0:T(8,128)(2,1)} reverse(bf16[1,1,3,384,384]{4,3,2,1,0:T(8,128)(2,1)S(1)} %get-tuple-element.7), dimensions={2} | reverse | bytes 1769472 | tf_op jit(solution)/shard_map/rev | solution.py:44
  64.7 1.0 %rev.69 = bf16[1,1,3,384,384]{4,3,2,1,0:T(8,128)(2,1)} reverse(bf16[1,1,3,384,384]{4,3,2,1,0:T(8,128)(2,1)S(1)} %get-tuple-element.6), dimensions={2} | reverse | bytes 1769472 | tf_op jit(solution)/shard_map/rev | solution.py:44
  65.7 0.1 rev.70
  65.8 0.1 rev.71
  65.9 1.2 %fusion.117 = (bf16[2,4,32,1,384]{4,2,1,0,3:T(8,128)(2,1)S(1)}, bf16[2,4,32,1,384]{4,2,1,0,3:T(8,128)(2,1)S(1)}) fusion(bf16[2,4,32,384]{3,2,1,0:T(8,128)(2,1)} %copy-done.5, bf16[2,1,32,384]{3,2,1,0:T(8,128)(2,1)} %copy-done.16, bf16[2,1,32,384]{3,2,1,0:T(8,128)(2,1)} %copy-done.17), kind=kLoop, calls=%fused_computation.195 | loop fusion | flops 196608 | bytes 688128 | tf_op jit(solution)/shard_map/stack | solution.py:41
  67.1 1.1 %pad_maximum_fusion.9 = bf16[4,6,32,384]{3,2,1,0:T(8,128)(2,1)S(1)} fusion(bf16[2,6,32,384]{3,2,1,0:T(8,128)(2,1)} %collective-permute-done.5, bf16[2,1,32,384]{3,2,1,0:T(8,128)(2,1)} %copy-done.17, bf16[2,4,32,384]{3,2,1,0:T(8,128)(2,1)} %copy-done.5, bf16[2,1,32,384]{3,2,1,0:T(8,128)(2,1)} %copy-done.16), kind=kLoop, calls=%fused_computation.60 | loop fusion | flops 884736 | bytes 1179648 | tf_op jit(solution)/shard_map/concatenate | solution.py:32
  68.2 0.7 fusion.98
  69.0 1.7 %fusion.26 = f32[2,4,32,384,1]{3,2,0,1,4:T(8,128)S(1)} fusion(bf16[1,1,3,384,384]{4,3,2,1,0:T(8,128)(2,1)} %rev.63, bf16[2,4,32,1,384]{4,2,1,0,3:T(8,128)(2,1)S(1)} %get-tuple-element.24, bf16[2,4,32,1,384]{4,2,1,0,3:T(8,128)(2,1)S(1)} %get-tuple-element.71, bf16[2,4,32,1,384]{4,2,1,0,3:T(8,128)(2,1)S(1)} %get-tuple-element.23), kind=kOutput, calls=%fused_computation.27 | convolution fusion | flops 227082240 | bytes 1867776 | tf_op jit(solution)/shard_map/frwkc,kdc->frwd/dot_general | solution.py:45
  70.7 0.5 fusion.24
  71.2 0.5 fusion.22
  71.7 0.5 fusion.20
  72.3 0.5 fusion.18
  72.8 0.5 fusion.16
  73.3 1.2 %slice_bitcast_fusion.2 = (bf16[2,4,32,1,384]{4,2,1,0,3:T(8,128)(2,1)S(1)}, bf16[2,4,32,1,384]{4,2,1,0,3:T(8,128)(2,1)S(1)}, bf16[2,4,32,1,384]{4,2,1,0,3:T(8,128)(2,1)S(1)}) fusion(bf16[2,6,32,384]{3,2,1,0:T(8,128)(2,1)} %collective-permute-done.5), kind=kLoop, calls=%fused_computation.188 | loop fusion | bytes 1179648 | tf_op jit(solution)/shard_map/stack | solution.py:41
  74.5 0.5 fusion.14
  75.0 0.5 fusion.12
  75.5 0.5 fusion.10
  76.0 0.4 fusion.79
  76.4 0.3 copy.46
  76.7 19.3 %all_to_all.15 = f32[1,1,2,4,32,384]{5,3,2,1,0,4:T(4,128)S(1)} all-to-all(f32[1,1,2,4,32,384]{5,3,2,1,0,4:T(4,128)S(1)} %copy.46), channel_id=1, replica_groups=mesh['dp'=4,'tm'=4,'rows'=2] {'tm','rows'}, dimensions={4} | all-to-all | bytes 786432 | tf_op jit(solution)/shard_map/all_to_all | solution.py:75
  96.0 0.8 copy.47
  (56 shorter events, 0.3 us)
Async XLA Ops:
  1.7 22.4 %collective-permute-start = (bf16[2,1,32,384]{3,2,1,0:T(8,128)(2,1)S(1)}, bf16[2,1,32,384]{3,2,1,0:T(8,128)(2,1)S(1)}, u32[]{:S(2)}, u32[]{:S(2)}) collective-permute-start(bf16[2,1,32,384]{3,2,1,0:T(8,128)(2,1)S(1)} %get-tuple-element.77), channel_id=1, source_target_pairs={{0,1},{2,3},{4,5},{6,7},{8,9},{10,11},{12,13},{14,15},{16,17},{18,... | collective-permute-start | bytes 147464 | tf_op jit(solution)/shard_map/ppermute | solution.py:12
  4.1 20.0 %collective-permute-start.1 = (bf16[2,1,32,384]{3,2,1,0:T(8,128)(2,1)S(1)}, bf16[2,1,32,384]{3,2,1,0:T(8,128)(2,1)S(1)}, u32[]{:S(2)}, u32[]{:S(2)}) collective-permute-start(bf16[2,1,32,384]{3,2,1,0:T(8,128)(2,1)S(1)} %get-tuple-element.78), channel_id=1, source_target_pairs={{1,0},{3,2},{5,4},{7,6},{9,8},{11,10},{13,12},{15,14},{17,16},{19,... | collective-permute-start | bytes 147464 | tf_op jit(solution)/shard_map/ppermute | solution.py:15
  10.7 14.9 %copy-start.7 = (bf16[1,2,4,32,384]{4,3,2,1,0:T(8,128)(2,1)S(1)}, bf16[1,2,4,32,384]{4,3,2,1,0:T(8,128)(2,1)}, u32[]{:S(2)}) copy-start(bf16[1,2,4,32,384]{4,3,2,1,0:T(8,128)(2,1)} %param.8) | copy-start | bytes 589828
  24.2 12.9 %copy-start.4 = (bf16[1,1,3,384,384]{4,3,2,1,0:T(8,128)(2,1)S(1)}, bf16[1,1,3,384,384]{4,3,2,1,0:T(8,128)(2,1)}, u32[]{:S(2)}) copy-start(bf16[1,1,3,384,384]{4,3,2,1,0:T(8,128)(2,1)} %rev.55) | copy-start | bytes 2654212
  24.2 13.4 %copy-start.3 = (bf16[1,1,3,384,384]{4,3,2,1,0:T(8,128)(2,1)S(1)}, bf16[1,1,3,384,384]{4,3,2,1,0:T(8,128)(2,1)}, u32[]{:S(2)}) copy-start(bf16[1,1,3,384,384]{4,3,2,1,0:T(8,128)(2,1)} %rev.56) | copy-start | bytes 2654212
  24.2 11.8 %collective-permute-start.2 = (bf16[2,6,32,384]{3,2,1,0:T(8,128)(2,1)S(1)}, bf16[2,6,32,384]{3,2,1,0:T(8,128)(2,1)S(1)}, u32[]{:S(2)}, u32[]{:S(2)}) collective-permute-start(bf16[2,6,32,384]{3,2,1,0:T(8,128)(2,1)S(1)} %pad_maximum_fusion.19), channel_id=1, source_target_pairs={{2,0},{4,2},{6,4},{3,1},{5,3},{7,5},{10,8},{12,10},{14,12},{11,9},... | collective-permute-start | bytes 884744 | tf_op jit(solution)/shard_map/ppermute | solution.py:23
  25.8 12.5 %copy-start.2 = (bf16[1,1,3,384,384]{4,3,2,1,0:T(8,128)(2,1)S(1)}, bf16[1,1,3,384,384]{4,3,2,1,0:T(8,128)(2,1)}, u32[]{:S(2)}) copy-start(bf16[1,1,3,384,384]{4,3,2,1,0:T(8,128)(2,1)} %rev.57) | copy-start | bytes 2654212
  36.2 2.6 %copy-start.1 = (bf16[1,1,3,384,384]{4,3,2,1,0:T(8,128)(2,1)S(1)}, bf16[1,1,3,384,384]{4,3,2,1,0:T(8,128)(2,1)}, u32[]{:S(2)}) copy-start(bf16[1,1,3,384,384]{4,3,2,1,0:T(8,128)(2,1)} %rev.58) | copy-start | bytes 2654212
  36.9 2.6 %copy-start = (bf16[1,1,3,384,384]{4,3,2,1,0:T(8,128)(2,1)S(1)}, bf16[1,1,3,384,384]{4,3,2,1,0:T(8,128)(2,1)}, u32[]{:S(2)}) copy-start(bf16[1,1,3,384,384]{4,3,2,1,0:T(8,128)(2,1)} %rev.59) | copy-start | bytes 2654212
  38.8 3.0 %copy-start.9 = (bf16[1,1,3,384,384]{4,3,2,1,0:T(8,128)(2,1)S(1)}, bf16[1,1,3,384,384]{4,3,2,1,0:T(8,128)(2,1)}, u32[]{:S(2)}) copy-start(bf16[1,1,3,384,384]{4,3,2,1,0:T(8,128)(2,1)} %rev.54) | copy-start | bytes 2654212
  38.8 3.0 %copy-start.19 = (bf16[1,2,4,32,384]{4,3,2,1,0:T(8,128)(2,1)S(1)}, bf16[1,2,4,32,384]{4,3,2,1,0:T(8,128)(2,1)}, u32[]{:S(2)}) copy-start(bf16[1,2,4,32,384]{4,3,2,1,0:T(8,128)(2,1)} %param.7) | copy-start | bytes 589828
  40.0 9.9 %slice-start = ((s8[7962624]{0:T(1024)(128)(4,1)}), s8[4194304]{0:T(1024)(128)(4,1)S(1)}, s32[]{:S(2)}) async-start(s8[7962624]{0:T(1024)(128)(4,1)} %bitcast.332), calls=%async_computation.1 | async-start | bytes 8388608
  41.2 8.8 %slice-start.1 = ((s8[7962624]{0:T(1024)(128)(4,1)}), s8[3768320]{0:T(1024)(128)(4,1)S(1)}, s32[]{:S(2)}) async-start(s8[7962624]{0:T(1024)(128)(4,1)} %bitcast.332), calls=%async_computation.2 | async-start | bytes 7536640
  42.4 6.1 %copy-start.5 = (bf16[2,4,32,384]{3,2,1,0:T(8,128)(2,1)}, bf16[2,4,32,384]{3,2,1,0:T(8,128)(2,1)S(1)}, u32[]{:S(2)}) copy-start(bf16[2,4,32,384]{3,2,1,0:T(8,128)(2,1)S(1)} %fusion.9) | copy-start | bytes 589828
  42.4 3.5 %collective-permute-start.3 = (bf16[2,1,32,384]{3,2,1,0:T(8,128)(2,1)S(1)}, bf16[2,1,32,384]{3,2,1,0:T(8,128)(2,1)S(1)}, u32[]{:S(2)}, u32[]{:S(2)}) collective-permute-start(bf16[2,1,32,384]{3,2,1,0:T(8,128)(2,1)S(1)} %get-tuple-element.73), channel_id=1, source_target_pairs={{0,1},{2,3},{4,5},{6,7},{8,9},{10,11},{12,13},{14,15},{16,17},{18,... | collective-permute-start | bytes 147464 | tf_op jit(solution)/shard_map/ppermute | solution.py:12
  44.6 3.1 %collective-permute-start.4 = (bf16[2,1,32,384]{3,2,1,0:T(8,128)(2,1)S(1)}, bf16[2,1,32,384]{3,2,1,0:T(8,128)(2,1)S(1)}, u32[]{:S(2)}, u32[]{:S(2)}) collective-permute-start(bf16[2,1,32,384]{3,2,1,0:T(8,128)(2,1)S(1)} %get-tuple-element.74), channel_id=1, source_target_pairs={{1,0},{3,2},{5,4},{7,6},{9,8},{11,10},{13,12},{15,14},{17,16},{19,... | collective-permute-start | bytes 147464 | tf_op jit(solution)/shard_map/ppermute | solution.py:15
  45.9 2.6 %copy-start.16 = (bf16[2,1,32,384]{3,2,1,0:T(8,128)(2,1)}, bf16[2,1,32,384]{3,2,1,0:T(8,128)(2,1)S(1)}, u32[]{:S(2)}) copy-start(bf16[2,1,32,384]{3,2,1,0:T(8,128)(2,1)S(1)} %collective-permute-done.3) | copy-start | bytes 147460
  47.7 0.8 copy-start.17
  48.5 18.6 %collective-permute-start.5 = (bf16[2,6,32,384]{3,2,1,0:T(8,128)(2,1)}, bf16[2,6,32,384]{3,2,1,0:T(8,128)(2,1)}, u32[]{:S(2)}, u32[]{:S(2)}) collective-permute-start(bf16[2,6,32,384]{3,2,1,0:T(8,128)(2,1)} %pad_maximum_fusion.20), channel_id=1, source_target_pairs={{2,0},{4,2},{6,4},{3,1},{5,3},{7,5},{10,8},{12,10},{14,12},{11,9},... | collective-permute-start | bytes 884744 | tf_op jit(solution)/shard_map/ppermute | solution.py:23
  64.7 6.0 %copy-start.6 = (bf16[2,4,32,384]{3,2,1,0:T(8,128)(2,1)S(1)}, bf16[2,4,32,384]{3,2,1,0:T(8,128)(2,1)}, u32[]{:S(2)}) copy-start(bf16[2,4,32,384]{3,2,1,0:T(8,128)(2,1)} %copy-done.5) | copy-start | bytes 589828
  65.9 4.8 %copy-start.15 = (bf16[1,1,3,384,384]{4,3,2,1,0:T(8,128)(2,1)S(1)}, bf16[1,1,3,384,384]{4,3,2,1,0:T(8,128)(2,1)}, u32[]{:S(2)}) copy-start(bf16[1,1,3,384,384]{4,3,2,1,0:T(8,128)(2,1)} %rev.64) | copy-start | bytes 2654212
  65.9 5.4 %copy-start.14 = (bf16[1,1,3,384,384]{4,3,2,1,0:T(8,128)(2,1)S(1)}, bf16[1,1,3,384,384]{4,3,2,1,0:T(8,128)(2,1)}, u32[]{:S(2)}) copy-start(bf16[1,1,3,384,384]{4,3,2,1,0:T(8,128)(2,1)} %rev.65) | copy-start | bytes 2654212
  65.9 5.8 %copy-start.13 = (bf16[1,1,3,384,384]{4,3,2,1,0:T(8,128)(2,1)S(1)}, bf16[1,1,3,384,384]{4,3,2,1,0:T(8,128)(2,1)}, u32[]{:S(2)}) copy-start(bf16[1,1,3,384,384]{4,3,2,1,0:T(8,128)(2,1)} %rev.66) | copy-start | bytes 2654212
  68.2 4.0 %copy-start.12 = (bf16[1,1,3,384,384]{4,3,2,1,0:T(8,128)(2,1)S(1)}, bf16[1,1,3,384,384]{4,3,2,1,0:T(8,128)(2,1)}, u32[]{:S(2)}) copy-start(bf16[1,1,3,384,384]{4,3,2,1,0:T(8,128)(2,1)} %rev.67) | copy-start | bytes 2654212
  68.9 3.9 %copy-start.11 = (bf16[1,1,3,384,384]{4,3,2,1,0:T(8,128)(2,1)S(1)}, bf16[1,1,3,384,384]{4,3,2,1,0:T(8,128)(2,1)}, u32[]{:S(2)}) copy-start(bf16[1,1,3,384,384]{4,3,2,1,0:T(8,128)(2,1)} %rev.68) | copy-start | bytes 2654212
  70.7 3.7 %copy-start.10 = (bf16[1,1,3,384,384]{4,3,2,1,0:T(8,128)(2,1)S(1)}, bf16[1,1,3,384,384]{4,3,2,1,0:T(8,128)(2,1)}, u32[]{:S(2)}) copy-start(bf16[1,1,3,384,384]{4,3,2,1,0:T(8,128)(2,1)} %rev.69) | copy-start | bytes 2654212
  72.2 3.7 %copy-start.8 = (bf16[1,2,4,32,384]{4,3,2,1,0:T(8,128)(2,1)S(1)}, bf16[1,2,4,32,384]{4,3,2,1,0:T(8,128)(2,1)}, u32[]{:S(2)}) copy-start(bf16[1,2,4,32,384]{4,3,2,1,0:T(8,128)(2,1)} %param.8) | copy-start | bytes 589828
  72.3 3.7 %copy-start.18 = (bf16[1,2,4,32,384]{4,3,2,1,0:T(8,128)(2,1)S(1)}, bf16[1,2,4,32,384]{4,3,2,1,0:T(8,128)(2,1)}, u32[]{:S(2)}) copy-start(bf16[1,2,4,32,384]{4,3,2,1,0:T(8,128)(2,1)} %param.6) | copy-start | bytes 589828
where the time goes:
time: 97.7 us; the launch traced here: 96.8 us
  local copies, waits for them, and re-layouts  38.4 us (39%)
  blocking collectives  19.3 us (20%)
  waiting for transfers between devices  12.1 us (12%)
  matrix products  10.2 us (10%)
  starting transfers between devices  10 us (10%)
  other arithmetic  5.43 us (6%)
  between operations  1.33 us (1%)
    rev x18, local copies, waits for them, and re-layouts, transposed_conv(): kernel_slice = kernel[2 - time_tap, 2 - row_tap, ::-1]  26.5 us
    all_to_all x1, blocking collectives, on_device(): lax.all_to_all(result[:, None], ('tm', 'rows'), split_axis=4, concat_axis...  19.3 us
    ppermute x2, waiting for transfers between devices, shifted(): return lax.ppermute(value, axis, pairs)  10.3 us
    dot_general x18, matrix products, transposed_conv(): jnp.einsum('frwkc,kdc->frwd', stacked, kernel_slice, preferred_element_ty...  10.2 us
    slice x2, local copies, waits for them, and re-layouts, transposed_conv(): kernel_slice = kernel[2 - time_tap, 2 - row_tap, ::-1]  8.04 us
    ppermute x2, starting transfers between devices, with_halo(): lax.ppermute(lax.slice_in_dim(block, block.shape[dim] - width, None, axis...  4.57 us
    ppermute x2, starting transfers between devices, shifted(): return lax.ppermute(value, axis, pairs)  2.89 us
    another operation x6, local copies, waits for them, and re-layouts, transposed_conv(): jnp.stack([slab_rows[:, :, col_tap:col_tap + col_count] for col_tap in ra...  2.65 us
  transfers between devices with their start and end apart: 6, of which 2 were waited for; matrix products, arithmetic and copies ran while one was open for 37% of the time, Pallas kernels for 0%

commit v1 on v0

v1 whole, which is shorter than its diff:
```python
import functools

import jax
import jax.numpy as jnp
from jax import lax
from jax.experimental import pallas as pl
from jax.experimental.pallas import tpu as pltpu
from jax.sharding import PartitionSpec as P

F32 = jnp.float32
BF16 = jnp.bfloat16
VMEM = pl.BlockSpec(memory_space=pltpu.VMEM)
SMEM = pl.BlockSpec(memory_space=pltpu.SMEM)
ANY = pl.BlockSpec(memory_space=pl.ANY)
LANES = 128


def lanes(channels):
    return [(at, slice(at * LANES, (at + 1) * LANES)) for at in range(channels // LANES)]


def pairing(count):
    if count & (count - 1) == 0:
        return [
            ([(i, i ^ s) for i in range(count)], lambda i, s=s: i ^ s, lambda i, s=s: i ^ s)
            for s in range(1, count)
        ]
    return [
        (
            [(i, (i + s) % count) for i in range(count)],
            lambda i, s=s: lax.rem(i + s, count),
            lambda i, s=s: lax.rem(i + count - s, count),
        )
        for s in range(1, count)
    ]


def silu_slope(values):
    sigmoid_of = jax.nn.sigmoid(values)
    return sigmoid_of * (1.0 + values * (1.0 - sigmoid_of))


def dot_last(a, b):
    return lax.dot_general(a, b, (((1,), (1,)), ((), ())), preferred_element_type=F32)


def pack_kernel(time_devs, halos, masked, *refs):
    count = len(halos)
    len_ref, ins = refs[0], refs[1 : 1 + count]
    outs, turned = refs[1 + count : -count], refs[-count:]
    me = lax.axis_index("tm")
    targets = [me] + [to(me) for _, to, _ in pairing(time_devs)]
    for at in range(count):
        ref, stage, halo = ins[at], turned[at], halos[at]
        frames, rows, cols, _ = ref.shape
        unit = frames * rows
        if halo:
            edge = jnp.zeros((stage.shape[0], halo * unit, LANES), F32)
            stage[:, 0 : halo * unit, :] = edge
            stage[:, (halo + cols) * unit :, :] = edge
        for frame in range(frames):
            for row in range(rows):
                value = ref[frame, row].astype(F32)
                if masked:
                    value = jnp.where(me * frames + frame < len_ref[0], value, 0.0)
                start = halo * unit + frame * rows + row
                for at_lane, lane in lanes(value.shape[1]):
                    stage[at_lane, pl.ds(start, cols, stride=unit), :] = value[:, lane]
        block = cols // time_devs
        size = (block + 2 * halo) * unit
        for step, target in enumerate(targets):
            start = pl.multiple_of(target * (block * unit), unit)
            for at_lane, lane in lanes(ref.shape[3]):
                outs[at * time_devs + step][:, lane] = stage[at_lane, pl.ds(start, size), :].astype(BF16)


def pack(arrays, lengths, halos, masked, time_devs):
    frames, rows, cols, channels = arrays[0].shape
    unit = frames * rows
    shapes = [
        jax.ShapeDtypeStruct(((cols // time_devs + 2 * halo) * unit, channels), BF16)
        for halo in halos
        for _ in range(time_devs)
    ]
    out = pl.pallas_call(
        functools.partial(pack_kernel, time_devs, halos, masked),
        out_shape=shapes,
        in_specs=[SMEM] + [VMEM] * len(arrays),
        out_specs=[VMEM] * len(shapes),
        scratch_shapes=[
            pltpu.VMEM((channels // LANES, (cols + 2 * halo) * unit, LANES), F32) for halo in halos
        ],
        compiler_params=pltpu.CompilerParams(vmem_limit_bytes=12 << 20),
        cost_estimate=pl.CostEstimate(flops=1000, bytes_accessed=2 << 20, transcendentals=0),
    )(lengths, *arrays)
    return [out[at * time_devs : (at + 1) * time_devs] for at in range(len(arrays))]


def gather_block(dims, wins, halo, stage, dest, col_stride, row_pad):
    time_devs, row_devs, frame_dev, row_dev, col_dev = dims
    frames = time_devs * frame_dev
    unit = frame_dev * row_dev
    tm, row_at = lax.axis_index("tm"), lax.axis_index("rows")
    from_tm = [tm] + [source(tm) for _, _, source in pairing(time_devs)]
    from_row = [row_at] + [source(row_at) for _, _, source in pairing(row_devs)]
    cols = col_dev + 2 * halo
    for s in range(time_devs):
        for q in range(row_devs):
            at = s * row_devs + q
            first = row_at * (col_dev * unit)
            for at_lane, lane in lanes(wins[at].shape[1]):
                slot = at * dest.shape[0] + at_lane
                stage[slot, 0 : wins[at].shape[0], :] = wins[at][:, lane].astype(F32)
                for frame in range(frame_dev):
                    for row in range(row_dev):
                        start = first + frame * row_dev + row
                        target = (
                            (from_row[q] * row_dev + row + row_pad) * frames
                            + from_tm[s] * frame_dev
                            + frame
                        )
                        dest[at_lane, pl.ds(target, cols, stride=col_stride), :] = stage[
                            slot, pl.ds(start, cols, stride=unit), :
                        ]


def spread(full, shifts, cols, rows, frames):
    size = cols * (rows + 2) * frames
    place = lax.rem(lax.broadcasted_iota(jnp.int32, (size, LANES), 0), frames)
    for a in range(3):
        for p in range(2):
            count = size - p * frames
            for at_lane, lane in lanes(shifts.shape[3]):
                value = full[at_lane, pl.ds(a + p * frames, count), :]
                value = jnp.where(place[:count] < frames - a, value, 0.0).astype(BF16)
                shifts[a, p, 0:count, lane] = value


def tap(shifts, a, r, c, cols, rows, frames):
    parity = r % 2
    start = (r - parity) * frames
    pitch = (rows + 2) * frames
    return jnp.concatenate(
        [
            shifts[a, parity, (c + w) * pitch + start : (c + w) * pitch + start + rows * frames, :]
            for w in range(cols)
        ],
        axis=0,
    )


def taps_of(shifts, weights, a, cols, rows, frames):
    order = [(r, c) for r in range(3) for c in range(3)]
    moved = jnp.concatenate([tap(shifts, a, r, c, cols, rows, frames) for r, c in order], axis=1)
    mixed = jnp.concatenate([weights[a, 2 - r, 2 - c] for r, c in order], axis=1)
    return moved, mixed


def weight_copies(source, buffer, sems):
    return [pltpu.make_async_copy(source.at[2 - a], buffer.at[a], sems.at[a]) for a in range(3)]


def first_kernel(dims, count, *refs):
    wins, weight_ref = refs[:count], refs[count]
    acc_ref, mid_ref = refs[count + 1 : count + 3]
    stage, full, shifts, buffer, sems = refs[count + 3 :]
    time_devs, row_devs, frame_dev, row_dev, col_dev = dims
    frames, rows = time_devs * frame_dev, row_devs * row_dev
    copies = weight_copies(weight_ref, buffer, sems)
    for copy in copies:
        copy.start()
    full[...] = jnp.zeros_like(full)
    pitch = (rows + 2) * frames
    gather_block(dims, wins, 2, stage, full, pitch, 1)
    spread(full, shifts, col_dev + 4, rows, frames)
    plane = rows * frames
    for w in range(col_dev):
        start = (w + 2) * pitch + frames
        mid_ref[:, w * plane : (w + 1) * plane, :] = full[:, start : start + plane, :]
    acc_ref[...] = jnp.zeros_like(acc_ref)

    @pl.loop(0, 3)
    def _(a):
        pltpu.make_async_copy(weight_ref.at[2 - a], buffer.at[a], sems.at[a]).wait()
        moved, mixed = taps_of(shifts, buffer, a, col_dev + 2, rows, frames)
        acc_ref[...] += dot_last(moved, mixed)


def second_kernel(dims, count, cols_all, *refs):
    hid, lat = refs[:count], refs[count : 2 * count]
    acc_ref, mid_ref, weight_ref = refs[2 * count : 2 * count + 3]
    out_ref = refs[2 * count + 3]
    stage, slopes, full, shifts, acc, buffer, sems = refs[2 * count + 4 :]
    time_devs, row_devs, frame_dev, row_dev, col_dev = dims
    frames, rows = time_devs * frame_dev, row_devs * row_dev
    copies = weight_copies(weight_ref, buffer, sems)
    for copy in copies:
        copy.start()
    plane, pitch = rows * frames, (rows + 2) * frames
    gather_block(dims, hid, 1, stage, slopes, plane, 0)
    full[...] = jnp.zeros_like(full)
    first_col = (lax.axis_index("tm") * row_devs + lax.axis_index("rows")) * col_dev - 1
    for w in range(col_dev + 2):
        col = first_col + w
        inside = jnp.logical_and(col >= 0, col < cols_all)
        here = slice(w * plane, (w + 1) * plane)
        start = w * pitch + frames
        for at_lane, lane in lanes(acc_ref.shape[1]):
            value = acc_ref[here, lane] * silu_slope(slopes[at_lane, here, :])
            full[at_lane, start : start + plane, :] = jnp.where(inside, value, 0.0)
    spread(full, shifts, col_dev + 2, rows, frames)
    acc[...] = jnp.zeros_like(acc)

    @pl.loop(0, 3)
    def _(a):
        pltpu.make_async_copy(weight_ref.at[2 - a], buffer.at[a], sems.at[a]).wait()
        moved, mixed = taps_of(shifts, buffer, a, col_dev, rows, frames)
        acc[...] += dot_last(mixed, moved)

    gather_block(dims, lat, 0, stage, slopes, plane, 0)
    size = col_dev * plane
    for at_lane, lane in lanes(acc.shape[0]):
        full[at_lane, 0:size, :] = mid_ref[at_lane] + acc[lane, :].T * silu_slope(
            slopes[at_lane, 0:size, :]
        )
        for frame in range(frames):
            for row in range(rows):
                out_ref[0, frame, row, :, lane] = full[
                    at_lane, pl.ds(row * frames + frame, col_dev, stride=plane), :
                ]


def on_device(latents, hidden, cotangent, conv_one, conv_two, lengths):
    _, frame_dev, row_dev, cols, channels = latents.shape
    time_devs, row_devs = lax.axis_size("tm"), lax.axis_size("rows")
    col_dev = cols // (time_devs * row_devs)
    frames, rows = time_devs * frame_dev, row_devs * row_dev
    unit = frame_dev * row_dev
    dims = (time_devs, row_devs, frame_dev, row_dev, col_dev)
    count = time_devs * row_devs

    def over_tm(windows):
        return [windows[0]] + [
            lax.ppermute(windows[step + 1], "tm", pairs)
            for step, (pairs, _, _) in enumerate(pairing(time_devs))
        ]

    def over_rows(windows):
        out = []
        for window in windows:
            out.append(window)
            out += [lax.ppermute(window, "rows", pairs) for pairs, _, _ in pairing(row_devs)]
        return out

    (cot,) = pack([cotangent[0]], lengths, (2,), True, time_devs)
    hid, lat = pack([hidden[0], latents[0]], lengths, (1, 0), False, time_devs)
    cot = over_rows(over_tm(cot))
    hid = over_rows(over_tm(hid))
    lat = over_rows(over_tm(lat))

    plane, pitch = rows * frames, (rows + 2) * frames
    chip, parts = cols // time_devs, channels // LANES

    def scratch(halo):
        return [
            pltpu.VMEM((count * parts, (chip + 2 * halo) * unit, LANES), F32),
        ]

    acc, mid = pl.pallas_call(
        functools.partial(first_kernel, dims, count),
        out_shape=[
            jax.ShapeDtypeStruct(((col_dev + 2) * plane, channels), F32),
            jax.ShapeDtypeStruct((parts, col_dev * plane, LANES), F32),
        ],
        in_specs=[VMEM] * count + [ANY],
        out_specs=[VMEM] * 2,
        scratch_shapes=scratch(2)
        + [
            pltpu.VMEM((parts, (col_dev + 4) * pitch + frames, LANES), F32),
            pltpu.VMEM((3, 2, (col_dev + 4) * pitch, channels), BF16),
            pltpu.VMEM((3,) + conv_two.shape[1:], BF16),
            pltpu.SemaphoreType.DMA((3,)),
        ],
        compiler_params=pltpu.CompilerParams(vmem_limit_bytes=32 << 20),
        cost_estimate=pl.CostEstimate(
            flops=2 * 27 * (col_dev + 2) * plane * channels * channels,
            bytes_accessed=10 << 20,
            transcendentals=0,
        ),
    )(*cot, conv_two)
    return pl.pallas_call(
        functools.partial(second_kernel, dims, count, cols),
        out_shape=jax.ShapeDtypeStruct((1, frames, rows, col_dev, channels), F32),
        in_specs=[VMEM] * (2 * count + 2) + [ANY],
        out_specs=VMEM,
        scratch_shapes=scratch(1)
        + [
            pltpu.VMEM((parts, (col_dev + 2) * plane, LANES), F32),
            pltpu.VMEM((parts, (col_dev + 2) * pitch + frames, LANES), F32),
            pltpu.VMEM((3, 2, (col_dev + 2) * pitch, channels), BF16),
            pltpu.VMEM((channels, col_dev * plane), F32),
            pltpu.VMEM((3,) + conv_one.shape[1:], BF16),
            pltpu.SemaphoreType.DMA((3,)),
        ],
        compiler_params=pltpu.CompilerParams(vmem_limit_bytes=32 << 20),
        cost_estimate=pl.CostEstimate(
            flops=2 * 27 * col_dev * plane * channels * channels,
            bytes_accessed=10 << 20,
            transcendentals=0,
        ),
    )(*hid, *lat, acc, mid, conv_one)


def solution(mesh):
    spec = P("dp", "tm", "rows", None, None)
    return jax.shard_map(
        on_device,
        mesh=mesh,
        in_specs=(spec, spec, spec, P(), P(), P("dp")),
        out_specs=P("dp", None, None, ("tm", "rows"), None),
        check_vma=False,
    )
```

time: 97.7 us -> 44.8 us (0.46)
  local copies, waits for them, and re-layouts: 38.4 us -> 6.49 us
  blocking collectives: 19.3 us -> 0 us
  Pallas kernels: 0 us -> 13.1 us
  matrix products: 10.2 us -> 0 us
  starting transfers between devices: 10 us -> 18.4 us
  waiting for transfers between devices: 12.1 us -> 5.24 us
  other arithmetic: 5.43 us -> 0 us
    rev x18 -> x0, local copies, waits for them, and re-layouts: 26.5 us -> none  [transposed_conv(): kernel_slice = kernel[2 - time_tap, 2 - row_tap, ::-1]]
    all_to_all x1 -> x0, blocking collectives: 19.3 us -> none  [on_device(): lax.all_to_all(result[:, None], ('tm', 'rows'), split_axis=4, concat_axis...]
    pallas_call x0 -> x4, Pallas kernels: none -> 13.1 us  [the longest x1 6.64 us: on_device(): pl.pallas_call(functools.partial(first_kernel, dims, count), out_shape=[j...]
    dot_general x18 -> x0, matrix products: 10.2 us -> none  [transposed_conv(): jnp.einsum('frwkc,kdc->frwd', stacked, kernel_slice, preferred_element_ty...]
    ppermute x6 -> x21, starting transfers between devices: 10 us -> 18.4 us  [the longest x9 15.9 us: over_tm(): lax.ppermute(windows[step + 1], 'tm', pairs)]
    slice x4 -> x0, local copies, waits for them, and re-layouts: 8.07 us -> none  [the longest x2 8.04 us: transposed_conv(): kernel_slice = kernel[2 - time_tap, 2 - row_tap, ::-1]]
    ppermute x6 -> x21, waiting for transfers between devices: 12.1 us -> 5.24 us  [the longest x9 4.5 us: over_tm(): lax.ppermute(windows[step + 1], 'tm', pairs)]
    unnamed x44 -> x10, local copies, waits for them, and re-layouts: 0.11 us -> 6.49 us
  transfers between devices with their start and end apart: 6 -> 21, of which waited for: 2 -> 4; matrix products, arithmetic and copies ran while one was open for 37% -> 0% of each run, Pallas kernels for 0% -> 15%
where the time goes in v1:
time: 44.8 us; the launch traced here: 44.2 us
  starting transfers between devices  18.4 us (41%)
  Pallas kernels  13.1 us (29%)
  local copies, waits for them, and re-layouts  6.49 us (14%)
  waiting for transfers between devices  5.24 us (12%)
  between operations  0.91 us (2%)
    ppermute x9, starting transfers between devices, over_tm(): lax.ppermute(windows[step + 1], 'tm', pairs)  15.9 us
    pallas_call x1, Pallas kernels, on_device(): pl.pallas_call(functools.partial(first_kernel, dims, count), out_shape=[j...  6.64 us
    unnamed x10, local copies, waits for them, and re-layouts  6.49 us
    pallas_call x1, Pallas kernels, on_device(): pl.pallas_call(functools.partial(second_kernel, dims, count, cols), out_s...  6.07 us
    ppermute x9, waiting for transfers between devices, over_tm(): lax.ppermute(windows[step + 1], 'tm', pairs)  4.5 us
    ppermute x12, starting transfers between devices, over_rows(): lax.ppermute(window, 'rows', pairs)  2.56 us
  transfers between devices with their start and end apart: 21, of which 4 were waited for; matrix products, arithmetic and copies ran while one was open for 0% of the time, Pallas kernels for 15%

profile of v1, /device:TPU:0, one launch (start us, length us, event | category | flops | bytes accessed | tf_op | source)
XLA Modules:
  0.0 44.2 jit_solution(3649757867597672067)
XLA Ops:
  0.0 0.0 copy-start
  0.8 0.0 copy-start.1
  0.8 1.0 %copy-done.1 = bf16[1,2,4,32,384]{4,3,2,1,0:T(8,128)(2,1)S(1)} copy-done((bf16[1,2,4,32,384]{4,3,2,1,0:T(8,128)(2,1)S(1)}, bf16[1,2,4,32,384]{4,3,2,1,0:T(8,128)(2,1)}, u32[]{:S(2)}) %copy-start.1) | copy-done | bytes 196632
  1.8 0.0 copy-start.2
  1.8 1.3 %copy-done.2 = bf16[1,2,4,32,384]{4,3,2,1,0:T(8,128)(2,1)S(1)} copy-done((bf16[1,2,4,32,384]{4,3,2,1,0:T(8,128)(2,1)S(1)}, bf16[1,2,4,32,384]{4,3,2,1,0:T(8,128)(2,1)}, u32[]{:S(2)}) %copy-start.2) | copy-done | bytes 196632
  3.1 0.2 shard_map.64
  3.4 3.1 %collective-permute-start.8 = (bf16[64,384]{1,0:T(8,128)(2,1)S(1)}, bf16[64,384]{1,0:T(8,128)(2,1)S(1)}, u32[]{:S(2)}, u32[]{:S(2)}) collective-permute-start(bf16[64,384]{1,0:T(8,128)(2,1)S(1)} %get-tuple-element.24), channel_id=1, source_target_pairs={{0,2},{2,0},{4,6},{6,4},{1,3},{3,1},{5,7},{7,5},{8,10},{10,8},{12,... | collective-permute-start | bytes 147464 | tf_op jit(solution)/shard_map/ppermute | solution.py:244
  6.5 0.1 collective-permute-start.1
  6.6 3.0 %collective-permute-start.10 = (bf16[64,384]{1,0:T(8,128)(2,1)S(1)}, bf16[64,384]{1,0:T(8,128)(2,1)S(1)}, u32[]{:S(2)}, u32[]{:S(2)}) collective-permute-start(bf16[64,384]{1,0:T(8,128)(2,1)S(1)} %get-tuple-element.25), channel_id=1, source_target_pairs={{0,4},{2,6},{4,0},{6,2},{1,5},{3,7},{5,1},{7,3},{8,12},{10,14},{12... | collective-permute-start | bytes 147464 | tf_op jit(solution)/shard_map/ppermute | solution.py:244
  9.5 1.3 %collective-permute-start.12 = (bf16[64,384]{1,0:T(8,128)(2,1)S(1)}, bf16[64,384]{1,0:T(8,128)(2,1)S(1)}, u32[]{:S(2)}, u32[]{:S(2)}) collective-permute-start(bf16[64,384]{1,0:T(8,128)(2,1)S(1)} %get-tuple-element.26), channel_id=1, source_target_pairs={{0,6},{2,4},{4,2},{6,0},{1,7},{3,5},{5,3},{7,1},{8,14},{10,12},{12... | collective-permute-start | bytes 147464 | tf_op jit(solution)/shard_map/ppermute | solution.py:244
  10.9 0.0 collective-permute-start.7
  10.9 0.0 collective-permute-done.8.refs_10_
  10.9 1.7 %collective-permute-start.3 = (bf16[80,384]{1,0:T(8,128)(2,1)S(1)}, bf16[80,384]{1,0:T(8,128)(2,1)S(1)}, u32[]{:S(2)}, u32[]{:S(2)}) collective-permute-start(bf16[80,384]{1,0:T(8,128)(2,1)S(1)} %get-tuple-element.21), channel_id=1, source_target_pairs={{0,4},{2,6},{4,0},{6,2},{1,5},{3,7},{5,1},{7,3},{8,12},{10,14},{12... | collective-permute-start | bytes 184328 | tf_op jit(solution)/shard_map/ppermute | solution.py:244
  12.6 0.0 copy-start.3
  12.6 0.9 %copy-done.3 = bf16[1,2,4,32,384]{4,3,2,1,0:T(8,128)(2,1)S(1)} copy-done((bf16[1,2,4,32,384]{4,3,2,1,0:T(8,128)(2,1)S(1)}, bf16[1,2,4,32,384]{4,3,2,1,0:T(8,128)(2,1)}, u32[]{:S(2)}) %copy-start.3) | copy-done | bytes 196632
  13.5 0.1 shard_map.65
  13.6 0.0 collective-permute-done.10.refs_12_
  13.7 1.4 %collective-permute-start.15 = (bf16[96,384]{1,0:T(8,128)(2,1)S(1)}, bf16[96,384]{1,0:T(8,128)(2,1)S(1)}, u32[]{:S(2)}, u32[]{:S(2)}) collective-permute-start(bf16[96,384]{1,0:T(8,128)(2,1)S(1)} %get-tuple-element.28), channel_id=1, source_target_pairs={{0,2},{2,0},{4,6},{6,4},{1,3},{3,1},{5,7},{7,5},{8,10},{10,8},{12,... | collective-permute-start | bytes 221192 | tf_op jit(solution)/shard_map/ppermute | solution.py:244
  15.1 0.9 %collective-permute-done.12.refs_14_ = bf16[64,384]{1,0:T(8,128)(2,1)S(1)} collective-permute-done((bf16[64,384]{1,0:T(8,128)(2,1)S(1)}, bf16[64,384]{1,0:T(8,128)(2,1)S(1)}, u32[]{:S(2)}, u32[]{:S(2)}) %collective-permute-start.12) | collective-permute-done | bytes 49184 | tf_op jit(solution)/shard_map/ppermute | solution.py:244
  16.0 1.4 %collective-permute-start.17 = (bf16[96,384]{1,0:T(8,128)(2,1)S(1)}, bf16[96,384]{1,0:T(8,128)(2,1)S(1)}, u32[]{:S(2)}, u32[]{:S(2)}) collective-permute-start(bf16[96,384]{1,0:T(8,128)(2,1)S(1)} %get-tuple-element.29), channel_id=1, source_target_pairs={{0,4},{2,6},{4,0},{6,2},{1,5},{3,7},{5,1},{7,3},{8,12},{10,14},{12... | collective-permute-start | bytes 221192 | tf_op jit(solution)/shard_map/ppermute | solution.py:244
  17.4 0.0 collective-permute-done.7.refs_9_
  17.4 0.7 %collective-permute-start.19 = (bf16[96,384]{1,0:T(8,128)(2,1)S(1)}, bf16[96,384]{1,0:T(8,128)(2,1)S(1)}, u32[]{:S(2)}, u32[]{:S(2)}) collective-permute-start(bf16[96,384]{1,0:T(8,128)(2,1)S(1)} %get-tuple-element.30), channel_id=1, source_target_pairs={{0,6},{2,4},{4,2},{6,0},{1,7},{3,5},{5,3},{7,1},{8,14},{10,12},{12... | collective-permute-start | bytes 221192 | tf_op jit(solution)/shard_map/ppermute | solution.py:244
  18.1 0.0 collective-permute-done.1.refs_2_
  18.1 3.2 %collective-permute-start.5 = (bf16[80,384]{1,0:T(8,128)(2,1)S(1)}, bf16[80,384]{1,0:T(8,128)(2,1)S(1)}, u32[]{:S(2)}, u32[]{:S(2)}) collective-permute-start(bf16[80,384]{1,0:T(8,128)(2,1)S(1)} %get-tuple-element.22), channel_id=1, source_target_pairs={{0,6},{2,4},{4,2},{6,0},{1,7},{3,5},{5,3},{7,1},{8,14},{10,12},{12... | collective-permute-start | bytes 184328 | tf_op jit(solution)/shard_map/ppermute | solution.py:244
  21.3 0.0 collective-permute-done.3.refs_4_
  21.3 0.0 collective-permute-start
  21.3 3.0 %collective-permute-done.5.refs_6_ = bf16[80,384]{1,0:T(8,128)(2,1)S(1)} collective-permute-done((bf16[80,384]{1,0:T(8,128)(2,1)S(1)}, bf16[80,384]{1,0:T(8,128)(2,1)S(1)}, u32[]{:S(2)}, u32[]{:S(2)}) %collective-permute-start.5) | collective-permute-done | bytes 61472 | tf_op jit(solution)/shard_map/ppermute | solution.py:244
  24.3 0.0 collective-permute-start.14
  24.3 0.0 collective-permute-done.15.refs_2_
  24.3 0.5 %collective-permute-start.16 = (bf16[96,384]{1,0:T(8,128)(2,1)S(1)}, bf16[96,384]{1,0:T(8,128)(2,1)S(1)}, u32[]{:S(2)}, u32[]{:S(2)}) collective-permute-start(bf16[96,384]{1,0:T(8,128)(2,1)S(1)} %collective-permute-done.15.refs_2_), channel_id=1, source_target_pairs={{0,1},{1,0},{2,3},{3,2},{4,5},{5,4},{6,7},{7,6},{8,9},{9,8},{10,11... | collective-permute-start | bytes 221192 | tf_op jit(solution)/shard_map/ppermute | solution.py:252
  24.8 0.6 %collective-permute-done.17.refs_4_ = bf16[96,384]{1,0:T(8,128)(2,1)S(1)} collective-permute-done((bf16[96,384]{1,0:T(8,128)(2,1)S(1)}, bf16[96,384]{1,0:T(8,128)(2,1)S(1)}, u32[]{:S(2)}, u32[]{:S(2)}) %collective-permute-start.17) | collective-permute-done | bytes 73760 | tf_op jit(solution)/shard_map/ppermute | solution.py:244
  25.4 0.0 collective-permute-start.18
  25.4 0.0 collective-permute-done.19.refs_6_
  25.4 0.5 %collective-permute-start.20 = (bf16[96,384]{1,0:T(8,128)(2,1)S(1)}, bf16[96,384]{1,0:T(8,128)(2,1)S(1)}, u32[]{:S(2)}, u32[]{:S(2)}) collective-permute-start(bf16[96,384]{1,0:T(8,128)(2,1)S(1)} %collective-permute-done.19.refs_6_), channel_id=1, source_target_pairs={{0,1},{1,0},{2,3},{3,2},{4,5},{5,4},{6,7},{7,6},{8,9},{9,8},{10,11... | collective-permute-start | bytes 221192 | tf_op jit(solution)/shard_map/ppermute | solution.py:252
  25.9 0.0 collective-permute-done.refs_1_
  25.9 0.1 collective-permute-start.9
  25.9 0.0 collective-permute-done.14.refs_1_
  25.9 0.4 collective-permute-start.11
  26.4 0.7 %collective-permute-done.9.refs_11_ = bf16[64,384]{1,0:T(8,128)(2,1)S(1)} collective-permute-done((bf16[64,384]{1,0:T(8,128)(2,1)S(1)}, bf16[64,384]{1,0:T(8,128)(2,1)S(1)}, u32[]{:S(2)}, u32[]{:S(2)}) %collective-permute-start.9) | collective-permute-done | bytes 49184 | tf_op jit(solution)/shard_map/ppermute | solution.py:252
  27.1 0.2 collective-permute-start.13
  27.3 0.0 collective-permute-done.16.refs_3_
  27.3 0.3 collective-permute-start.2
  27.6 0.0 collective-permute-done.18.refs_5_
  27.6 0.2 collective-permute-start.4
  27.8 0.0 collective-permute-done.20.refs_7_
  27.8 0.3 collective-permute-start.6
  28.1 0.0 copy-start.4
  28.1 3.3 %copy-done.4 = bf16[3,3,3,384,384]{4,3,2,1,0:T(8,128)(2,1)S(1)} copy-done((bf16[3,3,3,384,384]{4,3,2,1,0:T(8,128)(2,1)S(1)}, bf16[3,3,3,384,384]{4,3,2,1,0:T(8,128)(2,1)}, u32[]{:S(2)}) %copy-start.4) | copy-done | bytes 7962648
  31.4 6.6 %shard_map.66 = (f32[384,384]{1,0:T(8,128)S(1)}, f32[3,256,128]{2,1,0:T(8,128)S(1)}) custom-call(bf16[96,384]{1,0:T(8,128)(2,1)S(1)} %get-tuple-element.27.refs_0_, bf16[96,384]{1,0:T(8,128)(2,1)S(1)} %collective-permute-done.14.refs_1_, bf16[96,384]{1,0:T(8,128)(2,1)S(1)} %collective-permute-done.15.refs_2_, ...), custom_call_target="tpu_custom_call" | custom-call | flops 3057647616 | bytes 10485760 | tf_op jit(solution)/shard_map/pallas_call | solution.py:269
  38.1 0.0 collective-permute-done.11.refs_13_
  38.1 0.0 collective-permute-done.13.refs_15_
  38.1 0.0 collective-permute-done.2.refs_3_
  38.1 0.0 collective-permute-done.4.refs_5_
  38.1 0.0 collective-permute-done.6.refs_7_
  38.1 0.0 copy-done
  38.1 6.1 %shard_map.67 = f32[1,8,8,4,384]{4,3,2,1,0:T(4,128)} custom-call(bf16[80,384]{1,0:T(8,128)(2,1)S(1)} %get-tuple-element.19.refs_0_, bf16[80,384]{1,0:T(8,128)(2,1)S(1)} %collective-permute-done.refs_1_, bf16[80,384]{1,0:T(8,128)(2,1)S(1)} %collective-permute-done.1.refs_2_, bf16[80,384]{1,0:T(8,128)(2,1)S(1)} %collective-permute-done.2.refs_3_, ...), custom_call_target="tpu_custom_call" | custom-call | flops 2038431744 | bytes 10485760 | tf_op jit(solution)/shard_map/pallas_call | solution.py:291
Async XLA Ops:
  0.0 38.1 %copy-start = (bf16[3,3,3,384,384]{4,3,2,1,0:T(8,128)(2,1)S(1)}, bf16[3,3,3,384,384]{4,3,2,1,0:T(8,128)(2,1)}, u32[]{:S(2)}) copy-start(bf16[3,3,3,384,384]{4,3,2,1,0:T(8,128)(2,1)} %refs_18_.1) | copy-start | bytes 23887876
  0.8 1.0 %copy-start.1 = (bf16[1,2,4,32,384]{4,3,2,1,0:T(8,128)(2,1)S(1)}, bf16[1,2,4,32,384]{4,3,2,1,0:T(8,128)(2,1)}, u32[]{:S(2)}) copy-start(bf16[1,2,4,32,384]{4,3,2,1,0:T(8,128)(2,1)} %param.7) | copy-start | bytes 589828
  1.8 1.3 %copy-start.2 = (bf16[1,2,4,32,384]{4,3,2,1,0:T(8,128)(2,1)S(1)}, bf16[1,2,4,32,384]{4,3,2,1,0:T(8,128)(2,1)}, u32[]{:S(2)}) copy-start(bf16[1,2,4,32,384]{4,3,2,1,0:T(8,128)(2,1)} %param.6) | copy-start | bytes 589828
  3.4 7.5 %collective-permute-start.8 = (bf16[64,384]{1,0:T(8,128)(2,1)S(1)}, bf16[64,384]{1,0:T(8,128)(2,1)S(1)}, u32[]{:S(2)}, u32[]{:S(2)}) collective-permute-start(bf16[64,384]{1,0:T(8,128)(2,1)S(1)} %get-tuple-element.24), channel_id=1, source_target_pairs={{0,2},{2,0},{4,6},{6,4},{1,3},{3,1},{5,7},{7,5},{8,10},{10,8},{12,... | collective-permute-start | bytes 147464 | tf_op jit(solution)/shard_map/ppermute | solution.py:244
  6.5 11.6 %collective-permute-start.1 = (bf16[80,384]{1,0:T(8,128)(2,1)S(1)}, bf16[80,384]{1,0:T(8,128)(2,1)S(1)}, u32[]{:S(2)}, u32[]{:S(2)}) collective-permute-start(bf16[80,384]{1,0:T(8,128)(2,1)S(1)} %get-tuple-element.20), channel_id=1, source_target_pairs={{0,2},{2,0},{4,6},{6,4},{1,3},{3,1},{5,7},{7,5},{8,10},{10,8},{12,... | collective-permute-start | bytes 184328 | tf_op jit(solution)/shard_map/ppermute | solution.py:244
  6.6 7.1 %collective-permute-start.10 = (bf16[64,384]{1,0:T(8,128)(2,1)S(1)}, bf16[64,384]{1,0:T(8,128)(2,1)S(1)}, u32[]{:S(2)}, u32[]{:S(2)}) collective-permute-start(bf16[64,384]{1,0:T(8,128)(2,1)S(1)} %get-tuple-element.25), channel_id=1, source_target_pairs={{0,4},{2,6},{4,0},{6,2},{1,5},{3,7},{5,1},{7,3},{8,12},{10,14},{12... | collective-permute-start | bytes 147464 | tf_op jit(solution)/shard_map/ppermute | solution.py:244
  9.5 6.5 %collective-permute-start.12 = (bf16[64,384]{1,0:T(8,128)(2,1)S(1)}, bf16[64,384]{1,0:T(8,128)(2,1)S(1)}, u32[]{:S(2)}, u32[]{:S(2)}) collective-permute-start(bf16[64,384]{1,0:T(8,128)(2,1)S(1)} %get-tuple-element.26), channel_id=1, source_target_pairs={{0,6},{2,4},{4,2},{6,0},{1,7},{3,5},{5,3},{7,1},{8,14},{10,12},{12... | collective-permute-start | bytes 147464 | tf_op jit(solution)/shard_map/ppermute | solution.py:244
  10.9 6.6 %collective-permute-start.7 = (bf16[64,384]{1,0:T(8,128)(2,1)S(1)}, bf16[64,384]{1,0:T(8,128)(2,1)S(1)}, u32[]{:S(2)}, u32[]{:S(2)}) collective-permute-start(bf16[64,384]{1,0:T(8,128)(2,1)S(1)} %get-tuple-element.23.refs_8_), channel_id=1, source_target_pairs={{0,1},{1,0},{2,3},{3,2},{4,5},{5,4},{6,7},{7,6},{8,9},{9,8},{10,11... | collective-permute-start | bytes 147464 | tf_op jit(solution)/shard_map/ppermute | solution.py:252
  10.9 10.4 %collective-permute-start.3 = (bf16[80,384]{1,0:T(8,128)(2,1)S(1)}, bf16[80,384]{1,0:T(8,128)(2,1)S(1)}, u32[]{:S(2)}, u32[]{:S(2)}) collective-permute-start(bf16[80,384]{1,0:T(8,128)(2,1)S(1)} %get-tuple-element.21), channel_id=1, source_target_pairs={{0,4},{2,6},{4,0},{6,2},{1,5},{3,7},{5,1},{7,3},{8,12},{10,14},{12... | collective-permute-start | bytes 184328 | tf_op jit(solution)/shard_map/ppermute | solution.py:244
  12.6 0.9 %copy-start.3 = (bf16[1,2,4,32,384]{4,3,2,1,0:T(8,128)(2,1)S(1)}, bf16[1,2,4,32,384]{4,3,2,1,0:T(8,128)(2,1)}, u32[]{:S(2)}) copy-start(bf16[1,2,4,32,384]{4,3,2,1,0:T(8,128)(2,1)} %param.8) | copy-start | bytes 589828
  13.7 10.6 %collective-permute-start.15 = (bf16[96,384]{1,0:T(8,128)(2,1)S(1)}, bf16[96,384]{1,0:T(8,128)(2,1)S(1)}, u32[]{:S(2)}, u32[]{:S(2)}) collective-permute-start(bf16[96,384]{1,0:T(8,128)(2,1)S(1)} %get-tuple-element.28), channel_id=1, source_target_pairs={{0,2},{2,0},{4,6},{6,4},{1,3},{3,1},{5,7},{7,5},{8,10},{10,8},{12,... | collective-permute-start | bytes 221192 | tf_op jit(solution)/shard_map/ppermute | solution.py:244
  16.0 9.4 %collective-permute-start.17 = (bf16[96,384]{1,0:T(8,128)(2,1)S(1)}, bf16[96,384]{1,0:T(8,128)(2,1)S(1)}, u32[]{:S(2)}, u32[]{:S(2)}) collective-permute-start(bf16[96,384]{1,0:T(8,128)(2,1)S(1)} %get-tuple-element.29), channel_id=1, source_target_pairs={{0,4},{2,6},{4,0},{6,2},{1,5},{3,7},{5,1},{7,3},{8,12},{10,14},{12... | collective-permute-start | bytes 221192 | tf_op jit(solution)/shard_map/ppermute | solution.py:244
  17.4 7.9 %collective-permute-start.19 = (bf16[96,384]{1,0:T(8,128)(2,1)S(1)}, bf16[96,384]{1,0:T(8,128)(2,1)S(1)}, u32[]{:S(2)}, u32[]{:S(2)}) collective-permute-start(bf16[96,384]{1,0:T(8,128)(2,1)S(1)} %get-tuple-element.30), channel_id=1, source_target_pairs={{0,6},{2,4},{4,2},{6,0},{1,7},{3,5},{5,3},{7,1},{8,14},{10,12},{12... | collective-permute-start | bytes 221192 | tf_op jit(solution)/shard_map/ppermute | solution.py:244
  18.1 6.1 %collective-permute-start.5 = (bf16[80,384]{1,0:T(8,128)(2,1)S(1)}, bf16[80,384]{1,0:T(8,128)(2,1)S(1)}, u32[]{:S(2)}, u32[]{:S(2)}) collective-permute-start(bf16[80,384]{1,0:T(8,128)(2,1)S(1)} %get-tuple-element.22), channel_id=1, source_target_pairs={{0,6},{2,4},{4,2},{6,0},{1,7},{3,5},{5,3},{7,1},{8,14},{10,12},{12... | collective-permute-start | bytes 184328 | tf_op jit(solution)/shard_map/ppermute | solution.py:244
  21.3 4.6 %collective-permute-start = (bf16[80,384]{1,0:T(8,128)(2,1)S(1)}, bf16[80,384]{1,0:T(8,128)(2,1)S(1)}, u32[]{:S(2)}, u32[]{:S(2)}) collective-permute-start(bf16[80,384]{1,0:T(8,128)(2,1)S(1)} %get-tuple-element.19.refs_0_), channel_id=1, source_target_pairs={{0,1},{1,0},{2,3},{3,2},{4,5},{5,4},{6,7},{7,6},{8,9},{9,8},{10,11... | collective-permute-start | bytes 184328 | tf_op jit(solution)/shard_map/ppermute | solution.py:252
  24.3 1.7 %collective-permute-start.14 = (bf16[96,384]{1,0:T(8,128)(2,1)S(1)}, bf16[96,384]{1,0:T(8,128)(2,1)S(1)}, u32[]{:S(2)}, u32[]{:S(2)}) collective-permute-start(bf16[96,384]{1,0:T(8,128)(2,1)S(1)} %get-tuple-element.27.refs_0_), channel_id=1, source_target_pairs={{0,1},{1,0},{2,3},{3,2},{4,5},{5,4},{6,7},{7,6},{8,9},{9,8},{10,11... | collective-permute-start | bytes 221192 | tf_op jit(solution)/shard_map/ppermute | solution.py:252
  24.3 3.0 %collective-permute-start.16 = (bf16[96,384]{1,0:T(8,128)(2,1)S(1)}, bf16[96,384]{1,0:T(8,128)(2,1)S(1)}, u32[]{:S(2)}, u32[]{:S(2)}) collective-permute-start(bf16[96,384]{1,0:T(8,128)(2,1)S(1)} %collective-permute-done.15.refs_2_), channel_id=1, source_target_pairs={{0,1},{1,0},{2,3},{3,2},{4,5},{5,4},{6,7},{7,6},{8,9},{9,8},{10,11... | collective-permute-start | bytes 221192 | tf_op jit(solution)/shard_map/ppermute | solution.py:252
  25.4 2.3 %collective-permute-start.18 = (bf16[96,384]{1,0:T(8,128)(2,1)S(1)}, bf16[96,384]{1,0:T(8,128)(2,1)S(1)}, u32[]{:S(2)}, u32[]{:S(2)}) collective-permute-start(bf16[96,384]{1,0:T(8,128)(2,1)S(1)} %collective-permute-done.17.refs_4_), channel_id=1, source_target_pairs={{0,1},{1,0},{2,3},{3,2},{4,5},{5,4},{6,7},{7,6},{8,9},{9,8},{10,11... | collective-permute-start | bytes 221192 | tf_op jit(solution)/shard_map/ppermute | solution.py:252
  25.4 2.4 %collective-permute-start.20 = (bf16[96,384]{1,0:T(8,128)(2,1)S(1)}, bf16[96,384]{1,0:T(8,128)(2,1)S(1)}, u32[]{:S(2)}, u32[]{:S(2)}) collective-permute-start(bf16[96,384]{1,0:T(8,128)(2,1)S(1)} %collective-permute-done.19.refs_6_), channel_id=1, source_target_pairs={{0,1},{1,0},{2,3},{3,2},{4,5},{5,4},{6,7},{7,6},{8,9},{9,8},{10,11... | collective-permute-start | bytes 221192 | tf_op jit(solution)/shard_map/ppermute | solution.py:252
  25.9 1.2 %collective-permute-start.9 = (bf16[64,384]{1,0:T(8,128)(2,1)S(1)}, bf16[64,384]{1,0:T(8,128)(2,1)S(1)}, u32[]{:S(2)}, u32[]{:S(2)}) collective-permute-start(bf16[64,384]{1,0:T(8,128)(2,1)S(1)} %collective-permute-done.8.refs_10_), channel_id=1, source_target_pairs={{0,1},{1,0},{2,3},{3,2},{4,5},{5,4},{6,7},{7,6},{8,9},{9,8},{10,11... | collective-permute-start | bytes 147464 | tf_op jit(solution)/shard_map/ppermute | solution.py:252
  25.9 12.1 %collective-permute-start.11 = (bf16[64,384]{1,0:T(8,128)(2,1)S(1)}, bf16[64,384]{1,0:T(8,128)(2,1)S(1)}, u32[]{:S(2)}, u32[]{:S(2)}) collective-permute-start(bf16[64,384]{1,0:T(8,128)(2,1)S(1)} %collective-permute-done.10.refs_12_), channel_id=1, source_target_pairs={{0,1},{1,0},{2,3},{3,2},{4,5},{5,4},{6,7},{7,6},{8,9},{9,8},{10,11... | collective-permute-start | bytes 147464 | tf_op jit(solution)/shard_map/ppermute | solution.py:252
  27.1 11.0 %collective-permute-start.13 = (bf16[64,384]{1,0:T(8,128)(2,1)S(1)}, bf16[64,384]{1,0:T(8,128)(2,1)S(1)}, u32[]{:S(2)}, u32[]{:S(2)}) collective-permute-start(bf16[64,384]{1,0:T(8,128)(2,1)S(1)} %collective-permute-done.12.refs_14_), channel_id=1, source_target_pairs={{0,1},{1,0},{2,3},{3,2},{4,5},{5,4},{6,7},{7,6},{8,9},{9,8},{10,11... | collective-permute-start | bytes 147464 | tf_op jit(solution)/shard_map/ppermute | solution.py:252
  27.3 10.8 %collective-permute-start.2 = (bf16[80,384]{1,0:T(8,128)(2,1)S(1)}, bf16[80,384]{1,0:T(8,128)(2,1)S(1)}, u32[]{:S(2)}, u32[]{:S(2)}) collective-permute-start(bf16[80,384]{1,0:T(8,128)(2,1)S(1)} %collective-permute-done.1.refs_2_), channel_id=1, source_target_pairs={{0,1},{1,0},{2,3},{3,2},{4,5},{5,4},{6,7},{7,6},{8,9},{9,8},{10,11... | collective-permute-start | bytes 184328 | tf_op jit(solution)/shard_map/ppermute | solution.py:252
  27.6 10.5 %collective-permute-start.4 = (bf16[80,384]{1,0:T(8,128)(2,1)S(1)}, bf16[80,384]{1,0:T(8,128)(2,1)S(1)}, u32[]{:S(2)}, u32[]{:S(2)}) collective-permute-start(bf16[80,384]{1,0:T(8,128)(2,1)S(1)} %collective-permute-done.3.refs_4_), channel_id=1, source_target_pairs={{0,1},{1,0},{2,3},{3,2},{4,5},{5,4},{6,7},{7,6},{8,9},{9,8},{10,11... | collective-permute-start | bytes 184328 | tf_op jit(solution)/shard_map/ppermute | solution.py:252
  27.8 10.3 %collective-permute-start.6 = (bf16[80,384]{1,0:T(8,128)(2,1)S(1)}, bf16[80,384]{1,0:T(8,128)(2,1)S(1)}, u32[]{:S(2)}, u32[]{:S(2)}) collective-permute-start(bf16[80,384]{1,0:T(8,128)(2,1)S(1)} %collective-permute-done.5.refs_6_), channel_id=1, source_target_pairs={{0,1},{1,0},{2,3},{3,2},{4,5},{5,4},{6,7},{7,6},{8,9},{9,8},{10,11... | collective-permute-start | bytes 184328 | tf_op jit(solution)/shard_map/ppermute | solution.py:252
  28.1 3.3 %copy-start.4 = (bf16[3,3,3,384,384]{4,3,2,1,0:T(8,128)(2,1)S(1)}, bf16[3,3,3,384,384]{4,3,2,1,0:T(8,128)(2,1)}, u32[]{:S(2)}) copy-start(bf16[3,3,3,384,384]{4,3,2,1,0:T(8,128)(2,1)} %refs_8_.1) | copy-start | bytes 23887876

commit v2 on v1

v2 whole, which is shorter than its diff:
```python
import functools

import jax
import jax.numpy as jnp
from jax import lax
from jax.experimental import pallas as pl
from jax.experimental.pallas import tpu as pltpu
from jax.sharding import PartitionSpec as P


F32 = jnp.float32
BF16 = jnp.bfloat16
VMEM = pl.BlockSpec(memory_space=pltpu.VMEM)
SMEM = pl.BlockSpec(memory_space=pltpu.SMEM)
HBM = pl.BlockSpec(memory_space=pltpu.HBM)
LANES = 128


def lanes(channels):
    return [(at, slice(at * LANES, (at + 1) * LANES)) for at in range(channels // LANES)]


def pairing(count):
    if count & (count - 1) == 0:
        return [
            ([(i, i ^ s) for i in range(count)], lambda i, s=s: i ^ s, lambda i, s=s: i ^ s)
            for s in range(1, count)
        ]
    return [
        (
            [(i, (i + s) % count) for i in range(count)],
            lambda i, s=s: lax.rem(i + s, count),
            lambda i, s=s: lax.rem(i + count - s, count),
        )
        for s in range(1, count)
    ]


def silu_slope(values):
    sigmoid_of = jax.nn.sigmoid(values)
    return sigmoid_of * (1.0 + values * (1.0 - sigmoid_of))


def dot_last(a, b):
    return lax.dot_general(a, b, (((1,), (1,)), ((), ())), preferred_element_type=F32)


def pack_kernel(time_devs, halos, masked, *refs):
    count = len(halos)
    len_ref, ins = refs[0], refs[1 : 1 + count]
    outs, turned = refs[1 + count : -count], refs[-count:]
    me = lax.axis_index("tm")
    targets = [me] + [to(me) for _, to, _ in pairing(time_devs)]
    for at in range(count):
        ref, stage, halo = ins[at], turned[at], halos[at]
        frames, rows, cols, _ = ref.shape
        unit = frames * rows
        if halo:
            edge = jnp.zeros((stage.shape[0], halo * unit, LANES), F32)
            stage[:, 0 : halo * unit, :] = edge
            stage[:, (halo + cols) * unit :, :] = edge
        for frame in range(frames):
            for row in range(rows):
                value = ref[frame, row].astype(F32)
                if masked:
                    value = jnp.where(me * frames + frame < len_ref[0], value, 0.0)
                start = halo * unit + frame * rows + row
                for at_lane, lane in lanes(value.shape[1]):
                    stage[at_lane, pl.ds(start, cols, stride=unit), :] = value[:, lane]
        block = cols // time_devs
        size = (block + 2 * halo) * unit
        for step, target in enumerate(targets):
            start = pl.multiple_of(target * (block * unit), unit)
            for at_lane, lane in lanes(ref.shape[3]):
                outs[at * time_devs + step][:, lane] = stage[at_lane, pl.ds(start, size), :].astype(BF16)


def pack(arrays, lengths, halos, masked, time_devs):
    frames, rows, cols, channels = arrays[0].shape
    unit = frames * rows
    shapes = [
        jax.ShapeDtypeStruct(((cols // time_devs + 2 * halo) * unit, channels), BF16)
        for halo in halos
        for _ in range(time_devs)
    ]
    out = pl.pallas_call(
        functools.partial(pack_kernel, time_devs, halos, masked),
        out_shape=shapes,
        in_specs=[SMEM] + [VMEM] * len(arrays),
        out_specs=[VMEM] * len(shapes),
        scratch_shapes=[
            pltpu.VMEM((channels // LANES, (cols + 2 * halo) * unit, LANES), F32) for halo in halos
        ],
        compiler_params=pltpu.CompilerParams(vmem_limit_bytes=12 << 20),
        cost_estimate=pl.CostEstimate(flops=6 * 10**9, bytes_accessed=2 << 20, transcendentals=0),
    )(lengths, *arrays)
    return [out[at * time_devs : (at + 1) * time_devs] for at in range(len(arrays))]


def gather_block(dims, wins, halo, stage, dest, col_stride, row_pad):
    time_devs, row_devs, frame_dev, row_dev, col_dev = dims
    frames = time_devs * frame_dev
    unit = frame_dev * row_dev
    tm, row_at = lax.axis_index("tm"), lax.axis_index("rows")
    from_tm = [tm] + [source(tm) for _, _, source in pairing(time_devs)]
    from_row = [row_at] + [source(row_at) for _, _, source in pairing(row_devs)]
    cols = col_dev + 2 * halo
    for s in range(time_devs):
        for q in range(row_devs):
            at = s * row_devs + q
            first = row_at * (col_dev * unit)
            for at_lane, lane in lanes(wins[at].shape[1]):
                slot = at * dest.shape[0] + at_lane
                stage[slot, 0 : wins[at].shape[0], :] = wins[at][:, lane].astype(F32)
                for frame in range(frame_dev):
                    for row in range(row_dev):
                        start = first + frame * row_dev + row
                        target = (
                            (from_row[q] * row_dev + row + row_pad) * frames
                            + from_tm[s] * frame_dev
                            + frame
                        )
                        dest[at_lane, pl.ds(target, cols, stride=col_stride), :] = stage[
                            slot, pl.ds(start, cols, stride=unit), :
                        ]


def spread(full, targets, cols, rows, frames):
    size = cols * (rows + 2) * frames
    place = lax.rem(lax.broadcasted_iota(jnp.int32, (size, LANES), 0), frames)
    for a, target in enumerate(targets):
        for p in range(2):
            count = size - p * frames
            for at_lane, lane in lanes(target.shape[2]):
                value = full[at_lane, pl.ds(a + p * frames, count), :]
                value = jnp.where(place[:count] < frames - a, value, 0.0).astype(BF16)
                target[p, 0:count, lane] = value


def tap(shifts, r, c, cols, rows, frames):
    parity = r % 2
    start = (r - parity) * frames
    pitch = (rows + 2) * frames
    return jnp.concatenate(
        [
            shifts[parity, (c + w) * pitch + start : (c + w) * pitch + start + rows * frames, :]
            for w in range(cols)
        ],
        axis=0,
    )


def taps_of(shifts, weights, cols, rows, frames):
    order = [(r, c) for r in range(3) for c in range(3)]
    moved = jnp.concatenate([tap(shifts, r, c, cols, rows, frames) for r, c in order], axis=1)
    mixed = jnp.concatenate([weights[2 - r, 2 - c] for r, c in order], axis=1)
    return moved, mixed


def chunk_copy(source, at, target, sem):
    return pltpu.make_async_copy(source.at[2 - at], target, sem)


def first_kernel(dims, count, *refs):
    wins, weight_ref = refs[:count], refs[count]
    acc_ref, mid_ref, last_ref, next_ref = refs[count + 1 : count + 5]
    stage, full, shifts, buffer, sems = refs[count + 5 :]
    time_devs, row_devs, frame_dev, row_dev, col_dev = dims
    frames, rows = time_devs * frame_dev, row_devs * row_dev
    for a in range(2):
        chunk_copy(weight_ref, a, buffer.at[a], sems.at[a]).start()
    chunk_copy(weight_ref, 2, next_ref, sems.at[2]).start()
    full[...] = jnp.zeros_like(full)
    plane, pitch = rows * frames, (rows + 2) * frames
    gather_block(dims, wins, 2, stage, full, pitch, 1)
    spread(full, [shifts.at[0], shifts.at[1], last_ref], col_dev + 4, rows, frames)
    for w in range(col_dev):
        start = (w + 2) * pitch + frames
        mid_ref[:, w * plane : (w + 1) * plane, :] = full[:, start : start + plane, :]
    acc_ref[...] = jnp.zeros_like(acc_ref)

    @pl.loop(0, 2)
    def _(a):
        chunk_copy(weight_ref, a, buffer.at[a], sems.at[a]).wait()
        moved, mixed = taps_of(shifts.at[a], buffer.at[a], col_dev + 2, rows, frames)
        acc_ref[...] += dot_last(moved, mixed)

    chunk_copy(weight_ref, 2, next_ref, sems.at[2]).wait()


def last_tap_kernel(dims, acc_in, shifts, weights, acc_ref):
    time_devs, row_devs, frame_dev, row_dev, col_dev = dims
    frames, rows = time_devs * frame_dev, row_devs * row_dev
    moved, mixed = taps_of(shifts, weights, col_dev + 2, rows, frames)
    acc_ref[...] = acc_in[...] + dot_last(moved, mixed)


def second_kernel(dims, count, cols_all, *refs):
    hid = refs[:count]
    acc_ref, weight_ref, out_ref = refs[count : count + 3]
    stage, slopes, full, shifts, buffer, sems = refs[count + 3 :]
    time_devs, row_devs, frame_dev, row_dev, col_dev = dims
    frames, rows = time_devs * frame_dev, row_devs * row_dev
    for a in range(3):
        chunk_copy(weight_ref, a, buffer.at[a], sems.at[a]).start()
    plane, pitch = rows * frames, (rows + 2) * frames
    gather_block(dims, hid, 1, stage, slopes, plane, 0)
    full[...] = jnp.zeros_like(full)
    first_col = (lax.axis_index("tm") * row_devs + lax.axis_index("rows")) * col_dev - 1
    for w in range(col_dev + 2):
        col = first_col + w
        inside = jnp.logical_and(col >= 0, col < cols_all)
        here = slice(w * plane, (w + 1) * plane)
        start = w * pitch + frames
        for at_lane, lane in lanes(acc_ref.shape[1]):
            value = acc_ref[here, lane] * silu_slope(slopes[at_lane, here, :])
            full[at_lane, start : start + plane, :] = jnp.where(inside, value, 0.0)
    spread(full, [shifts.at[a] for a in range(3)], col_dev + 2, rows, frames)
    out_ref[...] = jnp.zeros_like(out_ref)

    @pl.loop(0, 3)
    def _(a):
        chunk_copy(weight_ref, a, buffer.at[a], sems.at[a]).wait()
        moved, mixed = taps_of(shifts.at[a], buffer.at[a], col_dev, rows, frames)
        out_ref[...] += dot_last(mixed, moved)


def final_kernel(dims, count, *refs):
    lat = refs[:count]
    acc_ref, mid_ref, out_ref, stage, slopes, full = refs[count:]
    time_devs, row_devs, frame_dev, row_dev, col_dev = dims
    frames, rows = time_devs * frame_dev, row_devs * row_dev
    plane = rows * frames
    gather_block(dims, lat, 0, stage, slopes, plane, 0)
    for at_lane, lane in lanes(acc_ref.shape[0]):
        full[at_lane] = mid_ref[at_lane] + acc_ref[lane, :].T * silu_slope(slopes[at_lane])
        for frame in range(frames):
            for row in range(rows):
                out_ref[0, frame, row, :, lane] = full[
                    at_lane, pl.ds(row * frames + frame, col_dev, stride=plane), :
                ]


def kernel_call(body, out_shape, in_specs, scratch, flops, room=24):
    return pl.pallas_call(
        body,
        out_shape=out_shape,
        in_specs=in_specs,
        out_specs=jax.tree.map(lambda _: VMEM, out_shape),
        scratch_shapes=scratch,
        compiler_params=pltpu.CompilerParams(vmem_limit_bytes=room << 20),
        cost_estimate=pl.CostEstimate(flops=flops, bytes_accessed=4 << 20, transcendentals=0),
    )


def on_device(latents, hidden, cotangent, conv_one, conv_two, lengths):
    _, frame_dev, row_dev, cols, channels = latents.shape
    time_devs, row_devs = lax.axis_size("tm"), lax.axis_size("rows")
    col_dev = cols // (time_devs * row_devs)
    frames, rows = time_devs * frame_dev, row_devs * row_dev
    unit = frame_dev * row_dev
    dims = (time_devs, row_devs, frame_dev, row_dev, col_dev)
    count = time_devs * row_devs
    plane, pitch = rows * frames, (rows + 2) * frames
    chip, parts = cols // time_devs, channels // LANES

    def over_tm(windows):
        out = [windows[0]]
        for step, (pairs, _, _) in enumerate(pairing(time_devs)):
            out.append(lax.ppermute(windows[step + 1], "tm", pairs))
        return out

    def over_rows(windows):
        out = []
        for window in windows:
            out.append(window)
            for pairs, _, _ in pairing(row_devs):
                out.append(lax.ppermute(window, "rows", pairs))
        return out

    def stage(halo):
        return pltpu.VMEM((count * parts, (chip + 2 * halo) * unit, LANES), F32)

    def part_rows(size):
        return pltpu.VMEM((parts, size, LANES), F32)

    mac = 2 * 9 * channels * channels
    wide, narrow = (col_dev + 2) * plane, col_dev * plane
    chunk = jax.ShapeDtypeStruct(conv_two.shape[1:], BF16)
    acc_shape = jax.ShapeDtypeStruct((wide, channels), F32)
    (cot,) = pack([cotangent[0]], lengths, (2,), True, time_devs)
    cot = over_rows(over_tm(cot))
    hid, lat = pack([hidden[0], latents[0]], lengths, (1, 0), False, time_devs)
    hid = over_rows(over_tm(hid))
    lat = over_rows(over_tm(lat))
    acc, mid, shifted, weights = kernel_call(
        functools.partial(first_kernel, dims, count),
        [
            acc_shape,
            jax.ShapeDtypeStruct((parts, narrow, LANES), F32),
            jax.ShapeDtypeStruct((2, (col_dev + 4) * pitch, channels), BF16),
            chunk,
        ],
        [VMEM] * count + [HBM],
        [
            stage(2),
            part_rows((col_dev + 4) * pitch + frames),
            pltpu.VMEM((2, 2, (col_dev + 4) * pitch, channels), BF16),
            pltpu.VMEM((2,) + chunk.shape, BF16),
            pltpu.SemaphoreType.DMA((3,)),
        ],
        2 * mac * wide,
    )(*cot, conv_two)
    acc = kernel_call(
        functools.partial(last_tap_kernel, dims), acc_shape, [VMEM] * 3, [], mac * wide
    )(acc, shifted, weights)
    grad = kernel_call(
        functools.partial(second_kernel, dims, count, cols),
        jax.ShapeDtypeStruct((channels, narrow), F32),
        [VMEM] * (count + 1) + [HBM],
        [
            stage(1),
            part_rows(wide),
            part_rows((col_dev + 2) * pitch + frames),
            pltpu.VMEM((3, 2, (col_dev + 2) * pitch, channels), BF16),
            pltpu.VMEM((3,) + chunk.shape, BF16),
            pltpu.SemaphoreType.DMA((3,)),
        ],
        3 * mac * narrow,
    )(*hid, acc, conv_one)
    return kernel_call(
        functools.partial(final_kernel, dims, count),
        jax.ShapeDtypeStruct((1, frames, rows, col_dev, channels), F32),
        [VMEM] * (count + 2),
        [stage(0), part_rows(narrow), part_rows(narrow)],
        1000000,
    )(*lat, grad, mid)


def solution(mesh):
    spec = P("dp", "tm", "rows", None, None)
    return jax.shard_map(
        on_device,
        mesh=mesh,
        in_specs=(spec, spec, spec, P(), P(), P("dp")),
        out_specs=P("dp", None, None, ("tm", "rows"), None),
        check_vma=False,
    )
```

time: 44.8 us -> 39.4 us (0.88); the launches traced: 44.2 us -> 39.2 us
  local copies, waits for them, and re-layouts: 6.49 us -> 0.94 us
  waiting for transfers between devices: 5.24 us -> 7.94 us
  starting transfers between devices: 18.4 us -> 16.4 us
    unnamed x10 -> x14, local copies, waits for them, and re-layouts: 6.49 us -> 0.94 us
    ppermute x21, waiting for transfers between devices: 5.24 us -> 7.94 us  [the longest x9 7.91 us: over_tm(): out.append(lax.ppermute(windows[step + 1], 'tm', pairs))]
    ppermute x21, starting transfers between devices: 18.4 us -> 16.4 us  [the longest x9 14.3 us: over_tm(): out.append(lax.ppermute(windows[step + 1], 'tm', pairs))]
    pallas_call x2 -> x4, Pallas kernels: 12.7 us -> 12.7 us  [the longest x1 5.08 us: on_device(): kernel_call(functools.partial(first_kernel, dims, count), [acc_shape, jax...]
  transfers between devices with their start and end apart: 21 -> 21, of which waited for: 4 -> 3; matrix products, arithmetic and copies ran while one was open for 0% -> 0% of each run, Pallas kernels for 15% -> 29%
where the time goes in v2:
time: 39.4 us; the launch traced here: 39.2 us
  starting transfers between devices  16.4 us (42%)
  Pallas kernels  13.1 us (33%)
  waiting for transfers between devices  7.94 us (20%)
  local copies, waits for them, and re-layouts  0.94 us (2%)
  between operations  0.81 us (2%)
    ppermute x9, starting transfers between devices, over_tm(): out.append(lax.ppermute(windows[step + 1], 'tm', pairs))  14.3 us
    ppermute x9, waiting for transfers between devices, over_tm(): out.append(lax.ppermute(windows[step + 1], 'tm', pairs))  7.91 us
    pallas_call x1, Pallas kernels, on_device(): kernel_call(functools.partial(first_kernel, dims, count), [acc_shape, jax...  5.08 us
    pallas_call x1, Pallas kernels, on_device(): kernel_call(functools.partial(second_kernel, dims, count, cols), jax.Shap...  4.64 us
    ppermute x12, starting transfers between devices, over_rows(): out.append(lax.ppermute(window, 'rows', pairs))  2.18 us
    pallas_call x1, Pallas kernels, on_device(): kernel_call(functools.partial(last_tap_kernel, dims), acc_shape, [VMEM] *...  1.56 us
    pallas_call x1, Pallas kernels, on_device(): kernel_call(functools.partial(final_kernel, dims, count), jax.ShapeDtypeS...  1.43 us
    unnamed x14, local copies, waits for them, and re-layouts  0.94 us
  transfers between devices with their start and end apart: 21, of which 3 were waited for; matrix products, arithmetic and copies ran while one was open for 0% of the time, Pallas kernels for 29%

profile of v2, /device:TPU:0, one launch (start us, length us, event | category | flops | bytes accessed | tf_op | source)
XLA Modules:
  0.0 39.2 jit_solution(8534772559509932639)
XLA Ops:
  0.7 0.0 copy-start
  0.7 0.9 %copy-done = bf16[1,2,4,32,384]{4,3,2,1,0:T(8,128)(2,1)S(1)} copy-done((bf16[1,2,4,32,384]{4,3,2,1,0:T(8,128)(2,1)S(1)}, bf16[1,2,4,32,384]{4,3,2,1,0:T(8,128)(2,1)}, u32[]{:S(2)}) %copy-start) | copy-done | bytes 196632
  1.6 0.0 copy-start.1
  1.6 0.0 copy-start.2
  1.6 0.0 slice-start
  1.6 0.1 shard_map.65
  1.7 3.1 %collective-permute-start.15 = (bf16[96,384]{1,0:T(8,128)(2,1)S(1)}, bf16[96,384]{1,0:T(8,128)(2,1)S(1)}, u32[]{:S(2)}, u32[]{:S(2)}) collective-permute-start(bf16[96,384]{1,0:T(8,128)(2,1)S(1)} %get-tuple-element.30), channel_id=1, source_target_pairs={{0,2},{2,0},{4,6},{6,4},{1,3},{3,1},{5,7},{7,5},{8,10},{10,8},{12,... | collective-permute-start | bytes 221192 | tf_op jit(solution)/shard_map/ppermute | solution.py:270
  4.9 2.6 %collective-permute-start.17 = (bf16[96,384]{1,0:T(8,128)(2,1)S(1)}, bf16[96,384]{1,0:T(8,128)(2,1)S(1)}, u32[]{:S(2)}, u32[]{:S(2)}) collective-permute-start(bf16[96,384]{1,0:T(8,128)(2,1)S(1)} %get-tuple-element.31), channel_id=1, source_target_pairs={{0,4},{2,6},{4,0},{6,2},{1,5},{3,7},{5,1},{7,3},{8,12},{10,14},{12... | collective-permute-start | bytes 221192 | tf_op jit(solution)/shard_map/ppermute | solution.py:270
  7.4 0.0 collective-permute-start.19
  7.5 0.0 collective-permute-start.14
  7.5 0.0 collective-permute-done.15.refs_2_
  7.5 0.5 %collective-permute-start.16 = (bf16[96,384]{1,0:T(8,128)(2,1)S(1)}, bf16[96,384]{1,0:T(8,128)(2,1)S(1)}, u32[]{:S(2)}, u32[]{:S(2)}) collective-permute-start(bf16[96,384]{1,0:T(8,128)(2,1)S(1)} %collective-permute-done.15.refs_2_), channel_id=1, source_target_pairs={{0,1},{1,0},{2,3},{3,2},{4,5},{5,4},{6,7},{7,6},{8,9},{9,8},{10,11... | collective-permute-start | bytes 221192 | tf_op jit(solution)/shard_map/ppermute | solution.py:278
  8.0 4.7 %collective-permute-done.17.refs_4_ = bf16[96,384]{1,0:T(8,128)(2,1)S(1)} collective-permute-done((bf16[96,384]{1,0:T(8,128)(2,1)S(1)}, bf16[96,384]{1,0:T(8,128)(2,1)S(1)}, u32[]{:S(2)}, u32[]{:S(2)}) %collective-permute-start.17) | collective-permute-done | bytes 73760 | tf_op jit(solution)/shard_map/ppermute | solution.py:270
  12.6 0.0 collective-permute-start.18
  12.6 1.1 %collective-permute-done.19.refs_6_ = bf16[96,384]{1,0:T(8,128)(2,1)S(1)} collective-permute-done((bf16[96,384]{1,0:T(8,128)(2,1)S(1)}, bf16[96,384]{1,0:T(8,128)(2,1)S(1)}, u32[]{:S(2)}, u32[]{:S(2)}) %collective-permute-start.19) | collective-permute-done | bytes 73760 | tf_op jit(solution)/shard_map/ppermute | solution.py:270
  13.7 0.0 collective-permute-start.20
  13.7 0.0 slice-start.1
  13.7 0.0 slice-start.2
  13.7 0.0 copy-done.1
  13.7 0.0 copy-done.2
  13.7 0.0 slice-start.3
  13.7 0.2 shard_map.64
  14.0 2.2 %collective-permute-start.10 = (bf16[80,384]{1,0:T(8,128)(2,1)S(1)}, bf16[80,384]{1,0:T(8,128)(2,1)S(1)}, u32[]{:S(2)}, u32[]{:S(2)}) collective-permute-start(bf16[80,384]{1,0:T(8,128)(2,1)S(1)} %get-tuple-element.27), channel_id=1, source_target_pairs={{0,4},{2,6},{4,0},{6,2},{1,5},{3,7},{5,1},{7,3},{8,12},{10,14},{12... | collective-permute-start | bytes 184328 | tf_op jit(solution)/shard_map/ppermute | solution.py:270
  16.2 0.0 collective-permute-done.14.refs_1_
  16.2 1.3 %collective-permute-start.12 = (bf16[80,384]{1,0:T(8,128)(2,1)S(1)}, bf16[80,384]{1,0:T(8,128)(2,1)S(1)}, u32[]{:S(2)}, u32[]{:S(2)}) collective-permute-start(bf16[80,384]{1,0:T(8,128)(2,1)S(1)} %get-tuple-element.28), channel_id=1, source_target_pairs={{0,6},{2,4},{4,2},{6,0},{1,7},{3,5},{5,3},{7,1},{8,14},{10,12},{12... | collective-permute-start | bytes 184328 | tf_op jit(solution)/shard_map/ppermute | solution.py:270
  17.5 0.0 collective-permute-done.16.refs_3_
  17.5 0.0 collective-permute-start.8
  17.6 0.0 collective-permute-done.18.refs_5_
  17.6 2.0 %collective-permute-start.1 = (bf16[64,384]{1,0:T(8,128)(2,1)S(1)}, bf16[64,384]{1,0:T(8,128)(2,1)S(1)}, u32[]{:S(2)}, u32[]{:S(2)}) collective-permute-start(bf16[64,384]{1,0:T(8,128)(2,1)S(1)} %get-tuple-element.22), channel_id=1, source_target_pairs={{0,2},{2,0},{4,6},{6,4},{1,3},{3,1},{5,7},{7,5},{8,10},{10,8},{12,... | collective-permute-start | bytes 147464 | tf_op jit(solution)/shard_map/ppermute | solution.py:270
  19.5 0.0 collective-permute-done.20.refs_7_
  19.5 1.3 %collective-permute-start.3 = (bf16[64,384]{1,0:T(8,128)(2,1)S(1)}, bf16[64,384]{1,0:T(8,128)(2,1)S(1)}, u32[]{:S(2)}, u32[]{:S(2)}) collective-permute-start(bf16[64,384]{1,0:T(8,128)(2,1)S(1)} %get-tuple-element.23), channel_id=1, source_target_pairs={{0,4},{2,6},{4,0},{6,2},{1,5},{3,7},{5,1},{7,3},{8,12},{10,14},{12... | collective-permute-start | bytes 147464 | tf_op jit(solution)/shard_map/ppermute | solution.py:270
  20.8 0.0 slice-done
  20.8 0.0 slice-done.1
  20.8 5.1 %shard_map.66 = (f32[384,384]{1,0:T(8,128)S(1)}, f32[3,256,128]{2,1,0:T(8,128)S(1)}, bf16[2,640,384]{2,1,0:T(8,128)(2,1)S(1)}, bf16[3,3,384,384]{3,2,1,0:T(8,128)(2,1)S(1)}) custom-call(bf16[96,384]{1,0:T(8,128)(2,1)S(1)} %get-tuple-element.29.refs_0_, bf16[96,384]{1,0:T(8,128)(2,1)S(1)} %collective-permute-done.14.refs_1_, ...), custom_call_target="tpu_custom_call" | custom-call | flops 2038431744 | bytes 4194304 | tf_op jit(solution)/shard_map/pallas_call | solution.py:296
  25.9 0.0 collective-permute-done.1.refs_2_
  25.9 0.1 collective-permute-start.7
  26.0 0.0 collective-permute-done.3.refs_4_
  26.0 1.7 %collective-permute-start.5 = (bf16[64,384]{1,0:T(8,128)(2,1)S(1)}, bf16[64,384]{1,0:T(8,128)(2,1)S(1)}, u32[]{:S(2)}, u32[]{:S(2)}) collective-permute-start(bf16[64,384]{1,0:T(8,128)(2,1)S(1)} %get-tuple-element.24), channel_id=1, source_target_pairs={{0,6},{2,4},{4,2},{6,0},{1,7},{3,5},{5,3},{7,1},{8,14},{10,12},{12... | collective-permute-start | bytes 147464 | tf_op jit(solution)/shard_map/ppermute | solution.py:270
  27.7 0.0 collective-permute-done.10.refs_4_
  27.7 0.0 collective-permute-start.11
  27.7 0.0 collective-permute-done.12.refs_6_
  27.8 0.5 %collective-permute-start.13 = (bf16[80,384]{1,0:T(8,128)(2,1)S(1)}, bf16[80,384]{1,0:T(8,128)(2,1)S(1)}, u32[]{:S(2)}, u32[]{:S(2)}) collective-permute-start(bf16[80,384]{1,0:T(8,128)(2,1)S(1)} %collective-permute-done.12.refs_6_), channel_id=1, source_target_pairs={{0,1},{1,0},{2,3},{3,2},{4,5},{5,4},{6,7},{7,6},{8,9},{9,8},{10,11... | collective-permute-start | bytes 184328 | tf_op jit(solution)/shard_map/ppermute | solution.py:278
  28.3 0.0 collective-permute-done.8.refs_2_
  28.3 0.1 collective-permute-start.9
  28.3 1.6 %shard_map.67.refs_8_ = f32[384,384]{1,0:T(8,128)S(1)} custom-call(f32[384,384]{1,0:T(8,128)S(1)} %get-tuple-element.33.acc_in, bf16[2,640,384]{2,1,0:T(8,128)(2,1)S(1)} %get-tuple-element.34.shifts, bf16[3,3,384,384]{3,2,1,0:T(8,128)(2,1)S(1)} %get-tuple-element.35.weights), custom_call_target="tpu_custom_call" | custom-call | flops 1019215872 | bytes 4194304 | tf_op jit(solution)/shard_map/pallas_call | solution.py:314
  29.9 2.2 %collective-permute-done.5.refs_6_ = bf16[64,384]{1,0:T(8,128)(2,1)S(1)} collective-permute-done((bf16[64,384]{1,0:T(8,128)(2,1)S(1)}, bf16[64,384]{1,0:T(8,128)(2,1)S(1)}, u32[]{:S(2)}, u32[]{:S(2)}) %collective-permute-start.5) | collective-permute-done | bytes 49184 | tf_op jit(solution)/shard_map/ppermute | solution.py:270
  32.1 0.0 collective-permute-start
  32.1 0.0 collective-permute-done.7.refs_1_
  32.1 0.5 %collective-permute-start.2 = (bf16[64,384]{1,0:T(8,128)(2,1)S(1)}, bf16[64,384]{1,0:T(8,128)(2,1)S(1)}, u32[]{:S(2)}, u32[]{:S(2)}) collective-permute-start(bf16[64,384]{1,0:T(8,128)(2,1)S(1)} %collective-permute-done.1.refs_2_), channel_id=1, source_target_pairs={{0,1},{1,0},{2,3},{3,2},{4,5},{5,4},{6,7},{7,6},{8,9},{9,8},{10,11... | collective-permute-start | bytes 147464 | tf_op jit(solution)/shard_map/ppermute | solution.py:278
  32.6 0.0 collective-permute-done.11.refs_5_
  32.6 0.1 collective-permute-start.4
  32.7 0.0 collective-permute-done.13.refs_7_
  32.7 0.4 %collective-permute-start.6 = (bf16[64,384]{1,0:T(8,128)(2,1)S(1)}, bf16[64,384]{1,0:T(8,128)(2,1)S(1)}, u32[]{:S(2)}, u32[]{:S(2)}) collective-permute-start(bf16[64,384]{1,0:T(8,128)(2,1)S(1)} %collective-permute-done.5.refs_6_), channel_id=1, source_target_pairs={{0,1},{1,0},{2,3},{3,2},{4,5},{5,4},{6,7},{7,6},{8,9},{9,8},{10,11... | collective-permute-start | bytes 147464 | tf_op jit(solution)/shard_map/ppermute | solution.py:278
  33.1 0.0 collective-permute-done.9.refs_3_
  33.1 0.0 slice-done.2
  33.1 0.0 slice-done.3
  33.1 4.6 %shard_map.68.refs_8_ = f32[384,256]{1,0:T(8,128)S(1)} custom-call(bf16[80,384]{1,0:T(8,128)(2,1)S(1)} %get-tuple-element.25.refs_0_, bf16[80,384]{1,0:T(8,128)(2,1)S(1)} %collective-permute-done.7.refs_1_, bf16[80,384]{1,0:T(8,128)(2,1)S(1)} %collective-permute-done.8.refs_2_, bf16[80,384]{1,0:T(8,128)(2,1)S(1)} %collective-permute-done.9.refs_3_, ...), custom_call_target="tpu_custom_call" | custom-call | flops 2038431744 | bytes 4194304 | tf_op jit(solution)/shard_map/pallas_call | solution.py:317
  37.8 0.0 collective-permute-done.refs_1_
  37.8 0.0 collective-permute-done.2.refs_3_
  37.8 0.0 collective-permute-done.4.refs_5_
  37.8 0.0 collective-permute-done.6.refs_7_
  37.8 1.4 %shard_map.69 = f32[1,8,8,4,384]{4,3,2,1,0:T(4,128)} custom-call(bf16[64,384]{1,0:T(8,128)(2,1)S(1)} %get-tuple-element.21.refs_0_, bf16[64,384]{1,0:T(8,128)(2,1)S(1)} %collective-permute-done.refs_1_, bf16[64,384]{1,0:T(8,128)(2,1)S(1)} %collective-permute-done.1.refs_2_, bf16[64,384]{1,0:T(8,128)(2,1)S(1)} %collective-permute-done.2.refs_3_, ...), custom_call_target="tpu_custom_call" | custom-call | flops 1000000 | bytes 4194304 | tf_op jit(solution)/shard_map/pallas_call | solution.py:331
  (2 shorter events, 0.0 us)
Async XLA Ops:
  0.7 0.9 %copy-start = (bf16[1,2,4,32,384]{4,3,2,1,0:T(8,128)(2,1)S(1)}, bf16[1,2,4,32,384]{4,3,2,1,0:T(8,128)(2,1)}, u32[]{:S(2)}) copy-start(bf16[1,2,4,32,384]{4,3,2,1,0:T(8,128)(2,1)} %param.8) | copy-start | bytes 589828
  1.6 12.1 %copy-start.1 = (bf16[1,2,4,32,384]{4,3,2,1,0:T(8,128)(2,1)S(1)}, bf16[1,2,4,32,384]{4,3,2,1,0:T(8,128)(2,1)}, u32[]{:S(2)}) copy-start(bf16[1,2,4,32,384]{4,3,2,1,0:T(8,128)(2,1)} %param.7) | copy-start | bytes 589828
  1.6 12.1 %copy-start.2 = (bf16[1,2,4,32,384]{4,3,2,1,0:T(8,128)(2,1)S(1)}, bf16[1,2,4,32,384]{4,3,2,1,0:T(8,128)(2,1)}, u32[]{:S(2)}) copy-start(bf16[1,2,4,32,384]{4,3,2,1,0:T(8,128)(2,1)} %param.6) | copy-start | bytes 589828
  1.6 19.3 %slice-start = ((s8[7962624]{0:T(1024)(128)(4,1)}), s8[4194304]{0:T(1024)(128)(4,1)S(1)}, s32[]{:S(2)}) async-start(s8[7962624]{0:T(1024)(128)(4,1)} %bitcast.3), calls=%async_computation | async-start | bytes 8388608
  1.7 5.7 %collective-permute-start.15 = (bf16[96,384]{1,0:T(8,128)(2,1)S(1)}, bf16[96,384]{1,0:T(8,128)(2,1)S(1)}, u32[]{:S(2)}, u32[]{:S(2)}) collective-permute-start(bf16[96,384]{1,0:T(8,128)(2,1)S(1)} %get-tuple-element.30), channel_id=1, source_target_pairs={{0,2},{2,0},{4,6},{6,4},{1,3},{3,1},{5,7},{7,5},{8,10},{10,8},{12,... | collective-permute-start | bytes 221192 | tf_op jit(solution)/shard_map/ppermute | solution.py:270
  4.9 7.8 %collective-permute-start.17 = (bf16[96,384]{1,0:T(8,128)(2,1)S(1)}, bf16[96,384]{1,0:T(8,128)(2,1)S(1)}, u32[]{:S(2)}, u32[]{:S(2)}) collective-permute-start(bf16[96,384]{1,0:T(8,128)(2,1)S(1)} %get-tuple-element.31), channel_id=1, source_target_pairs={{0,4},{2,6},{4,0},{6,2},{1,5},{3,7},{5,1},{7,3},{8,12},{10,14},{12... | collective-permute-start | bytes 221192 | tf_op jit(solution)/shard_map/ppermute | solution.py:270
  7.4 6.3 %collective-permute-start.19 = (bf16[96,384]{1,0:T(8,128)(2,1)S(1)}, bf16[96,384]{1,0:T(8,128)(2,1)S(1)}, u32[]{:S(2)}, u32[]{:S(2)}) collective-permute-start(bf16[96,384]{1,0:T(8,128)(2,1)S(1)} %get-tuple-element.32), channel_id=1, source_target_pairs={{0,6},{2,4},{4,2},{6,0},{1,7},{3,5},{5,3},{7,1},{8,14},{10,12},{12... | collective-permute-start | bytes 221192 | tf_op jit(solution)/shard_map/ppermute | solution.py:270
  7.5 8.7 %collective-permute-start.14 = (bf16[96,384]{1,0:T(8,128)(2,1)S(1)}, bf16[96,384]{1,0:T(8,128)(2,1)S(1)}, u32[]{:S(2)}, u32[]{:S(2)}) collective-permute-start(bf16[96,384]{1,0:T(8,128)(2,1)S(1)} %get-tuple-element.29.refs_0_), channel_id=1, source_target_pairs={{0,1},{1,0},{2,3},{3,2},{4,5},{5,4},{6,7},{7,6},{8,9},{9,8},{10,11... | collective-permute-start | bytes 221192 | tf_op jit(solution)/shard_map/ppermute | solution.py:278
  7.5 10.0 %collective-permute-start.16 = (bf16[96,384]{1,0:T(8,128)(2,1)S(1)}, bf16[96,384]{1,0:T(8,128)(2,1)S(1)}, u32[]{:S(2)}, u32[]{:S(2)}) collective-permute-start(bf16[96,384]{1,0:T(8,128)(2,1)S(1)} %collective-permute-done.15.refs_2_), channel_id=1, source_target_pairs={{0,1},{1,0},{2,3},{3,2},{4,5},{5,4},{6,7},{7,6},{8,9},{9,8},{10,11... | collective-permute-start | bytes 221192 | tf_op jit(solution)/shard_map/ppermute | solution.py:278
  12.6 4.9 %collective-permute-start.18 = (bf16[96,384]{1,0:T(8,128)(2,1)S(1)}, bf16[96,384]{1,0:T(8,128)(2,1)S(1)}, u32[]{:S(2)}, u32[]{:S(2)}) collective-permute-start(bf16[96,384]{1,0:T(8,128)(2,1)S(1)} %collective-permute-done.17.refs_4_), channel_id=1, source_target_pairs={{0,1},{1,0},{2,3},{3,2},{4,5},{5,4},{6,7},{7,6},{8,9},{9,8},{10,11... | collective-permute-start | bytes 221192 | tf_op jit(solution)/shard_map/ppermute | solution.py:278
  13.7 5.8 %collective-permute-start.20 = (bf16[96,384]{1,0:T(8,128)(2,1)S(1)}, bf16[96,384]{1,0:T(8,128)(2,1)S(1)}, u32[]{:S(2)}, u32[]{:S(2)}) collective-permute-start(bf16[96,384]{1,0:T(8,128)(2,1)S(1)} %collective-permute-done.19.refs_6_), channel_id=1, source_target_pairs={{0,1},{1,0},{2,3},{3,2},{4,5},{5,4},{6,7},{7,6},{8,9},{9,8},{10,11... | collective-permute-start | bytes 221192 | tf_op jit(solution)/shard_map/ppermute | solution.py:278
  13.7 7.1 %slice-start.1 = ((s8[7962624]{0:T(1024)(128)(4,1)}), s8[3768320]{0:T(1024)(128)(4,1)S(1)}, s32[]{:S(2)}) async-start(s8[7962624]{0:T(1024)(128)(4,1)} %bitcast.3), calls=%async_computation.1 | async-start | bytes 7536640
  13.7 19.4 %slice-start.2 = ((s8[7962624]{0:T(1024)(128)(4,1)}), s8[4194304]{0:T(1024)(128)(4,1)S(1)}, s32[]{:S(2)}) async-start(s8[7962624]{0:T(1024)(128)(4,1)} %bitcast.5), calls=%async_computation.2 | async-start | bytes 8388608
  13.7 19.4 %slice-start.3 = ((s8[7962624]{0:T(1024)(128)(4,1)}), s8[3768320]{0:T(1024)(128)(4,1)S(1)}, s32[]{:S(2)}) async-start(s8[7962624]{0:T(1024)(128)(4,1)} %bitcast.5), calls=%async_computation.3 | async-start | bytes 7536640
  14.0 13.8 %collective-permute-start.10 = (bf16[80,384]{1,0:T(8,128)(2,1)S(1)}, bf16[80,384]{1,0:T(8,128)(2,1)S(1)}, u32[]{:S(2)}, u32[]{:S(2)}) collective-permute-start(bf16[80,384]{1,0:T(8,128)(2,1)S(1)} %get-tuple-element.27), channel_id=1, source_target_pairs={{0,4},{2,6},{4,0},{6,2},{1,5},{3,7},{5,1},{7,3},{8,12},{10,14},{12... | collective-permute-start | bytes 184328 | tf_op jit(solution)/shard_map/ppermute | solution.py:270
  16.2 11.6 %collective-permute-start.12 = (bf16[80,384]{1,0:T(8,128)(2,1)S(1)}, bf16[80,384]{1,0:T(8,128)(2,1)S(1)}, u32[]{:S(2)}, u32[]{:S(2)}) collective-permute-start(bf16[80,384]{1,0:T(8,128)(2,1)S(1)} %get-tuple-element.28), channel_id=1, source_target_pairs={{0,6},{2,4},{4,2},{6,0},{1,7},{3,5},{5,3},{7,1},{8,14},{10,12},{12... | collective-permute-start | bytes 184328 | tf_op jit(solution)/shard_map/ppermute | solution.py:270
  17.5 10.8 %collective-permute-start.8 = (bf16[80,384]{1,0:T(8,128)(2,1)S(1)}, bf16[80,384]{1,0:T(8,128)(2,1)S(1)}, u32[]{:S(2)}, u32[]{:S(2)}) collective-permute-start(bf16[80,384]{1,0:T(8,128)(2,1)S(1)} %get-tuple-element.26), channel_id=1, source_target_pairs={{0,2},{2,0},{4,6},{6,4},{1,3},{3,1},{5,7},{7,5},{8,10},{10,8},{12,... | collective-permute-start | bytes 184328 | tf_op jit(solution)/shard_map/ppermute | solution.py:270
  17.6 8.4 %collective-permute-start.1 = (bf16[64,384]{1,0:T(8,128)(2,1)S(1)}, bf16[64,384]{1,0:T(8,128)(2,1)S(1)}, u32[]{:S(2)}, u32[]{:S(2)}) collective-permute-start(bf16[64,384]{1,0:T(8,128)(2,1)S(1)} %get-tuple-element.22), channel_id=1, source_target_pairs={{0,2},{2,0},{4,6},{6,4},{1,3},{3,1},{5,7},{7,5},{8,10},{10,8},{12,... | collective-permute-start | bytes 147464 | tf_op jit(solution)/shard_map/ppermute | solution.py:270
  19.5 6.5 %collective-permute-start.3 = (bf16[64,384]{1,0:T(8,128)(2,1)S(1)}, bf16[64,384]{1,0:T(8,128)(2,1)S(1)}, u32[]{:S(2)}, u32[]{:S(2)}) collective-permute-start(bf16[64,384]{1,0:T(8,128)(2,1)S(1)} %get-tuple-element.23), channel_id=1, source_target_pairs={{0,4},{2,6},{4,0},{6,2},{1,5},{3,7},{5,1},{7,3},{8,12},{10,14},{12... | collective-permute-start | bytes 147464 | tf_op jit(solution)/shard_map/ppermute | solution.py:270
  25.9 6.1 %collective-permute-start.7 = (bf16[80,384]{1,0:T(8,128)(2,1)S(1)}, bf16[80,384]{1,0:T(8,128)(2,1)S(1)}, u32[]{:S(2)}, u32[]{:S(2)}) collective-permute-start(bf16[80,384]{1,0:T(8,128)(2,1)S(1)} %get-tuple-element.25.refs_0_), channel_id=1, source_target_pairs={{0,1},{1,0},{2,3},{3,2},{4,5},{5,4},{6,7},{7,6},{8,9},{9,8},{10,11... | collective-permute-start | bytes 184328 | tf_op jit(solution)/shard_map/ppermute | solution.py:278
  26.0 6.0 %collective-permute-start.5 = (bf16[64,384]{1,0:T(8,128)(2,1)S(1)}, bf16[64,384]{1,0:T(8,128)(2,1)S(1)}, u32[]{:S(2)}, u32[]{:S(2)}) collective-permute-start(bf16[64,384]{1,0:T(8,128)(2,1)S(1)} %get-tuple-element.24), channel_id=1, source_target_pairs={{0,6},{2,4},{4,2},{6,0},{1,7},{3,5},{5,3},{7,1},{8,14},{10,12},{12... | collective-permute-start | bytes 147464 | tf_op jit(solution)/shard_map/ppermute | solution.py:270
  27.7 4.8 %collective-permute-start.11 = (bf16[80,384]{1,0:T(8,128)(2,1)S(1)}, bf16[80,384]{1,0:T(8,128)(2,1)S(1)}, u32[]{:S(2)}, u32[]{:S(2)}) collective-permute-start(bf16[80,384]{1,0:T(8,128)(2,1)S(1)} %collective-permute-done.10.refs_4_), channel_id=1, source_target_pairs={{0,1},{1,0},{2,3},{3,2},{4,5},{5,4},{6,7},{7,6},{8,9},{9,8},{10,11... | collective-permute-start | bytes 184328 | tf_op jit(solution)/shard_map/ppermute | solution.py:278
  27.8 4.9 %collective-permute-start.13 = (bf16[80,384]{1,0:T(8,128)(2,1)S(1)}, bf16[80,384]{1,0:T(8,128)(2,1)S(1)}, u32[]{:S(2)}, u32[]{:S(2)}) collective-permute-start(bf16[80,384]{1,0:T(8,128)(2,1)S(1)} %collective-permute-done.12.refs_6_), channel_id=1, source_target_pairs={{0,1},{1,0},{2,3},{3,2},{4,5},{5,4},{6,7},{7,6},{8,9},{9,8},{10,11... | collective-permute-start | bytes 184328 | tf_op jit(solution)/shard_map/ppermute | solution.py:278
  28.3 4.8 %collective-permute-start.9 = (bf16[80,384]{1,0:T(8,128)(2,1)S(1)}, bf16[80,384]{1,0:T(8,128)(2,1)S(1)}, u32[]{:S(2)}, u32[]{:S(2)}) collective-permute-start(bf16[80,384]{1,0:T(8,128)(2,1)S(1)} %collective-permute-done.8.refs_2_), channel_id=1, source_target_pairs={{0,1},{1,0},{2,3},{3,2},{4,5},{5,4},{6,7},{7,6},{8,9},{9,8},{10,11... | collective-permute-start | bytes 184328 | tf_op jit(solution)/shard_map/ppermute | solution.py:278
  32.1 5.7 %collective-permute-start = (bf16[64,384]{1,0:T(8,128)(2,1)S(1)}, bf16[64,384]{1,0:T(8,128)(2,1)S(1)}, u32[]{:S(2)}, u32[]{:S(2)}) collective-permute-start(bf16[64,384]{1,0:T(8,128)(2,1)S(1)} %get-tuple-element.21.refs_0_), channel_id=1, source_target_pairs={{0,1},{1,0},{2,3},{3,2},{4,5},{5,4},{6,7},{7,6},{8,9},{9,8},{10,11... | collective-permute-start | bytes 147464 | tf_op jit(solution)/shard_map/ppermute | solution.py:278
  32.1 5.7 %collective-permute-start.2 = (bf16[64,384]{1,0:T(8,128)(2,1)S(1)}, bf16[64,384]{1,0:T(8,128)(2,1)S(1)}, u32[]{:S(2)}, u32[]{:S(2)}) collective-permute-start(bf16[64,384]{1,0:T(8,128)(2,1)S(1)} %collective-permute-done.1.refs_2_), channel_id=1, source_target_pairs={{0,1},{1,0},{2,3},{3,2},{4,5},{5,4},{6,7},{7,6},{8,9},{9,8},{10,11... | collective-permute-start | bytes 147464 | tf_op jit(solution)/shard_map/ppermute | solution.py:278
  32.6 5.2 %collective-permute-start.4 = (bf16[64,384]{1,0:T(8,128)(2,1)S(1)}, bf16[64,384]{1,0:T(8,128)(2,1)S(1)}, u32[]{:S(2)}, u32[]{:S(2)}) collective-permute-start(bf16[64,384]{1,0:T(8,128)(2,1)S(1)} %collective-permute-done.3.refs_4_), channel_id=1, source_target_pairs={{0,1},{1,0},{2,3},{3,2},{4,5},{5,4},{6,7},{7,6},{8,9},{9,8},{10,11... | collective-permute-start | bytes 147464 | tf_op jit(solution)/shard_map/ppermute | solution.py:278
  32.7 5.1 %collective-permute-start.6 = (bf16[64,384]{1,0:T(8,128)(2,1)S(1)}, bf16[64,384]{1,0:T(8,128)(2,1)S(1)}, u32[]{:S(2)}, u32[]{:S(2)}) collective-permute-start(bf16[64,384]{1,0:T(8,128)(2,1)S(1)} %collective-permute-done.5.refs_6_), channel_id=1, source_target_pairs={{0,1},{1,0},{2,3},{3,2},{4,5},{5,4},{6,7},{7,6},{8,9},{9,8},{10,11... | collective-permute-start | bytes 147464 | tf_op jit(solution)/shard_map/ppermute | solution.py:278

commit v3 on v2

--- a/solution.py
+++ b/solution.py
@@ -14,6 +14,7 @@
 SMEM = pl.BlockSpec(memory_space=pltpu.SMEM)
 HBM = pl.BlockSpec(memory_space=pltpu.HBM)
 LANES = 128
+STEPS = {4: (2, 3, 1)}
 
 
 def lanes(channels):
@@ -24,7 +25,7 @@
     if count & (count - 1) == 0:
         return [
             ([(i, i ^ s) for i in range(count)], lambda i, s=s: i ^ s, lambda i, s=s: i ^ s)
-            for s in range(1, count)
+            for s in STEPS.get(count, range(1, count))
         ]
     return [
         (
@@ -45,16 +46,24 @@
     return lax.dot_general(a, b, (((1,), (1,)), ((), ())), preferred_element_type=F32)
 
 
+def window_rows(halos, unit, block):
+    ends = [0]
+    for halo in halos:
+        ends.append(ends[-1] + (block + 2 * halo) * unit)
+    return ends
+
+
 def pack_kernel(time_devs, halos, masked, *refs):
     count = len(halos)
     len_ref, ins = refs[0], refs[1 : 1 + count]
     outs, turned = refs[1 + count : -count], refs[-count:]
     me = lax.axis_index("tm")
     targets = [me] + [to(me) for _, to, _ in pairing(time_devs)]
+    frames, rows, cols, channels = ins[0].shape
+    unit, block = frames * rows, cols // time_devs
+    ends = window_rows(halos, unit, block)
     for at in range(count):
         ref, stage, halo = ins[at], turned[at], halos[at]
-        frames, rows, cols, _ = ref.shape
-        unit = frames * rows
         if halo:
             edge = jnp.zeros((stage.shape[0], halo * unit, LANES), F32)
             stage[:, 0 : halo * unit, :] = edge
@@ -65,39 +74,37 @@
                 if masked:
                     value = jnp.where(me * frames + frame < len_ref[0], value, 0.0)
                 start = halo * unit + frame * rows + row
-                for at_lane, lane in lanes(value.shape[1]):
+                for at_lane, lane in lanes(channels):
                     stage[at_lane, pl.ds(start, cols, stride=unit), :] = value[:, lane]
-        block = cols // time_devs
-        size = (block + 2 * halo) * unit
+        size = ends[at + 1] - ends[at]
         for step, target in enumerate(targets):
             start = pl.multiple_of(target * (block * unit), unit)
-            for at_lane, lane in lanes(ref.shape[3]):
-                outs[at * time_devs + step][:, lane] = stage[at_lane, pl.ds(start, size), :].astype(BF16)
+            for at_lane, lane in lanes(channels):
+                outs[step][ends[at] : ends[at + 1], lane] = stage[
+                    at_lane, pl.ds(start, size), :
+                ].astype(BF16)
 
 
 def pack(arrays, lengths, halos, masked, time_devs):
     frames, rows, cols, channels = arrays[0].shape
     unit = frames * rows
-    shapes = [
-        jax.ShapeDtypeStruct(((cols // time_devs + 2 * halo) * unit, channels), BF16)
-        for halo in halos
-        for _ in range(time_devs)
-    ]
-    out = pl.pallas_call(
+    size = window_rows(halos, unit, cols // time_devs)[-1]
+    return pl.pallas_call(
         functools.partial(pack_kernel, time_devs, halos, masked),
-        out_shape=shapes,
+        out_shape=[jax.ShapeDtypeStruct((size, channels), BF16)] * time_devs,
         in_specs=[SMEM] + [VMEM] * len(arrays),
-        out_specs=[VMEM] * len(shapes),
+        out_specs=[VMEM] * time_devs,
         scratch_shapes=[
             pltpu.VMEM((channels // LANES, (cols + 2 * halo) * unit, LANES), F32) for halo in halos
         ],
         compiler_params=pltpu.CompilerParams(vmem_limit_bytes=12 << 20),
-        cost_estimate=pl.CostEstimate(flops=6 * 10**9, bytes_accessed=2 << 20, transcendentals=0),
+        cost_estimate=pl.CostEstimate(
+            flops=6 * 10**9, bytes_accessed=2 << 20, transcendentals=0
+        ),
     )(lengths, *arrays)
-    return [out[at * time_devs : (at + 1) * time_devs] for at in range(len(arrays))]
-
-
-def gather_block(dims, wins, halo, stage, dest, col_stride, row_pad):
+
+
+def gather_block(dims, wins, halo, begin, stage, dest, col_stride, row_pad):
     time_devs, row_devs, frame_dev, row_dev, col_dev = dims
     frames = time_devs * frame_dev
     unit = frame_dev * row_dev
@@ -111,7 +118,8 @@
             first = row_at * (col_dev * unit)
             for at_lane, lane in lanes(wins[at].shape[1]):
                 slot = at * dest.shape[0] + at_lane
-                stage[slot, 0 : wins[at].shape[0], :] = wins[at][:, lane].astype(F32)
+                size = stage.shape[1]
+                stage[slot] = wins[at][begin : begin + size, lane].astype(F32)
                 for frame in range(frame_dev):
                     for row in range(row_dev):
                         start = first + frame * row_dev + row
@@ -157,54 +165,35 @@
     return moved, mixed
 
 
-def chunk_copy(source, at, target, sem):
-    return pltpu.make_async_copy(source.at[2 - at], target, sem)
-
-
 def first_kernel(dims, count, *refs):
     wins, weight_ref = refs[:count], refs[count]
-    acc_ref, mid_ref, last_ref, next_ref = refs[count + 1 : count + 5]
-    stage, full, shifts, buffer, sems = refs[count + 5 :]
+    acc_ref, mid_ref = refs[count + 1 : count + 3]
+    stage, full, shifts = refs[count + 3 :]
     time_devs, row_devs, frame_dev, row_dev, col_dev = dims
     frames, rows = time_devs * frame_dev, row_devs * row_dev
-    for a in range(2):
-        chunk_copy(weight_ref, a, buffer.at[a], sems.at[a]).start()
-    chunk_copy(weight_ref, 2, next_ref, sems.at[2]).start()
     full[...] = jnp.zeros_like(full)
     plane, pitch = rows * frames, (rows + 2) * frames
-    gather_block(dims, wins, 2, stage, full, pitch, 1)
-    spread(full, [shifts.at[0], shifts.at[1], last_ref], col_dev + 4, rows, frames)
+    gather_block(dims, wins, 2, 0, stage, full, pitch, 1)
+    spread(full, [shifts.at[0], shifts.at[1], shifts.at[2]], col_dev + 4, rows, frames)
     for w in range(col_dev):
         start = (w + 2) * pitch + frames
         mid_ref[:, w * plane : (w + 1) * plane, :] = full[:, start : start + plane, :]
     acc_ref[...] = jnp.zeros_like(acc_ref)
 
-    @pl.loop(0, 2)
+    @pl.loop(0, 3)
     def _(a):
-        chunk_copy(weight_ref, a, buffer.at[a], sems.at[a]).wait()
-        moved, mixed = taps_of(shifts.at[a], buffer.at[a], col_dev + 2, rows, frames)
+        moved, mixed = taps_of(shifts.at[a], weight_ref.at[2 - a], col_dev + 2, rows, frames)
         acc_ref[...] += dot_last(moved, mixed)
 
-    chunk_copy(weight_ref, 2, next_ref, sems.at[2]).wait()
-
-
-def last_tap_kernel(dims, acc_in, shifts, weights, acc_ref):
+
+def second_kernel(dims, count, cols_all, *refs):
+    wins = refs[:count]
+    acc_ref, mid_ref, weight_ref, out_ref = refs[count : count + 4]
+    stage, late, slopes, full, shifts, grad = refs[count + 4 :]
     time_devs, row_devs, frame_dev, row_dev, col_dev = dims
     frames, rows = time_devs * frame_dev, row_devs * row_dev
-    moved, mixed = taps_of(shifts, weights, col_dev + 2, rows, frames)
-    acc_ref[...] = acc_in[...] + dot_last(moved, mixed)
-
-
-def second_kernel(dims, count, cols_all, *refs):
-    hid = refs[:count]
-    acc_ref, weight_ref, out_ref = refs[count : count + 3]
-    stage, slopes, full, shifts, buffer, sems = refs[count + 3 :]
-    time_devs, row_devs, frame_dev, row_dev, col_dev = dims
-    frames, rows = time_devs * frame_dev, row_devs * row_dev
-    for a in range(3):
-        chunk_copy(weight_ref, a, buffer.at[a], sems.at[a]).start()
     plane, pitch = rows * frames, (rows + 2) * frames
-    gather_block(dims, hid, 1, stage, slopes, plane, 0)
+    gather_block(dims, wins, 1, 0, stage, slopes, plane, 0)
     full[...] = jnp.zeros_like(full)
     first_col = (lax.axis_index("tm") * row_devs + lax.axis_index("rows")) * col_dev - 1
     for w in range(col_dev + 2):
@@ -216,24 +205,19 @@
             value = acc_ref[here, lane] * silu_slope(slopes[at_lane, here, :])
             full[at_lane, start : start + plane, :] = jnp.where(inside, value, 0.0)
     spread(full, [shifts.at[a] for a in range(3)], col_dev + 2, rows, frames)
-    out_ref[...] = jnp.zeros_like(out_ref)
+    grad[...] = jnp.zeros_like(grad)
 
     @pl.loop(0, 3)
     def _(a):
-        chunk_copy(weight_ref, a, buffer.at[a], sems.at[a]).wait()
-        moved, mixed = taps_of(shifts.at[a], buffer.at[a], col_dev, rows, frames)
-        out_ref[...] += dot_last(mixed, moved)
-
-
-def final_kernel(dims, count, *refs):
-    lat = refs[:count]
-    acc_ref, mid_ref, out_ref, stage, slopes, full = refs[count:]
-    time_devs, row_devs, frame_dev, row_dev, col_dev = dims
-    frames, rows = time_devs * frame_dev, row_devs * row_dev
-    plane = rows * frames
-    gather_block(dims, lat, 0, stage, slopes, plane, 0)
-    for at_lane, lane in lanes(acc_ref.shape[0]):
-        full[at_lane] = mid_ref[at_lane] + acc_ref[lane, :].T * silu_slope(slopes[at_lane])
+        moved, mixed = taps_of(shifts.at[a], weight_ref.at[2 - a], col_dev, rows, frames)
+        grad[...] += dot_last(mixed, moved)
+
+    gather_block(dims, wins, 0, stage.shape[1], late, slopes, plane, 0)
+    size = col_dev * plane
+    for at_lane, lane in lanes(grad.shape[0]):
+        full[at_lane, 0:size, :] = mid_ref[at_lane] + grad[lane, :].T * silu_slope(
+            slopes[at_lane, 0:size, :]
+        )
         for frame in range(frames):
             for row in range(rows):
                 out_ref[0, frame, row, :, lane] = full[
@@ -286,55 +270,36 @@
 
     mac = 2 * 9 * channels * channels
     wide, narrow = (col_dev + 2) * plane, col_dev * plane
-    chunk = jax.ShapeDtypeStruct(conv_two.shape[1:], BF16)
     acc_shape = jax.ShapeDtypeStruct((wide, channels), F32)
-    (cot,) = pack([cotangent[0]], lengths, (2,), True, time_devs)
+    cot = pack([cotangent[0]], lengths, (2,), True, time_devs)
     cot = over_rows(over_tm(cot))
-    hid, lat = pack([hidden[0], latents[0]], lengths, (1, 0), False, time_devs)
+    hid = pack([hidden[0], latents[0]], lengths, (1, 0), False, time_devs)
     hid = over_rows(over_tm(hid))
-    lat = over_rows(over_tm(lat))
-    acc, mid, shifted, weights = kernel_call(
+    acc, mid = kernel_call(
         functools.partial(first_kernel, dims, count),
-        [
-            acc_shape,
-            jax.ShapeDtypeStruct((parts, narrow, LANES), F32),
-            jax.ShapeDtypeStruct((2, (col_dev + 4) * pitch, channels), BF16),
-            chunk,
-        ],
-        [VMEM] * count + [HBM],
+        [acc_shape, jax.ShapeDtypeStruct((parts, narrow, LANES), F32)],
+        [VMEM] * (count + 1),
         [
             stage(2),
             part_rows((col_dev + 4) * pitch + frames),
-            pltpu.VMEM((2, 2, (col_dev + 4) * pitch, channels), BF16),
-            pltpu.VMEM((2,) + chunk.shape, BF16),
-            pltpu.SemaphoreType.DMA((3,)),
+            pltpu.VMEM((3, 2, (col_dev + 4) * pitch, channels), BF16),
         ],
-        2 * mac * wide,
+        3 * mac * wide,
     )(*cot, conv_two)
-    acc = kernel_call(
-        functools.partial(last_tap_kernel, dims), acc_shape, [VMEM] * 3, [], mac * wide
-    )(acc, shifted, weights)
-    grad = kernel_call(
+    return kernel_call(
         functools.partial(second_kernel, dims, count, cols),
-        jax.ShapeDtypeStruct((channels, narrow), F32),
-        [VMEM] * (count + 1) + [HBM],
+        jax.ShapeDtypeStruct((1, frames, rows, col_dev, channels), F32),
+        [VMEM] * (count + 3),
         [
             stage(1),
+            stage(0),
             part_rows(wide),
             part_rows((col_dev + 2) * pitch + frames),
             pltpu.VMEM((3, 2, (col_dev + 2) * pitch, channels), BF16),
-            pltpu.VMEM((3,) + chunk.shape, BF16),
-            pltpu.SemaphoreType.DMA((3,)),
+            pltpu.VMEM((channels, narrow), F32),
         ],
         3 * mac * narrow,
-    )(*hid, acc, conv_one)
-    return kernel_call(
-        functools.partial(final_kernel, dims, count),
-        jax.ShapeDtypeStruct((1, frames, rows, col_dev, channels), F32),
-        [VMEM] * (count + 2),
-        [stage(0), part_rows(narrow), part_rows(narrow)],
-        1000000,
-    )(*lat, grad, mid)
+    )(*hid, acc, mid, conv_one)
 
 
 def solution(mesh):

time: 39.4 us -> 34.9 us (0.89)
  starting transfers between devices: 16.4 us -> 14.6 us
  Pallas kernels: 13.1 us -> 11.7 us
  waiting for transfers between devices: 7.94 us -> 6.68 us
    pallas_call x2 -> x0, Pallas kernels: 2.99 us -> none  [the longest x1 1.56 us: on_device(): kernel_call(functools.partial(last_tap_kernel, dims), acc_shape, [VMEM] *...]
    ppermute x9 -> x6, waiting for transfers between devices: 7.91 us -> 6.66 us  [over_tm(): out.append(lax.ppermute(windows[step + 1], 'tm', pairs))]
    ppermute x12 -> x8, starting transfers between devices: 2.18 us -> 1.23 us  [over_rows(): out.append(lax.ppermute(window, 'rows', pairs))]
    ppermute x9 -> x6, starting transfers between devices: 14.3 us -> 13.3 us  [over_tm(): out.append(lax.ppermute(windows[step + 1], 'tm', pairs))]
    pallas_call x1, Pallas kernels: 5.08 us -> 5.96 us  [on_device(): kernel_call(functools.partial(first_kernel, dims, count), [acc_shape, jax...]
    pallas_call x1, Pallas kernels: 4.64 us -> 5.38 us  [on_device(): kernel_call(functools.partial(second_kernel, dims, count, cols), jax.Shap...]
  transfers between devices with their start and end apart: 21 -> 14, of which waited for: 3 -> 3; matrix products, arithmetic and copies ran while one was open for 0% -> 0% of each run, Pallas kernels for 29% -> 18%
where the time goes in v3:
time: 34.9 us; the launch traced here: 34.7 us
  starting transfers between devices  14.6 us (42%)
  Pallas kernels  11.7 us (34%)
  waiting for transfers between devices  6.68 us (19%)
  local copies, waits for them, and re-layouts  0.94 us (3%)
  between operations  0.8 us (2%)
    ppermute x6, starting transfers between devices, over_tm(): out.append(lax.ppermute(windows[step + 1], 'tm', pairs))  13.3 us
    ppermute x6, waiting for transfers between devices, over_tm(): out.append(lax.ppermute(windows[step + 1], 'tm', pairs))  6.66 us
    pallas_call x1, Pallas kernels, on_device(): kernel_call(functools.partial(first_kernel, dims, count), [acc_shape, jax...  5.96 us
    pallas_call x1, Pallas kernels, on_device(): kernel_call(functools.partial(second_kernel, dims, count, cols), jax.Shap...  5.38 us
    ppermute x8, starting transfers between devices, over_rows(): out.append(lax.ppermute(window, 'rows', pairs))  1.23 us
    unnamed x14, local copies, waits for them, and re-layouts  0.94 us
  transfers between devices with their start and end apart: 14, of which 3 were waited for; matrix products, arithmetic and copies ran while one was open for 0% of the time, Pallas kernels for 18%

profile of v3, /device:TPU:0, one launch (start us, length us, event | category | flops | bytes accessed | tf_op | source)
XLA Modules:
  0.0 34.7 jit_solution(2809449983282737319)
XLA Ops:
  0.7 0.0 copy-start
  0.7 0.9 %copy-done = bf16[1,2,4,32,384]{4,3,2,1,0:T(8,128)(2,1)S(1)} copy-done((bf16[1,2,4,32,384]{4,3,2,1,0:T(8,128)(2,1)S(1)}, bf16[1,2,4,32,384]{4,3,2,1,0:T(8,128)(2,1)}, u32[]{:S(2)}) %copy-start) | copy-done | bytes 196632
  1.6 0.0 copy-start.1
  1.6 0.0 copy-start.2
  1.6 0.0 slice-start.2
  1.6 0.1 shard_map.65
  1.7 4.1 %collective-permute-start.8 = (bf16[96,384]{1,0:T(8,128)(2,1)S(1)}, bf16[96,384]{1,0:T(8,128)(2,1)S(1)}, u32[]{:S(2)}, u32[]{:S(2)}) collective-permute-start(bf16[96,384]{1,0:T(8,128)(2,1)S(1)} %get-tuple-element.20), channel_id=1, source_target_pairs={{0,4},{2,6},{4,0},{6,2},{1,5},{3,7},{5,1},{7,3},{8,12},{10,14},{12... | collective-permute-start | bytes 221192 | tf_op jit(solution)/shard_map/ppermute | solution.py:254
  5.9 1.3 %collective-permute-start.10 = (bf16[96,384]{1,0:T(8,128)(2,1)S(1)}, bf16[96,384]{1,0:T(8,128)(2,1)S(1)}, u32[]{:S(2)}, u32[]{:S(2)}) collective-permute-start(bf16[96,384]{1,0:T(8,128)(2,1)S(1)} %get-tuple-element.21), channel_id=1, source_target_pairs={{0,6},{2,4},{4,2},{6,0},{1,7},{3,5},{5,3},{7,1},{8,14},{10,12},{12... | collective-permute-start | bytes 221192 | tf_op jit(solution)/shard_map/ppermute | solution.py:254
  7.2 0.0 slice-start
  7.2 0.0 copy-done.1
  7.2 0.0 copy-done.2
  7.2 0.0 slice-start.3
  7.2 0.0 slice-start.1
  7.2 0.2 shard_map.64
  7.5 1.8 %collective-permute-start.1 = (bf16[144,384]{1,0:T(8,128)(2,1)S(1)}, bf16[144,384]{1,0:T(8,128)(2,1)S(1)}, u32[]{:S(2)}, u32[]{:S(2)}) collective-permute-start(bf16[144,384]{1,0:T(8,128)(2,1)S(1)} %get-tuple-element.16), channel_id=1, source_target_pairs={{0,4},{2,6},{4,0},{6,2},{1,5},{3,7},{5,1},{7,3},{8,12},{10,14},{12... | collective-permute-start | bytes 331784 | tf_op jit(solution)/shard_map/ppermute | solution.py:254
  9.3 1.3 %collective-permute-start.12 = (bf16[96,384]{1,0:T(8,128)(2,1)S(1)}, bf16[96,384]{1,0:T(8,128)(2,1)S(1)}, u32[]{:S(2)}, u32[]{:S(2)}) collective-permute-start(bf16[96,384]{1,0:T(8,128)(2,1)S(1)} %get-tuple-element.22), channel_id=1, source_target_pairs={{0,2},{2,0},{4,6},{6,4},{1,3},{3,1},{5,7},{7,5},{8,10},{10,8},{12,... | collective-permute-start | bytes 221192 | tf_op jit(solution)/shard_map/ppermute | solution.py:254
  10.6 0.0 collective-permute-start.7
  10.6 2.1 %collective-permute-done.8.refs_2_ = bf16[96,384]{1,0:T(8,128)(2,1)S(1)} collective-permute-done((bf16[96,384]{1,0:T(8,128)(2,1)S(1)}, bf16[96,384]{1,0:T(8,128)(2,1)S(1)}, u32[]{:S(2)}, u32[]{:S(2)}) %collective-permute-start.8) | collective-permute-done | bytes 73760 | tf_op jit(solution)/shard_map/ppermute | solution.py:254
  12.8 4.8 %collective-permute-start.3 = (bf16[144,384]{1,0:T(8,128)(2,1)S(1)}, bf16[144,384]{1,0:T(8,128)(2,1)S(1)}, u32[]{:S(2)}, u32[]{:S(2)}) collective-permute-start(bf16[144,384]{1,0:T(8,128)(2,1)S(1)} %get-tuple-element.17), channel_id=1, source_target_pairs={{0,6},{2,4},{4,2},{6,0},{1,7},{3,5},{5,3},{7,1},{8,14},{10,12},{12... | collective-permute-start | bytes 331784 | tf_op jit(solution)/shard_map/ppermute | solution.py:254
  17.5 0.0 collective-permute-done.10.refs_4_
  17.5 0.0 collective-permute-start.5
  17.5 0.0 collective-permute-done.12.refs_6_
  17.5 0.1 collective-permute-start.9
  17.6 0.0 collective-permute-done.7.refs_1_
  17.6 0.5 %collective-permute-start.11 = (bf16[96,384]{1,0:T(8,128)(2,1)S(1)}, bf16[96,384]{1,0:T(8,128)(2,1)S(1)}, u32[]{:S(2)}, u32[]{:S(2)}) collective-permute-start(bf16[96,384]{1,0:T(8,128)(2,1)S(1)} %collective-permute-done.10.refs_4_), channel_id=1, source_target_pairs={{0,1},{1,0},{2,3},{3,2},{4,5},{5,4},{6,7},{7,6},{8,9},{9,8},{10,11... | collective-permute-start | bytes 221192 | tf_op jit(solution)/shard_map/ppermute | solution.py:262
  18.1 0.0 collective-permute-done.1.refs_2_
  18.1 0.1 collective-permute-start.13
  18.2 2.6 %collective-permute-done.3.refs_4_ = bf16[144,384]{1,0:T(8,128)(2,1)S(1)} collective-permute-done((bf16[144,384]{1,0:T(8,128)(2,1)S(1)}, bf16[144,384]{1,0:T(8,128)(2,1)S(1)}, u32[]{:S(2)}, u32[]{:S(2)}) %collective-permute-start.3) | collective-permute-done | bytes 110624 | tf_op jit(solution)/shard_map/ppermute | solution.py:254
  20.8 0.0 collective-permute-start
  20.8 1.9 %collective-permute-done.5.refs_6_ = bf16[144,384]{1,0:T(8,128)(2,1)S(1)} collective-permute-done((bf16[144,384]{1,0:T(8,128)(2,1)S(1)}, bf16[144,384]{1,0:T(8,128)(2,1)S(1)}, u32[]{:S(2)}, u32[]{:S(2)}) %collective-permute-start.5) | collective-permute-done | bytes 110624 | tf_op jit(solution)/shard_map/ppermute | solution.py:254
  22.7 0.0 collective-permute-start.2
  22.7 0.0 collective-permute-done.9.refs_3_
  22.7 0.5 %collective-permute-start.4 = (bf16[144,384]{1,0:T(8,128)(2,1)S(1)}, bf16[144,384]{1,0:T(8,128)(2,1)S(1)}, u32[]{:S(2)}, u32[]{:S(2)}) collective-permute-start(bf16[144,384]{1,0:T(8,128)(2,1)S(1)} %collective-permute-done.3.refs_4_), channel_id=1, source_target_pairs={{0,1},{1,0},{2,3},{3,2},{4,5},{5,4},{6,7},{7,6},{8,9},{9,8},{10,11... | collective-permute-start | bytes 331784 | tf_op jit(solution)/shard_map/ppermute | solution.py:262
  23.2 0.0 collective-permute-done.11.refs_5_
  23.2 0.1 collective-permute-start.6
  23.3 0.0 collective-permute-done.13.refs_7_
  23.3 0.0 slice-done.2
  23.3 0.0 slice-done.3
  23.3 6.0 %shard_map.66 = (f32[384,384]{1,0:T(8,128)S(1)}, f32[3,256,128]{2,1,0:T(8,128)S(1)}) custom-call(bf16[96,384]{1,0:T(8,128)(2,1)S(1)} %get-tuple-element.19.refs_0_, bf16[96,384]{1,0:T(8,128)(2,1)S(1)} %collective-permute-done.7.refs_1_, bf16[96,384]{1,0:T(8,128)(2,1)S(1)} %collective-permute-done.8.refs_2_, ...), custom_call_target="tpu_custom_call" | custom-call | flops 3057647616 | bytes 4194304 | tf_op jit(solution)/shard_map/pallas_call | solution.py:278
  29.3 0.0 collective-permute-done.refs_1_
  29.3 0.0 collective-permute-done.2.refs_3_
  29.3 0.0 collective-permute-done.4.refs_5_
  29.3 0.0 collective-permute-done.6.refs_7_
  29.3 0.0 slice-done
  29.3 0.0 slice-done.1
  29.4 5.4 %shard_map.67 = f32[1,8,8,4,384]{4,3,2,1,0:T(4,128)} custom-call(bf16[144,384]{1,0:T(8,128)(2,1)S(1)} %get-tuple-element.15.refs_0_, bf16[144,384]{1,0:T(8,128)(2,1)S(1)} %collective-permute-done.refs_1_, bf16[144,384]{1,0:T(8,128)(2,1)S(1)} %collective-permute-done.1.refs_2_, bf16[144,384]{1,0:T(8,128)(2,1)S(1)} %collective-permute-done.2.refs_3_, ...), custom_call_target="tpu_custom_call" | custom-call | flops 2038431744 | bytes 4194304 | tf_op jit(solution)/shard_map/pallas_call | solution.py:289
  (2 shorter events, 0.0 us)
Async XLA Ops:
  0.7 0.9 %copy-start = (bf16[1,2,4,32,384]{4,3,2,1,0:T(8,128)(2,1)S(1)}, bf16[1,2,4,32,384]{4,3,2,1,0:T(8,128)(2,1)}, u32[]{:S(2)}) copy-start(bf16[1,2,4,32,384]{4,3,2,1,0:T(8,128)(2,1)} %param.8) | copy-start | bytes 589828
  1.6 5.6 %copy-start.1 = (bf16[1,2,4,32,384]{4,3,2,1,0:T(8,128)(2,1)S(1)}, bf16[1,2,4,32,384]{4,3,2,1,0:T(8,128)(2,1)}, u32[]{:S(2)}) copy-start(bf16[1,2,4,32,384]{4,3,2,1,0:T(8,128)(2,1)} %param.7) | copy-start | bytes 589828
  1.6 5.6 %copy-start.2 = (bf16[1,2,4,32,384]{4,3,2,1,0:T(8,128)(2,1)S(1)}, bf16[1,2,4,32,384]{4,3,2,1,0:T(8,128)(2,1)}, u32[]{:S(2)}) copy-start(bf16[1,2,4,32,384]{4,3,2,1,0:T(8,128)(2,1)} %param.6) | copy-start | bytes 589828
  1.6 21.7 %slice-start.2 = ((s8[7962624]{0:T(1024)(128)(4,1)}), s8[4194304]{0:T(1024)(128)(4,1)S(1)}, s32[]{:S(2)}) async-start(s8[7962624]{0:T(1024)(128)(4,1)} %bitcast.5), calls=%async_computation.2 | async-start | bytes 8388608
  1.7 11.0 %collective-permute-start.8 = (bf16[96,384]{1,0:T(8,128)(2,1)S(1)}, bf16[96,384]{1,0:T(8,128)(2,1)S(1)}, u32[]{:S(2)}, u32[]{:S(2)}) collective-permute-start(bf16[96,384]{1,0:T(8,128)(2,1)S(1)} %get-tuple-element.20), channel_id=1, source_target_pairs={{0,4},{2,6},{4,0},{6,2},{1,5},{3,7},{5,1},{7,3},{8,12},{10,14},{12... | collective-permute-start | bytes 221192 | tf_op jit(solution)/shard_map/ppermute | solution.py:254
  5.9 11.6 %collective-permute-start.10 = (bf16[96,384]{1,0:T(8,128)(2,1)S(1)}, bf16[96,384]{1,0:T(8,128)(2,1)S(1)}, u32[]{:S(2)}, u32[]{:S(2)}) collective-permute-start(bf16[96,384]{1,0:T(8,128)(2,1)S(1)} %get-tuple-element.21), channel_id=1, source_target_pairs={{0,6},{2,4},{4,2},{6,0},{1,7},{3,5},{5,3},{7,1},{8,14},{10,12},{12... | collective-permute-start | bytes 221192 | tf_op jit(solution)/shard_map/ppermute | solution.py:254
  7.2 22.1 %slice-start = ((s8[7962624]{0:T(1024)(128)(4,1)}), s8[4194304]{0:T(1024)(128)(4,1)S(1)}, s32[]{:S(2)}) async-start(s8[7962624]{0:T(1024)(128)(4,1)} %bitcast.3), calls=%async_computation | async-start | bytes 8388608
  7.2 16.1 %slice-start.3 = ((s8[7962624]{0:T(1024)(128)(4,1)}), s8[3768320]{0:T(1024)(128)(4,1)S(1)}, s32[]{:S(2)}) async-start(s8[7962624]{0:T(1024)(128)(4,1)} %bitcast.5), calls=%async_computation.3 | async-start | bytes 7536640
  7.2 22.1 %slice-start.1 = ((s8[7962624]{0:T(1024)(128)(4,1)}), s8[3768320]{0:T(1024)(128)(4,1)S(1)}, s32[]{:S(2)}) async-start(s8[7962624]{0:T(1024)(128)(4,1)} %bitcast.3), calls=%async_computation.1 | async-start | bytes 7536640
  7.5 10.6 %collective-permute-start.1 = (bf16[144,384]{1,0:T(8,128)(2,1)S(1)}, bf16[144,384]{1,0:T(8,128)(2,1)S(1)}, u32[]{:S(2)}, u32[]{:S(2)}) collective-permute-start(bf16[144,384]{1,0:T(8,128)(2,1)S(1)} %get-tuple-element.16), channel_id=1, source_target_pairs={{0,4},{2,6},{4,0},{6,2},{1,5},{3,7},{5,1},{7,3},{8,12},{10,14},{12... | collective-permute-start | bytes 331784 | tf_op jit(solution)/shard_map/ppermute | solution.py:254
  9.3 8.3 %collective-permute-start.12 = (bf16[96,384]{1,0:T(8,128)(2,1)S(1)}, bf16[96,384]{1,0:T(8,128)(2,1)S(1)}, u32[]{:S(2)}, u32[]{:S(2)}) collective-permute-start(bf16[96,384]{1,0:T(8,128)(2,1)S(1)} %get-tuple-element.22), channel_id=1, source_target_pairs={{0,2},{2,0},{4,6},{6,4},{1,3},{3,1},{5,7},{7,5},{8,10},{10,8},{12,... | collective-permute-start | bytes 221192 | tf_op jit(solution)/shard_map/ppermute | solution.py:254
  10.6 7.0 %collective-permute-start.7 = (bf16[96,384]{1,0:T(8,128)(2,1)S(1)}, bf16[96,384]{1,0:T(8,128)(2,1)S(1)}, u32[]{:S(2)}, u32[]{:S(2)}) collective-permute-start(bf16[96,384]{1,0:T(8,128)(2,1)S(1)} %get-tuple-element.19.refs_0_), channel_id=1, source_target_pairs={{0,1},{1,0},{2,3},{3,2},{4,5},{5,4},{6,7},{7,6},{8,9},{9,8},{10,11... | collective-permute-start | bytes 221192 | tf_op jit(solution)/shard_map/ppermute | solution.py:262
  12.8 8.1 %collective-permute-start.3 = (bf16[144,384]{1,0:T(8,128)(2,1)S(1)}, bf16[144,384]{1,0:T(8,128)(2,1)S(1)}, u32[]{:S(2)}, u32[]{:S(2)}) collective-permute-start(bf16[144,384]{1,0:T(8,128)(2,1)S(1)} %get-tuple-element.17), channel_id=1, source_target_pairs={{0,6},{2,4},{4,2},{6,0},{1,7},{3,5},{5,3},{7,1},{8,14},{10,12},{12... | collective-permute-start | bytes 331784 | tf_op jit(solution)/shard_map/ppermute | solution.py:254
  17.5 5.2 %collective-permute-start.5 = (bf16[144,384]{1,0:T(8,128)(2,1)S(1)}, bf16[144,384]{1,0:T(8,128)(2,1)S(1)}, u32[]{:S(2)}, u32[]{:S(2)}) collective-permute-start(bf16[144,384]{1,0:T(8,128)(2,1)S(1)} %get-tuple-element.18), channel_id=1, source_target_pairs={{0,2},{2,0},{4,6},{6,4},{1,3},{3,1},{5,7},{7,5},{8,10},{10,8},{12,... | collective-permute-start | bytes 331784 | tf_op jit(solution)/shard_map/ppermute | solution.py:254
  17.5 5.2 %collective-permute-start.9 = (bf16[96,384]{1,0:T(8,128)(2,1)S(1)}, bf16[96,384]{1,0:T(8,128)(2,1)S(1)}, u32[]{:S(2)}, u32[]{:S(2)}) collective-permute-start(bf16[96,384]{1,0:T(8,128)(2,1)S(1)} %collective-permute-done.8.refs_2_), channel_id=1, source_target_pairs={{0,1},{1,0},{2,3},{3,2},{4,5},{5,4},{6,7},{7,6},{8,9},{9,8},{10,11... | collective-permute-start | bytes 221192 | tf_op jit(solution)/shard_map/ppermute | solution.py:262
  17.6 5.6 %collective-permute-start.11 = (bf16[96,384]{1,0:T(8,128)(2,1)S(1)}, bf16[96,384]{1,0:T(8,128)(2,1)S(1)}, u32[]{:S(2)}, u32[]{:S(2)}) collective-permute-start(bf16[96,384]{1,0:T(8,128)(2,1)S(1)} %collective-permute-done.10.refs_4_), channel_id=1, source_target_pairs={{0,1},{1,0},{2,3},{3,2},{4,5},{5,4},{6,7},{7,6},{8,9},{9,8},{10,11... | collective-permute-start | bytes 221192 | tf_op jit(solution)/shard_map/ppermute | solution.py:262
  18.1 5.2 %collective-permute-start.13 = (bf16[96,384]{1,0:T(8,128)(2,1)S(1)}, bf16[96,384]{1,0:T(8,128)(2,1)S(1)}, u32[]{:S(2)}, u32[]{:S(2)}) collective-permute-start(bf16[96,384]{1,0:T(8,128)(2,1)S(1)} %collective-permute-done.12.refs_6_), channel_id=1, source_target_pairs={{0,1},{1,0},{2,3},{3,2},{4,5},{5,4},{6,7},{7,6},{8,9},{9,8},{10,11... | collective-permute-start | bytes 221192 | tf_op jit(solution)/shard_map/ppermute | solution.py:262
  20.8 8.5 %collective-permute-start = (bf16[144,384]{1,0:T(8,128)(2,1)S(1)}, bf16[144,384]{1,0:T(8,128)(2,1)S(1)}, u32[]{:S(2)}, u32[]{:S(2)}) collective-permute-start(bf16[144,384]{1,0:T(8,128)(2,1)S(1)} %get-tuple-element.15.refs_0_), channel_id=1, source_target_pairs={{0,1},{1,0},{2,3},{3,2},{4,5},{5,4},{6,7},{7,6},{8,9},{9,8},{10,11... | collective-permute-start | bytes 331784 | tf_op jit(solution)/shard_map/ppermute | solution.py:262
  22.7 6.6 %collective-permute-start.2 = (bf16[144,384]{1,0:T(8,128)(2,1)S(1)}, bf16[144,384]{1,0:T(8,128)(2,1)S(1)}, u32[]{:S(2)}, u32[]{:S(2)}) collective-permute-start(bf16[144,384]{1,0:T(8,128)(2,1)S(1)} %collective-permute-done.1.refs_2_), channel_id=1, source_target_pairs={{0,1},{1,0},{2,3},{3,2},{4,5},{5,4},{6,7},{7,6},{8,9},{9,8},{10,11... | collective-permute-start | bytes 331784 | tf_op jit(solution)/shard_map/ppermute | solution.py:262
  22.7 6.6 %collective-permute-start.4 = (bf16[144,384]{1,0:T(8,128)(2,1)S(1)}, bf16[144,384]{1,0:T(8,128)(2,1)S(1)}, u32[]{:S(2)}, u32[]{:S(2)}) collective-permute-start(bf16[144,384]{1,0:T(8,128)(2,1)S(1)} %collective-permute-done.3.refs_4_), channel_id=1, source_target_pairs={{0,1},{1,0},{2,3},{3,2},{4,5},{5,4},{6,7},{7,6},{8,9},{9,8},{10,11... | collective-permute-start | bytes 331784 | tf_op jit(solution)/shard_map/ppermute | solution.py:262
  23.2 6.1 %collective-permute-start.6 = (bf16[144,384]{1,0:T(8,128)(2,1)S(1)}, bf16[144,384]{1,0:T(8,128)(2,1)S(1)}, u32[]{:S(2)}, u32[]{:S(2)}) collective-permute-start(bf16[144,384]{1,0:T(8,128)(2,1)S(1)} %collective-permute-done.5.refs_6_), channel_id=1, source_target_pairs={{0,1},{1,0},{2,3},{3,2},{4,5},{5,4},{6,7},{7,6},{8,9},{9,8},{10,11... | collective-permute-start | bytes 331784 | tf_op jit(solution)/shard_map/ppermute | solution.py:262

commit v4 on v3

--- a/solution.py
+++ b/solution.py
@@ -12,9 +12,8 @@
 BF16 = jnp.bfloat16
 VMEM = pl.BlockSpec(memory_space=pltpu.VMEM)
 SMEM = pl.BlockSpec(memory_space=pltpu.SMEM)
-HBM = pl.BlockSpec(memory_space=pltpu.HBM)
 LANES = 128
-STEPS = {4: (2, 3, 1)}
+STEPS = {4: (3, 2, 1)}
 
 
 def lanes(channels):
@@ -104,33 +103,71 @@
     )(lengths, *arrays)
 
 
-def gather_block(dims, wins, halo, begin, stage, dest, col_stride, row_pad):
+def laid_out(dims, wins, halo, begin, target, stage, dest):
+    time_devs, _, frame_dev, row_dev, col_dev = dims
+    frames, unit = time_devs * frame_dev, frame_dev * row_dev
+    tm = lax.axis_index("tm")
+    from_tm = [tm] + [source(tm) for _, _, source in pairing(time_devs)]
+    cols = col_dev + 2 * halo
+    first = pl.multiple_of(target * (col_dev * unit), unit)
+    for s in range(time_devs):
+        for at_lane, lane in lanes(wins[s].shape[1]):
+            slot = s * stage.shape[0] // time_devs + at_lane
+            stage[slot] = wins[s][begin : begin + stage.shape[1], lane].astype(F32)
+            for frame in range(frame_dev):
+                for row in range(row_dev):
+                    start = first + frame * row_dev + row
+                    place = row * frames + from_tm[s] * frame_dev + frame
+                    dest[at_lane, pl.ds(place, cols, stride=row_dev * frames), :] = stage[
+                        slot, pl.ds(start, cols, stride=unit), :
+                    ]
+
+
+def share_kernel(dims, halos, own, *refs):
     time_devs, row_devs, frame_dev, row_dev, col_dev = dims
-    frames = time_devs * frame_dev
+    wins = refs[:time_devs]
+    me = lax.axis_index("rows")
+    targets = [me] if own else [to(me) for _, to, _ in pairing(row_devs)]
+    outs = refs[time_devs : time_devs + len(targets)]
+    scratch = refs[time_devs + len(targets) :]
     unit = frame_dev * row_dev
-    tm, row_at = lax.axis_index("tm"), lax.axis_index("rows")
-    from_tm = [tm] + [source(tm) for _, _, source in pairing(time_devs)]
-    from_row = [row_at] + [source(row_at) for _, _, source in pairing(row_devs)]
-    cols = col_dev + 2 * halo
-    for s in range(time_devs):
-        for q in range(row_devs):
-            at = s * row_devs + q
-            first = row_at * (col_dev * unit)
-            for at_lane, lane in lanes(wins[at].shape[1]):
-                slot = at * dest.shape[0] + at_lane
-                size = stage.shape[1]
-                stage[slot] = wins[at][begin : begin + size, lane].astype(F32)
-                for frame in range(frame_dev):
-                    for row in range(row_dev):
-                        start = first + frame * row_dev + row
-                        target = (
-                            (from_row[q] * row_dev + row + row_pad) * frames
-                            + from_tm[s] * frame_dev
-                            + frame
-                        )
-                        dest[at_lane, pl.ds(target, cols, stride=col_stride), :] = stage[
-                            slot, pl.ds(start, cols, stride=unit), :
-                        ]
+    ends = window_rows(halos, unit, row_devs * col_dev)
+    sizes = window_rows(halos, row_dev * time_devs * frame_dev, col_dev)
+    for at, target in enumerate(targets):
+        for k, halo in enumerate(halos):
+            stage, dest = scratch[2 * k], scratch[2 * k + 1]
+            laid_out(dims, wins, halo, ends[k], target, stage, dest)
+            for at_lane, lane in lanes(outs[at].shape[1]):
+                value = dest[at_lane]
+                if outs[at].dtype == F32:
+                    value = silu_slope(value)
+                outs[at][sizes[k] : sizes[k + 1], lane] = value.astype(outs[at].dtype)
+
+
+def share(dims, halos, own, slopes, windows):
+    time_devs, row_devs, frame_dev, row_dev, col_dev = dims
+    channels = windows[0].shape[1]
+    parts, unit, tall = channels // LANES, frame_dev * row_dev, row_dev * time_devs * frame_dev
+    size = window_rows(halos, tall, col_dev)[-1]
+    count = 1 if own else row_devs - 1
+    scratch = []
+    for halo in halos:
+        rows = (row_devs * col_dev + 2 * halo) * unit
+        scratch.append(pltpu.VMEM((time_devs * parts, rows, LANES), F32))
+        scratch.append(pltpu.VMEM((parts, (col_dev + 2 * halo) * tall, LANES), F32))
+    shape = jax.ShapeDtypeStruct((size, channels), F32 if slopes else BF16)
+    return kernel_call(
+        functools.partial(share_kernel, dims, halos, own),
+        [shape] * count,
+        [VMEM] * time_devs,
+        scratch,
+        10**8,
+    )(*windows)
+
+
+def row_sources(row_devs):
+    me = lax.axis_index("rows")
+    return [me] + [source(me) for _, _, source in pairing(row_devs)]
 
 
 def spread(full, targets, cols, rows, frames):
@@ -165,16 +202,24 @@
     return moved, mixed
 
 
-def first_kernel(dims, count, *refs):
-    wins, weight_ref = refs[:count], refs[count]
-    acc_ref, mid_ref = refs[count + 1 : count + 3]
-    stage, full, shifts = refs[count + 3 :]
+def first_kernel(dims, *refs):
     time_devs, row_devs, frame_dev, row_dev, col_dev = dims
+    pieces, weight_ref = refs[:row_devs], refs[row_devs]
+    acc_ref, mid_ref, full, shifts = refs[row_devs + 1 :]
     frames, rows = time_devs * frame_dev, row_devs * row_dev
-    full[...] = jnp.zeros_like(full)
-    plane, pitch = rows * frames, (rows + 2) * frames
-    gather_block(dims, wins, 2, 0, stage, full, pitch, 1)
-    spread(full, [shifts.at[0], shifts.at[1], shifts.at[2]], col_dev + 4, rows, frames)
+    plane, pitch, tall = rows * frames, (rows + 2) * frames, row_dev * frames
+    for w in range(col_dev + 4):
+        edge = jnp.zeros((full.shape[0], frames, LANES), F32)
+        full[:, w * pitch : w * pitch + frames, :] = edge
+        full[:, (w + 1) * pitch - frames : (w + 1) * pitch, :] = edge
+        for at, source in enumerate(row_sources(row_devs)):
+            start = pl.multiple_of(w * pitch + frames + source * tall, frames)
+            for at_lane, lane in lanes(acc_ref.shape[1]):
+                full[at_lane, pl.ds(start, tall), :] = pieces[at][
+                    w * tall : (w + 1) * tall, lane
+                ].astype(F32)
+    full[:, (col_dev + 4) * pitch :, :] = jnp.zeros((full.shape[0], frames, LANES), F32)
+    spread(full, [shifts.at[a] for a in range(3)], col_dev + 4, rows, frames)
     for w in range(col_dev):
         start = (w + 2) * pitch + frames
         mid_ref[:, w * plane : (w + 1) * plane, :] = full[:, start : start + plane, :]
@@ -186,24 +231,33 @@
         acc_ref[...] += dot_last(moved, mixed)
 
 
-def second_kernel(dims, count, cols_all, *refs):
-    wins = refs[:count]
-    acc_ref, mid_ref, weight_ref, out_ref = refs[count : count + 4]
-    stage, late, slopes, full, shifts, grad = refs[count + 4 :]
+def second_kernel(dims, cols_all, *refs):
     time_devs, row_devs, frame_dev, row_dev, col_dev = dims
+    pieces, acc_ref, mid_ref, weight_ref, out_ref = refs[:row_devs], *refs[row_devs : row_devs + 4]
+    slopes, full, shifts, grad = refs[row_devs + 4 :]
     frames, rows = time_devs * frame_dev, row_devs * row_dev
-    plane, pitch = rows * frames, (rows + 2) * frames
-    gather_block(dims, wins, 1, 0, stage, slopes, plane, 0)
-    full[...] = jnp.zeros_like(full)
+    plane, pitch, tall = rows * frames, (rows + 2) * frames, row_dev * frames
+    sizes = window_rows((1, 0), tall, col_dev)
+    sources = row_sources(row_devs)
     first_col = (lax.axis_index("tm") * row_devs + lax.axis_index("rows")) * col_dev - 1
+
+    def slope(at, begin, lane):
+        value = pieces[at][begin : begin + tall, lane]
+        return value if at == 0 else silu_slope(value.astype(F32))
+
     for w in range(col_dev + 2):
         col = first_col + w
         inside = jnp.logical_and(col >= 0, col < cols_all)
-        here = slice(w * plane, (w + 1) * plane)
-        start = w * pitch + frames
-        for at_lane, lane in lanes(acc_ref.shape[1]):
-            value = acc_ref[here, lane] * silu_slope(slopes[at_lane, here, :])
-            full[at_lane, start : start + plane, :] = jnp.where(inside, value, 0.0)
+        edge = jnp.zeros((full.shape[0], frames, LANES), F32)
+        full[:, w * pitch : w * pitch + frames, :] = edge
+        full[:, (w + 1) * pitch - frames : (w + 1) * pitch, :] = edge
+        for at, source in enumerate(sources):
+            here = pl.multiple_of(w * plane + source * tall, frames)
+            start = pl.multiple_of(w * pitch + frames + source * tall, frames)
+            for at_lane, lane in lanes(acc_ref.shape[1]):
+                value = acc_ref[pl.ds(here, tall), lane] * slope(at, w * tall, lane)
+                full[at_lane, pl.ds(start, tall), :] = jnp.where(inside, value, 0.0)
+    full[:, (col_dev + 2) * pitch :, :] = jnp.zeros((full.shape[0], frames, LANES), F32)
     spread(full, [shifts.at[a] for a in range(3)], col_dev + 2, rows, frames)
     grad[...] = jnp.zeros_like(grad)
 
@@ -212,12 +266,14 @@
         moved, mixed = taps_of(shifts.at[a], weight_ref.at[2 - a], col_dev, rows, frames)
         grad[...] += dot_last(mixed, moved)
 
-    gather_block(dims, wins, 0, stage.shape[1], late, slopes, plane, 0)
+    for w in range(col_dev):
+        for at, source in enumerate(sources):
+            here = pl.multiple_of(w * plane + source * tall, frames)
+            for at_lane, lane in lanes(acc_ref.shape[1]):
+                slopes[at_lane, pl.ds(here, tall), :] = slope(at, sizes[1] + w * tall, lane)
     size = col_dev * plane
     for at_lane, lane in lanes(grad.shape[0]):
-        full[at_lane, 0:size, :] = mid_ref[at_lane] + grad[lane, :].T * silu_slope(
-            slopes[at_lane, 0:size, :]
-        )
+        full[at_lane, 0:size, :] = mid_ref[at_lane] + grad[lane, :].T * slopes[at_lane]
         for frame in range(frames):
             for row in range(rows):
                 out_ref[0, frame, row, :, lane] = full[
@@ -242,11 +298,9 @@
     time_devs, row_devs = lax.axis_size("tm"), lax.axis_size("rows")
     col_dev = cols // (time_devs * row_devs)
     frames, rows = time_devs * frame_dev, row_devs * row_dev
-    unit = frame_dev * row_dev
     dims = (time_devs, row_devs, frame_dev, row_dev, col_dev)
-    count = time_devs * row_devs
     plane, pitch = rows * frames, (rows + 2) * frames
-    chip, parts = cols // time_devs, channels // LANES
+    parts = channels // LANES
 
     def over_tm(windows):
         out = [windows[0]]
@@ -254,46 +308,47 @@
             out.append(lax.ppermute(windows[step + 1], "tm", pairs))
         return out
 
-    def over_rows(windows):
+    def over_rows(pieces):
         out = []
-        for window in windows:
-            out.append(window)
-            for pairs, _, _ in pairing(row_devs):
-                out.append(lax.ppermute(window, "rows", pairs))
+        for at, (pairs, _, _) in enumerate(pairing(row_devs)):
+            out.append(lax.ppermute(pieces[at], "rows", pairs))
         return out
 
-    def stage(halo):
-        return pltpu.VMEM((count * parts, (chip + 2 * halo) * unit, LANES), F32)
+    def for_rows(windows, halos, slopes):
+        sent = []
+        if row_devs > 1:
+            sent = share(dims, halos, False, False, windows)
+        own = share(dims, halos, True, slopes, windows)
+        return [*own, *over_rows(sent)]
 
     def part_rows(size):
         return pltpu.VMEM((parts, size, LANES), F32)
 
     mac = 2 * 9 * channels * channels
     wide, narrow = (col_dev + 2) * plane, col_dev * plane
-    acc_shape = jax.ShapeDtypeStruct((wide, channels), F32)
     cot = pack([cotangent[0]], lengths, (2,), True, time_devs)
-    cot = over_rows(over_tm(cot))
+    cot = for_rows(over_tm(cot), (2,), False)
     hid = pack([hidden[0], latents[0]], lengths, (1, 0), False, time_devs)
-    hid = over_rows(over_tm(hid))
+    hid = for_rows(over_tm(hid), (1, 0), True)
     acc, mid = kernel_call(
-        functools.partial(first_kernel, dims, count),
-        [acc_shape, jax.ShapeDtypeStruct((parts, narrow, LANES), F32)],
-        [VMEM] * (count + 1),
+        functools.partial(first_kernel, dims),
         [
-            stage(2),
+            jax.ShapeDtypeStruct((wide, channels), F32),
+            jax.ShapeDtypeStruct((parts, narrow, LANES), F32),
+        ],
+        [VMEM] * (row_devs + 1),
+        [
             part_rows((col_dev + 4) * pitch + frames),
             pltpu.VMEM((3, 2, (col_dev + 4) * pitch, channels), BF16),
         ],
         3 * mac * wide,
     )(*cot, conv_two)
     return kernel_call(
-        functools.partial(second_kernel, dims, count, cols),
+        functools.partial(second_kernel, dims, cols),
         jax.ShapeDtypeStruct((1, frames, rows, col_dev, channels), F32),
-        [VMEM] * (count + 3),
+        [VMEM] * (row_devs + 3),
         [
-            stage(1),
-            stage(0),
-            part_rows(wide),
+            part_rows(narrow),
             part_rows((col_dev + 2) * pitch + frames),
             pltpu.VMEM((3, 2, (col_dev + 2) * pitch, channels), BF16),
             pltpu.VMEM((channels, narrow), F32),

time: 34.9 us -> 38.2 us (1.095)
  waiting for transfers between devices: 6.68 us -> 13.8 us
  starting transfers between devices: 14.6 us -> 10.4 us
  Pallas kernels: 11.7 us -> 12.1 us
    ppermute x6, waiting for transfers between devices: 6.66 us -> 13.8 us  [over_tm(): out.append(lax.ppermute(windows[step + 1], 'tm', pairs))]
    ppermute x6, starting transfers between devices: 13.3 us -> 10.2 us  [over_tm(): out.append(lax.ppermute(windows[step + 1], 'tm', pairs))]
    ppermute x8 -> x2, starting transfers between devices: 1.23 us -> 0.14 us  [over_rows(): out.append(lax.ppermute(pieces[at], 'rows', pairs))]
    pallas_call x2 -> x6, Pallas kernels: 11.3 us -> 11.7 us  [the longest x1 5.55 us: on_device(): kernel_call(functools.partial(first_kernel, dims), [jax.ShapeDtypeStruct(...]
  transfers between devices with their start and end apart: 14 -> 8, of which waited for: 3 -> 4; matrix products, arithmetic and copies ran while one was open for 0% -> 0% of each run, Pallas kernels for 18% -> 19%
where the time goes in v4:
time: 38.2 us; the launch traced here: 38.1 us
  waiting for transfers between devices  13.8 us (36%)
  Pallas kernels  12.1 us (32%)
  starting transfers between devices  10.4 us (27%)
  local copies, waits for them, and re-layouts  0.95 us (2%)
  between operations  0.84 us (2%)
    ppermute x6, waiting for transfers between devices, over_tm(): out.append(lax.ppermute(windows[step + 1], 'tm', pairs))  13.8 us
    ppermute x6, starting transfers between devices, over_tm(): out.append(lax.ppermute(windows[step + 1], 'tm', pairs))  10.2 us
    pallas_call x1, Pallas kernels, on_device(): kernel_call(functools.partial(first_kernel, dims), [jax.ShapeDtypeStruct(...  5.55 us
    pallas_call x1, Pallas kernels, on_device(): kernel_call(functools.partial(second_kernel, dims, cols), jax.ShapeDtypeS...  4.5 us
    pallas_call x4, Pallas kernels, share(): kernel_call(functools.partial(share_kernel, dims, halos, own), [shape] *...  1.63 us
    unnamed x14, local copies, waits for them, and re-layouts  0.95 us
  transfers between devices with their start and end apart: 8, of which 4 were waited for; matrix products, arithmetic and copies ran while one was open for 0% of the time, Pallas kernels for 19%

profile of v4, /device:TPU:0, one launch (start us, length us, event | category | flops | bytes accessed | tf_op | source)
XLA Modules:
  0.0 38.1 jit_solution(12877065502130363938)
XLA Ops:
  0.7 0.0 copy-start
  0.7 0.9 %copy-done = bf16[1,2,4,32,384]{4,3,2,1,0:T(8,128)(2,1)S(1)} copy-done((bf16[1,2,4,32,384]{4,3,2,1,0:T(8,128)(2,1)S(1)}, bf16[1,2,4,32,384]{4,3,2,1,0:T(8,128)(2,1)}, u32[]{:S(2)}) %copy-start) | copy-done | bytes 196632
  1.6 0.0 copy-start.1
  1.6 0.0 copy-start.2
  1.6 0.1 shard_map.67
  1.7 5.1 %collective-permute-start.4 = (bf16[96,384]{1,0:T(8,128)(2,1)S(1)}, bf16[96,384]{1,0:T(8,128)(2,1)S(1)}, u32[]{:S(2)}, u32[]{:S(2)}) collective-permute-start(bf16[96,384]{1,0:T(8,128)(2,1)S(1)} %get-tuple-element.20), channel_id=1, source_target_pairs={{0,6},{2,4},{4,2},{6,0},{1,7},{3,5},{5,3},{7,1},{8,14},{10,12},{12... | collective-permute-start | bytes 221192 | tf_op jit(solution)/shard_map/ppermute | solution.py:308
  6.9 0.0 collective-permute-start.5
  6.9 0.6 %collective-permute-start.6 = (bf16[96,384]{1,0:T(8,128)(2,1)S(1)}, bf16[96,384]{1,0:T(8,128)(2,1)S(1)}, u32[]{:S(2)}, u32[]{:S(2)}) collective-permute-start(bf16[96,384]{1,0:T(8,128)(2,1)S(1)} %get-tuple-element.22), channel_id=1, source_target_pairs={{0,2},{2,0},{4,6},{6,4},{1,3},{3,1},{5,7},{7,5},{8,10},{10,8},{12,... | collective-permute-start | bytes 221192 | tf_op jit(solution)/shard_map/ppermute | solution.py:308
  7.5 2.0 %collective-permute-done.4.refs_1_ = bf16[96,384]{1,0:T(8,128)(2,1)S(1)} collective-permute-done((bf16[96,384]{1,0:T(8,128)(2,1)S(1)}, bf16[96,384]{1,0:T(8,128)(2,1)S(1)}, u32[]{:S(2)}, u32[]{:S(2)}) %collective-permute-start.4) | collective-permute-done | bytes 73760 | tf_op jit(solution)/shard_map/ppermute | solution.py:308
  9.5 3.5 %collective-permute-done.5.refs_2_ = bf16[96,384]{1,0:T(8,128)(2,1)S(1)} collective-permute-done((bf16[96,384]{1,0:T(8,128)(2,1)S(1)}, bf16[96,384]{1,0:T(8,128)(2,1)S(1)}, u32[]{:S(2)}, u32[]{:S(2)}) %collective-permute-start.5) | collective-permute-done | bytes 73760 | tf_op jit(solution)/shard_map/ppermute | solution.py:308
  13.1 0.0 collective-permute-done.6.refs_3_
  13.1 0.0 slice-start.2
  13.1 0.4 shard_map.69
  13.5 0.1 collective-permute-start.7
  13.6 0.0 slice-start
  13.6 0.0 copy-done.1
  13.6 0.0 copy-done.2
  13.6 0.0 slice-start.3
  13.6 0.0 slice-start.1
  13.6 0.2 shard_map.64
  13.9 2.8 %collective-permute-start = (bf16[144,384]{1,0:T(8,128)(2,1)S(1)}, bf16[144,384]{1,0:T(8,128)(2,1)S(1)}, u32[]{:S(2)}, u32[]{:S(2)}) collective-permute-start(bf16[144,384]{1,0:T(8,128)(2,1)S(1)} %get-tuple-element.16), channel_id=1, source_target_pairs={{0,6},{2,4},{4,2},{6,0},{1,7},{3,5},{5,3},{7,1},{8,14},{10,12},{12... | collective-permute-start | bytes 331784 | tf_op jit(solution)/shard_map/ppermute | solution.py:308
  16.7 0.0 collective-permute-start.1
  16.7 1.7 %collective-permute-start.2 = (bf16[144,384]{1,0:T(8,128)(2,1)S(1)}, bf16[144,384]{1,0:T(8,128)(2,1)S(1)}, u32[]{:S(2)}, u32[]{:S(2)}) collective-permute-start(bf16[144,384]{1,0:T(8,128)(2,1)S(1)} %get-tuple-element.18), channel_id=1, source_target_pairs={{0,2},{2,0},{4,6},{6,4},{1,3},{3,1},{5,7},{7,5},{8,10},{10,8},{12,... | collective-permute-start | bytes 331784 | tf_op jit(solution)/shard_map/ppermute | solution.py:308
  18.3 0.3 shard_map.68.refs_0_
  18.7 3.1 %collective-permute-done.refs_1_ = bf16[144,384]{1,0:T(8,128)(2,1)S(1)} collective-permute-done((bf16[144,384]{1,0:T(8,128)(2,1)S(1)}, bf16[144,384]{1,0:T(8,128)(2,1)S(1)}, u32[]{:S(2)}, u32[]{:S(2)}) %collective-permute-start) | collective-permute-done | bytes 110624 | tf_op jit(solution)/shard_map/ppermute | solution.py:308
  21.8 5.1 %collective-permute-done.1.refs_2_ = bf16[144,384]{1,0:T(8,128)(2,1)S(1)} collective-permute-done((bf16[144,384]{1,0:T(8,128)(2,1)S(1)}, bf16[144,384]{1,0:T(8,128)(2,1)S(1)}, u32[]{:S(2)}, u32[]{:S(2)}) %collective-permute-start.1) | collective-permute-done | bytes 110624 | tf_op jit(solution)/shard_map/ppermute | solution.py:308
  26.9 0.0 collective-permute-done.2.refs_3_
  26.9 0.4 %shard_map.66 = bf16[320,384]{1,0:T(8,128)(2,1)S(1)} custom-call(bf16[144,384]{1,0:T(8,128)(2,1)S(1)} %get-tuple-element.15.refs_0_, bf16[144,384]{1,0:T(8,128)(2,1)S(1)} %collective-permute-done.refs_1_, bf16[144,384]{1,0:T(8,128)(2,1)S(1)} %collective-permute-done.1.refs_2_, bf16[144,384]{1,0:T(8,128)(2,1)S(1)} %collective-permute-done.2.refs_3_), custom_call_target="tpu_custom_call" | custom-call | flops 100000000 | bytes 4194304 | tf_op jit(solution)/shard_map/pallas_call | solution.py:159
  27.3 0.1 collective-permute-start.3
  27.4 0.5 %shard_map.65.refs_0_ = f32[320,384]{1,0:T(8,128)S(1)} custom-call(bf16[144,384]{1,0:T(8,128)(2,1)S(1)} %get-tuple-element.15.refs_0_, bf16[144,384]{1,0:T(8,128)(2,1)S(1)} %collective-permute-done.refs_1_, bf16[144,384]{1,0:T(8,128)(2,1)S(1)} %collective-permute-done.1.refs_2_, bf16[144,384]{1,0:T(8,128)(2,1)S(1)} %collective-permute-done.2.refs_3_), custom_call_target="tpu_custom_call" | custom-call | flops 100000000 | bytes 4194304 | tf_op jit(solution)/shard_map/pallas_call | solution.py:159
  27.9 0.0 collective-permute-done.7.refs_1_
  27.9 0.0 slice-done.2
  27.9 0.0 slice-done.3
  28.0 5.5 %shard_map.70 = (f32[384,384]{1,0:T(8,128)S(1)}, f32[3,256,128]{2,1,0:T(8,128)S(1)}) custom-call(bf16[256,384]{1,0:T(8,128)(2,1)S(1)} %shard_map.68.refs_0_, bf16[256,384]{1,0:T(8,128)(2,1)S(1)} %collective-permute-done.7.refs_1_, bf16[3,3,3,384,384]{4,3,2,1,0:T(8,128)(2,1)S(1)} %bitcast.6), custom_call_target="tpu_custom_call" | custom-call | flops 3057647616 | bytes 4194304 | tf_op jit(solution)/shard_map/pallas_call | solution.py:333
  33.5 0.0 collective-permute-done.3.refs_1_
  33.5 0.0 slice-done
  33.5 0.0 slice-done.1
  33.6 4.5 %shard_map.71 = f32[1,8,8,4,384]{4,3,2,1,0:T(4,128)} custom-call(f32[320,384]{1,0:T(8,128)S(1)} %shard_map.65.refs_0_, bf16[320,384]{1,0:T(8,128)(2,1)S(1)} %collective-permute-done.3.refs_1_, f32[384,384]{1,0:T(8,128)S(1)} %get-tuple-element.23.refs_2_, f32[3,256,128]{2,1,0:T(8,128)S(1)} %get-tuple-element.24.refs_3_, bf16[3,3,3,384,384]{4,3,2,1,0:T(8,128)(2,1)S(1)} %bitcast.4), custom_call_target="tpu_custom_call" | custom-call | flops 2038431744 | bytes 4194304 | tf_op jit(solution)/shard_map/pallas_call | solution.py:346
  (2 shorter events, 0.0 us)
Async XLA Ops:
  0.7 0.9 %copy-start = (bf16[1,2,4,32,384]{4,3,2,1,0:T(8,128)(2,1)S(1)}, bf16[1,2,4,32,384]{4,3,2,1,0:T(8,128)(2,1)}, u32[]{:S(2)}) copy-start(bf16[1,2,4,32,384]{4,3,2,1,0:T(8,128)(2,1)} %param.8) | copy-start | bytes 589828
  1.6 12.0 %copy-start.1 = (bf16[1,2,4,32,384]{4,3,2,1,0:T(8,128)(2,1)S(1)}, bf16[1,2,4,32,384]{4,3,2,1,0:T(8,128)(2,1)}, u32[]{:S(2)}) copy-start(bf16[1,2,4,32,384]{4,3,2,1,0:T(8,128)(2,1)} %param.7) | copy-start | bytes 589828
  1.6 12.0 %copy-start.2 = (bf16[1,2,4,32,384]{4,3,2,1,0:T(8,128)(2,1)S(1)}, bf16[1,2,4,32,384]{4,3,2,1,0:T(8,128)(2,1)}, u32[]{:S(2)}) copy-start(bf16[1,2,4,32,384]{4,3,2,1,0:T(8,128)(2,1)} %param.6) | copy-start | bytes 589828
  1.7 7.8 %collective-permute-start.4 = (bf16[96,384]{1,0:T(8,128)(2,1)S(1)}, bf16[96,384]{1,0:T(8,128)(2,1)S(1)}, u32[]{:S(2)}, u32[]{:S(2)}) collective-permute-start(bf16[96,384]{1,0:T(8,128)(2,1)S(1)} %get-tuple-element.20), channel_id=1, source_target_pairs={{0,6},{2,4},{4,2},{6,0},{1,7},{3,5},{5,3},{7,1},{8,14},{10,12},{12... | collective-permute-start | bytes 221192 | tf_op jit(solution)/shard_map/ppermute | solution.py:308
  6.9 6.2 %collective-permute-start.5 = (bf16[96,384]{1,0:T(8,128)(2,1)S(1)}, bf16[96,384]{1,0:T(8,128)(2,1)S(1)}, u32[]{:S(2)}, u32[]{:S(2)}) collective-permute-start(bf16[96,384]{1,0:T(8,128)(2,1)S(1)} %get-tuple-element.21), channel_id=1, source_target_pairs={{0,4},{2,6},{4,0},{6,2},{1,5},{3,7},{5,1},{7,3},{8,12},{10,14},{12... | collective-permute-start | bytes 221192 | tf_op jit(solution)/shard_map/ppermute | solution.py:308
  6.9 6.2 %collective-permute-start.6 = (bf16[96,384]{1,0:T(8,128)(2,1)S(1)}, bf16[96,384]{1,0:T(8,128)(2,1)S(1)}, u32[]{:S(2)}, u32[]{:S(2)}) collective-permute-start(bf16[96,384]{1,0:T(8,128)(2,1)S(1)} %get-tuple-element.22), channel_id=1, source_target_pairs={{0,2},{2,0},{4,6},{6,4},{1,3},{3,1},{5,7},{7,5},{8,10},{10,8},{12,... | collective-permute-start | bytes 221192 | tf_op jit(solution)/shard_map/ppermute | solution.py:308
  13.1 14.8 %slice-start.2 = ((s8[7962624]{0:T(1024)(128)(4,1)}), s8[4194304]{0:T(1024)(128)(4,1)S(1)}, s32[]{:S(2)}) async-start(s8[7962624]{0:T(1024)(128)(4,1)} %bitcast.5), calls=%async_computation.2 | async-start | bytes 8388608
  13.5 14.4 %collective-permute-start.7 = (bf16[256,384]{1,0:T(8,128)(2,1)S(1)}, bf16[256,384]{1,0:T(8,128)(2,1)S(1)}, u32[]{:S(2)}, u32[]{:S(2)}) collective-permute-start(bf16[256,384]{1,0:T(8,128)(2,1)S(1)} %shard_map.69), channel_id=1, source_target_pairs={{0,1},{1,0},{2,3},{3,2},{4,5},{5,4},{6,7},{7,6},{8,9},{9,8},{10,11... | collective-permute-start | bytes 589832 | tf_op jit(solution)/shard_map/ppermute | solution.py:314
  13.6 20.0 %slice-start = ((s8[7962624]{0:T(1024)(128)(4,1)}), s8[4194304]{0:T(1024)(128)(4,1)S(1)}, s32[]{:S(2)}) async-start(s8[7962624]{0:T(1024)(128)(4,1)} %bitcast.3), calls=%async_computation | async-start | bytes 8388608
  13.6 14.4 %slice-start.3 = ((s8[7962624]{0:T(1024)(128)(4,1)}), s8[3768320]{0:T(1024)(128)(4,1)S(1)}, s32[]{:S(2)}) async-start(s8[7962624]{0:T(1024)(128)(4,1)} %bitcast.5), calls=%async_computation.3 | async-start | bytes 7536640
  13.6 19.9 %slice-start.1 = ((s8[7962624]{0:T(1024)(128)(4,1)}), s8[3768320]{0:T(1024)(128)(4,1)S(1)}, s32[]{:S(2)}) async-start(s8[7962624]{0:T(1024)(128)(4,1)} %bitcast.3), calls=%async_computation.1 | async-start | bytes 7536640
  13.9 7.9 %collective-permute-start = (bf16[144,384]{1,0:T(8,128)(2,1)S(1)}, bf16[144,384]{1,0:T(8,128)(2,1)S(1)}, u32[]{:S(2)}, u32[]{:S(2)}) collective-permute-start(bf16[144,384]{1,0:T(8,128)(2,1)S(1)} %get-tuple-element.16), channel_id=1, source_target_pairs={{0,6},{2,4},{4,2},{6,0},{1,7},{3,5},{5,3},{7,1},{8,14},{10,12},{12... | collective-permute-start | bytes 331784 | tf_op jit(solution)/shard_map/ppermute | solution.py:308
  16.7 10.2 %collective-permute-start.1 = (bf16[144,384]{1,0:T(8,128)(2,1)S(1)}, bf16[144,384]{1,0:T(8,128)(2,1)S(1)}, u32[]{:S(2)}, u32[]{:S(2)}) collective-permute-start(bf16[144,384]{1,0:T(8,128)(2,1)S(1)} %get-tuple-element.17), channel_id=1, source_target_pairs={{0,4},{2,6},{4,0},{6,2},{1,5},{3,7},{5,1},{7,3},{8,12},{10,14},{12... | collective-permute-start | bytes 331784 | tf_op jit(solution)/shard_map/ppermute | solution.py:308
  16.7 10.2 %collective-permute-start.2 = (bf16[144,384]{1,0:T(8,128)(2,1)S(1)}, bf16[144,384]{1,0:T(8,128)(2,1)S(1)}, u32[]{:S(2)}, u32[]{:S(2)}) collective-permute-start(bf16[144,384]{1,0:T(8,128)(2,1)S(1)} %get-tuple-element.18), channel_id=1, source_target_pairs={{0,2},{2,0},{4,6},{6,4},{1,3},{3,1},{5,7},{7,5},{8,10},{10,8},{12,... | collective-permute-start | bytes 331784 | tf_op jit(solution)/shard_map/ppermute | solution.py:308
  27.3 6.2 %collective-permute-start.3 = (bf16[320,384]{1,0:T(8,128)(2,1)S(1)}, bf16[320,384]{1,0:T(8,128)(2,1)S(1)}, u32[]{:S(2)}, u32[]{:S(2)}) collective-permute-start(bf16[320,384]{1,0:T(8,128)(2,1)S(1)} %shard_map.66), channel_id=1, source_target_pairs={{0,1},{1,0},{2,3},{3,2},{4,5},{5,4},{6,7},{7,6},{8,9},{9,8},{10,11... | collective-permute-start | bytes 737288 | tf_op jit(solution)/shard_map/ppermute | solution.py:314

commit v5 on v4

--- a/solution.py
+++ b/solution.py
@@ -13,6 +13,7 @@
 VMEM = pl.BlockSpec(memory_space=pltpu.VMEM)
 SMEM = pl.BlockSpec(memory_space=pltpu.SMEM)
 LANES = 128
+EARLY, LATE = (0,), (1, 2)
 STEPS = {4: (3, 2, 1)}
 
 
@@ -178,8 +179,9 @@
             count = size - p * frames
             for at_lane, lane in lanes(target.shape[2]):
                 value = full[at_lane, pl.ds(a + p * frames, count), :]
-                value = jnp.where(place[:count] < frames - a, value, 0.0).astype(BF16)
-                target[p, 0:count, lane] = value
+                if a:
+                    value = jnp.where(place[:count] < frames - a, value, 0.0)
+                target[p, 0:count, lane] = value.astype(BF16)
 
 
 def tap(shifts, r, c, cols, rows, frames):
@@ -195,8 +197,8 @@
     )
 
 
-def taps_of(shifts, weights, cols, rows, frames):
-    order = [(r, c) for r in range(3) for c in range(3)]
+def taps_of(shifts, weights, cols, rows, frames, row_taps=(0, 1, 2)):
+    order = [(r, c) for r in row_taps for c in range(3)]
     moved = jnp.concatenate([tap(shifts, r, c, cols, rows, frames) for r, c in order], axis=1)
     mixed = jnp.concatenate([weights[2 - r, 2 - c] for r, c in order], axis=1)
     return moved, mixed
@@ -205,7 +207,7 @@
 def first_kernel(dims, *refs):
     time_devs, row_devs, frame_dev, row_dev, col_dev = dims
     pieces, weight_ref = refs[:row_devs], refs[row_devs]
-    acc_ref, mid_ref, full, shifts = refs[row_devs + 1 :]
+    acc_ref, mid_ref, last_ref, full, shifts = refs[row_devs + 1 :]
     frames, rows = time_devs * frame_dev, row_devs * row_dev
     plane, pitch, tall = rows * frames, (rows + 2) * frames, row_dev * frames
     for w in range(col_dev + 4):
@@ -219,16 +221,26 @@
                     w * tall : (w + 1) * tall, lane
                 ].astype(F32)
     full[:, (col_dev + 4) * pitch :, :] = jnp.zeros((full.shape[0], frames, LANES), F32)
-    spread(full, [shifts.at[a] for a in range(3)], col_dev + 4, rows, frames)
+    spread(full, [shifts.at[0], shifts.at[1], last_ref], col_dev + 4, rows, frames)
     for w in range(col_dev):
         start = (w + 2) * pitch + frames
         mid_ref[:, w * plane : (w + 1) * plane, :] = full[:, start : start + plane, :]
     acc_ref[...] = jnp.zeros_like(acc_ref)
 
-    @pl.loop(0, 3)
+    @pl.loop(0, 2)
     def _(a):
         moved, mixed = taps_of(shifts.at[a], weight_ref.at[2 - a], col_dev + 2, rows, frames)
         acc_ref[...] += dot_last(moved, mixed)
+
+    moved, mixed = taps_of(last_ref, weight_ref.at[0], col_dev + 2, rows, frames, EARLY)
+    acc_ref[...] += dot_last(moved, mixed)
+
+
+def last_tap_kernel(dims, cols, acc_in, shifts, weight_ref, acc_ref):
+    time_devs, row_devs, frame_dev, row_dev, _ = dims
+    frames, rows = time_devs * frame_dev, row_devs * row_dev
+    moved, mixed = taps_of(shifts, weight_ref.at[0], cols, rows, frames, LATE)
+    acc_ref[...] = acc_in[...] + dot_last(moved, mixed)
 
 
 def second_kernel(dims, cols_all, *refs):
@@ -330,19 +342,27 @@
     cot = for_rows(over_tm(cot), (2,), False)
     hid = pack([hidden[0], latents[0]], lengths, (1, 0), False, time_devs)
     hid = for_rows(over_tm(hid), (1, 0), True)
-    acc, mid = kernel_call(
+    acc, mid, moved = kernel_call(
         functools.partial(first_kernel, dims),
         [
             jax.ShapeDtypeStruct((wide, channels), F32),
             jax.ShapeDtypeStruct((parts, narrow, LANES), F32),
+            jax.ShapeDtypeStruct((2, (col_dev + 4) * pitch, channels), BF16),
         ],
         [VMEM] * (row_devs + 1),
         [
             part_rows((col_dev + 4) * pitch + frames),
-            pltpu.VMEM((3, 2, (col_dev + 4) * pitch, channels), BF16),
+            pltpu.VMEM((2, 2, (col_dev + 4) * pitch, channels), BF16),
         ],
         3 * mac * wide,
     )(*cot, conv_two)
+    acc = kernel_call(
+        functools.partial(last_tap_kernel, dims, col_dev + 2),
+        jax.ShapeDtypeStruct((wide, channels), F32),
+        [VMEM] * 3,
+        [],
+        mac * wide,
+    )(acc, moved, conv_two)
     return kernel_call(
         functools.partial(second_kernel, dims, cols),
         jax.ShapeDtypeStruct((1, frames, rows, col_dev, channels), F32),

time: 38.2 us -> 38.4 us (level)
    pallas_call x0 -> x1, Pallas kernels: none -> 1.1 us  [on_device(): kernel_call(functools.partial(last_tap_kernel, dims, col_dev + 2), jax.Sh...]
    pallas_call x1, Pallas kernels: 5.55 us -> 4.63 us  [on_device(): kernel_call(functools.partial(first_kernel, dims), [jax.ShapeDtypeStruct(...]
where the time goes in v5:
time: 38.4 us; the launch traced here: 38.2 us
  waiting for transfers between devices  13.8 us (36%)
  Pallas kernels  12.2 us (32%)
  starting transfers between devices  10.4 us (27%)
  local copies, waits for them, and re-layouts  0.95 us (2%)
  between operations  0.85 us (2%)
    ppermute x6, waiting for transfers between devices, over_tm(): out.append(lax.ppermute(windows[step + 1], 'tm', pairs))  13.8 us
    ppermute x6, starting transfers between devices, over_tm(): out.append(lax.ppermute(windows[step + 1], 'tm', pairs))  10.2 us
    pallas_call x1, Pallas kernels, on_device(): kernel_call(functools.partial(first_kernel, dims), [jax.ShapeDtypeStruct(...  4.63 us
    pallas_call x1, Pallas kernels, on_device(): kernel_call(functools.partial(second_kernel, dims, cols), jax.ShapeDtypeS...  4.49 us
    pallas_call x4, Pallas kernels, share(): kernel_call(functools.partial(share_kernel, dims, halos, own), [shape] *...  1.63 us
    pallas_call x1, Pallas kernels, on_device(): kernel_call(functools.partial(last_tap_kernel, dims, col_dev + 2), jax.Sh...  1.1 us
    unnamed x14, local copies, waits for them, and re-layouts  0.95 us
  transfers between devices with their start and end apart: 8, of which 4 were waited for; matrix products, arithmetic and copies ran while one was open for 0% of the time, Pallas kernels for 19%

profile of v5, /device:TPU:0, one launch (start us, length us, event | category | flops | bytes accessed | tf_op | source)
XLA Modules:
  0.0 38.2 jit_solution(15782957779208818920)
XLA Ops:
  0.7 0.0 copy-start
  0.7 0.9 %copy-done = bf16[1,2,4,32,384]{4,3,2,1,0:T(8,128)(2,1)S(1)} copy-done((bf16[1,2,4,32,384]{4,3,2,1,0:T(8,128)(2,1)S(1)}, bf16[1,2,4,32,384]{4,3,2,1,0:T(8,128)(2,1)}, u32[]{:S(2)}) %copy-start) | copy-done | bytes 196632
  1.6 0.0 copy-start.1
  1.6 0.0 copy-start.2
  1.6 0.1 shard_map.67
  1.7 5.1 %collective-permute-start.4 = (bf16[96,384]{1,0:T(8,128)(2,1)S(1)}, bf16[96,384]{1,0:T(8,128)(2,1)S(1)}, u32[]{:S(2)}, u32[]{:S(2)}) collective-permute-start(bf16[96,384]{1,0:T(8,128)(2,1)S(1)} %get-tuple-element.21), channel_id=1, source_target_pairs={{0,6},{2,4},{4,2},{6,0},{1,7},{3,5},{5,3},{7,1},{8,14},{10,12},{12... | collective-permute-start | bytes 221192 | tf_op jit(solution)/shard_map/ppermute | solution.py:320
  6.9 0.0 collective-permute-start.5
  6.9 0.6 %collective-permute-start.6 = (bf16[96,384]{1,0:T(8,128)(2,1)S(1)}, bf16[96,384]{1,0:T(8,128)(2,1)S(1)}, u32[]{:S(2)}, u32[]{:S(2)}) collective-permute-start(bf16[96,384]{1,0:T(8,128)(2,1)S(1)} %get-tuple-element.23), channel_id=1, source_target_pairs={{0,2},{2,0},{4,6},{6,4},{1,3},{3,1},{5,7},{7,5},{8,10},{10,8},{12,... | collective-permute-start | bytes 221192 | tf_op jit(solution)/shard_map/ppermute | solution.py:320
  7.5 2.0 %collective-permute-done.4.refs_1_ = bf16[96,384]{1,0:T(8,128)(2,1)S(1)} collective-permute-done((bf16[96,384]{1,0:T(8,128)(2,1)S(1)}, bf16[96,384]{1,0:T(8,128)(2,1)S(1)}, u32[]{:S(2)}, u32[]{:S(2)}) %collective-permute-start.4) | collective-permute-done | bytes 73760 | tf_op jit(solution)/shard_map/ppermute | solution.py:320
  9.5 3.5 %collective-permute-done.5.refs_2_ = bf16[96,384]{1,0:T(8,128)(2,1)S(1)} collective-permute-done((bf16[96,384]{1,0:T(8,128)(2,1)S(1)}, bf16[96,384]{1,0:T(8,128)(2,1)S(1)}, u32[]{:S(2)}, u32[]{:S(2)}) %collective-permute-start.5) | collective-permute-done | bytes 73760 | tf_op jit(solution)/shard_map/ppermute | solution.py:320
  13.1 0.0 collective-permute-done.6.refs_3_
  13.1 0.0 slice-start
  13.1 0.4 shard_map.69
  13.5 0.1 collective-permute-start.7
  13.6 0.0 copy-done.1
  13.6 0.0 copy-done.2
  13.6 0.0 slice-start.1
  13.6 0.2 shard_map.64
  13.8 2.8 %collective-permute-start = (bf16[144,384]{1,0:T(8,128)(2,1)S(1)}, bf16[144,384]{1,0:T(8,128)(2,1)S(1)}, u32[]{:S(2)}, u32[]{:S(2)}) collective-permute-start(bf16[144,384]{1,0:T(8,128)(2,1)S(1)} %get-tuple-element.17), channel_id=1, source_target_pairs={{0,6},{2,4},{4,2},{6,0},{1,7},{3,5},{5,3},{7,1},{8,14},{10,12},{12... | collective-permute-start | bytes 331784 | tf_op jit(solution)/shard_map/ppermute | solution.py:320
  16.6 0.0 collective-permute-start.1
  16.6 1.7 %collective-permute-start.2 = (bf16[144,384]{1,0:T(8,128)(2,1)S(1)}, bf16[144,384]{1,0:T(8,128)(2,1)S(1)}, u32[]{:S(2)}, u32[]{:S(2)}) collective-permute-start(bf16[144,384]{1,0:T(8,128)(2,1)S(1)} %get-tuple-element.19), channel_id=1, source_target_pairs={{0,2},{2,0},{4,6},{6,4},{1,3},{3,1},{5,7},{7,5},{8,10},{10,8},{12,... | collective-permute-start | bytes 331784 | tf_op jit(solution)/shard_map/ppermute | solution.py:320
  18.3 0.3 shard_map.68.refs_0_
  18.7 3.1 %collective-permute-done.refs_1_ = bf16[144,384]{1,0:T(8,128)(2,1)S(1)} collective-permute-done((bf16[144,384]{1,0:T(8,128)(2,1)S(1)}, bf16[144,384]{1,0:T(8,128)(2,1)S(1)}, u32[]{:S(2)}, u32[]{:S(2)}) %collective-permute-start) | collective-permute-done | bytes 110624 | tf_op jit(solution)/shard_map/ppermute | solution.py:320
  21.7 5.1 %collective-permute-done.1.refs_2_ = bf16[144,384]{1,0:T(8,128)(2,1)S(1)} collective-permute-done((bf16[144,384]{1,0:T(8,128)(2,1)S(1)}, bf16[144,384]{1,0:T(8,128)(2,1)S(1)}, u32[]{:S(2)}, u32[]{:S(2)}) %collective-permute-start.1) | collective-permute-done | bytes 110624 | tf_op jit(solution)/shard_map/ppermute | solution.py:320
  26.9 0.0 collective-permute-done.2.refs_3_
  26.9 0.4 %shard_map.66 = bf16[320,384]{1,0:T(8,128)(2,1)S(1)} custom-call(bf16[144,384]{1,0:T(8,128)(2,1)S(1)} %get-tuple-element.16.refs_0_, bf16[144,384]{1,0:T(8,128)(2,1)S(1)} %collective-permute-done.refs_1_, bf16[144,384]{1,0:T(8,128)(2,1)S(1)} %collective-permute-done.1.refs_2_, bf16[144,384]{1,0:T(8,128)(2,1)S(1)} %collective-permute-done.2.refs_3_), custom_call_target="tpu_custom_call" | custom-call | flops 100000000 | bytes 4194304 | tf_op jit(solution)/shard_map/pallas_call | solution.py:160
  27.3 0.1 collective-permute-start.3
  27.4 0.0 slice-start.2
  27.4 0.5 %shard_map.65.refs_0_ = f32[320,384]{1,0:T(8,128)S(1)} custom-call(bf16[144,384]{1,0:T(8,128)(2,1)S(1)} %get-tuple-element.16.refs_0_, bf16[144,384]{1,0:T(8,128)(2,1)S(1)} %collective-permute-done.refs_1_, bf16[144,384]{1,0:T(8,128)(2,1)S(1)} %collective-permute-done.1.refs_2_, bf16[144,384]{1,0:T(8,128)(2,1)S(1)} %collective-permute-done.2.refs_3_), custom_call_target="tpu_custom_call" | custom-call | flops 100000000 | bytes 4194304 | tf_op jit(solution)/shard_map/pallas_call | solution.py:160
  27.9 0.0 slice-start.3
  27.9 0.0 collective-permute-done.7.refs_1_
  27.9 0.0 slice-done
  27.9 0.0 slice-done.1
  28.0 4.6 %shard_map.70 = (f32[384,384]{1,0:T(8,128)S(1)}, f32[3,256,128]{2,1,0:T(8,128)S(1)}, bf16[2,640,384]{2,1,0:T(8,128)(2,1)S(1)}) custom-call(bf16[256,384]{1,0:T(8,128)(2,1)S(1)} %shard_map.68.refs_0_, bf16[256,384]{1,0:T(8,128)(2,1)S(1)} %collective-permute-done.7.refs_1_, bf16[3,3,3,384,384]{4,3,2,1,0:T(8,128)(2,1)S(1)} %bitcast.4), custom_call_target="tpu_custom_call" | custom-call | flops 3057647616 | bytes 4194304 | tf_op jit(solution)/shard_map/pallas_call | solution.py:345
  32.6 1.1 %shard_map.71.refs_2_ = f32[384,384]{1,0:T(8,128)S(1)} custom-call(f32[384,384]{1,0:T(8,128)S(1)} %get-tuple-element.24.acc_in, bf16[2,640,384]{2,1,0:T(8,128)(2,1)S(1)} %get-tuple-element.25.shifts, bf16[3,3,3,384,384]{4,3,2,1,0:T(8,128)(2,1)S(1)} %bitcast.4), custom_call_target="tpu_custom_call" | custom-call | flops 1019215872 | bytes 4194304 | tf_op jit(solution)/shard_map/pallas_call | solution.py:359
  33.7 0.0 collective-permute-done.3.refs_1_
  33.7 0.0 slice-done.2
  33.7 0.0 slice-done.3
  33.7 4.5 %shard_map.72 = f32[1,8,8,4,384]{4,3,2,1,0:T(4,128)} custom-call(f32[320,384]{1,0:T(8,128)S(1)} %shard_map.65.refs_0_, bf16[320,384]{1,0:T(8,128)(2,1)S(1)} %collective-permute-done.3.refs_1_, f32[384,384]{1,0:T(8,128)S(1)} %shard_map.71.refs_2_, f32[3,256,128]{2,1,0:T(8,128)S(1)} %get-tuple-element.26.refs_3_, bf16[3,3,3,384,384]{4,3,2,1,0:T(8,128)(2,1)S(1)} %bitcast.6), custom_call_target="tpu_custom_call" | custom-call | flops 2038431744 | bytes 4194304 | tf_op jit(solution)/shard_map/pallas_call | solution.py:366
  (2 shorter events, 0.0 us)
Async XLA Ops:
  0.7 0.9 %copy-start = (bf16[1,2,4,32,384]{4,3,2,1,0:T(8,128)(2,1)S(1)}, bf16[1,2,4,32,384]{4,3,2,1,0:T(8,128)(2,1)}, u32[]{:S(2)}) copy-start(bf16[1,2,4,32,384]{4,3,2,1,0:T(8,128)(2,1)} %param.8) | copy-start | bytes 589828
  1.6 12.0 %copy-start.1 = (bf16[1,2,4,32,384]{4,3,2,1,0:T(8,128)(2,1)S(1)}, bf16[1,2,4,32,384]{4,3,2,1,0:T(8,128)(2,1)}, u32[]{:S(2)}) copy-start(bf16[1,2,4,32,384]{4,3,2,1,0:T(8,128)(2,1)} %param.7) | copy-start | bytes 589828
  1.6 12.0 %copy-start.2 = (bf16[1,2,4,32,384]{4,3,2,1,0:T(8,128)(2,1)S(1)}, bf16[1,2,4,32,384]{4,3,2,1,0:T(8,128)(2,1)}, u32[]{:S(2)}) copy-start(bf16[1,2,4,32,384]{4,3,2,1,0:T(8,128)(2,1)} %param.6) | copy-start | bytes 589828
  1.7 7.8 %collective-permute-start.4 = (bf16[96,384]{1,0:T(8,128)(2,1)S(1)}, bf16[96,384]{1,0:T(8,128)(2,1)S(1)}, u32[]{:S(2)}, u32[]{:S(2)}) collective-permute-start(bf16[96,384]{1,0:T(8,128)(2,1)S(1)} %get-tuple-element.21), channel_id=1, source_target_pairs={{0,6},{2,4},{4,2},{6,0},{1,7},{3,5},{5,3},{7,1},{8,14},{10,12},{12... | collective-permute-start | bytes 221192 | tf_op jit(solution)/shard_map/ppermute | solution.py:320
  6.9 6.2 %collective-permute-start.5 = (bf16[96,384]{1,0:T(8,128)(2,1)S(1)}, bf16[96,384]{1,0:T(8,128)(2,1)S(1)}, u32[]{:S(2)}, u32[]{:S(2)}) collective-permute-start(bf16[96,384]{1,0:T(8,128)(2,1)S(1)} %get-tuple-element.22), channel_id=1, source_target_pairs={{0,4},{2,6},{4,0},{6,2},{1,5},{3,7},{5,1},{7,3},{8,12},{10,14},{12... | collective-permute-start | bytes 221192 | tf_op jit(solution)/shard_map/ppermute | solution.py:320
  6.9 6.2 %collective-permute-start.6 = (bf16[96,384]{1,0:T(8,128)(2,1)S(1)}, bf16[96,384]{1,0:T(8,128)(2,1)S(1)}, u32[]{:S(2)}, u32[]{:S(2)}) collective-permute-start(bf16[96,384]{1,0:T(8,128)(2,1)S(1)} %get-tuple-element.23), channel_id=1, source_target_pairs={{0,2},{2,0},{4,6},{6,4},{1,3},{3,1},{5,7},{7,5},{8,10},{10,8},{12,... | collective-permute-start | bytes 221192 | tf_op jit(solution)/shard_map/ppermute | solution.py:320
  13.1 14.8 %slice-start = ((s8[7962624]{0:T(1024)(128)(4,1)}), s8[4194304]{0:T(1024)(128)(4,1)S(1)}, s32[]{:S(2)}) async-start(s8[7962624]{0:T(1024)(128)(4,1)} %bitcast.3), calls=%async_computation | async-start | bytes 8388608
  13.5 14.4 %collective-permute-start.7 = (bf16[256,384]{1,0:T(8,128)(2,1)S(1)}, bf16[256,384]{1,0:T(8,128)(2,1)S(1)}, u32[]{:S(2)}, u32[]{:S(2)}) collective-permute-start(bf16[256,384]{1,0:T(8,128)(2,1)S(1)} %shard_map.69), channel_id=1, source_target_pairs={{0,1},{1,0},{2,3},{3,2},{4,5},{5,4},{6,7},{7,6},{8,9},{9,8},{10,11... | collective-permute-start | bytes 589832 | tf_op jit(solution)/shard_map/ppermute | solution.py:326
  13.6 14.4 %slice-start.1 = ((s8[7962624]{0:T(1024)(128)(4,1)}), s8[3768320]{0:T(1024)(128)(4,1)S(1)}, s32[]{:S(2)}) async-start(s8[7962624]{0:T(1024)(128)(4,1)} %bitcast.3), calls=%async_computation.1 | async-start | bytes 7536640
  13.8 7.9 %collective-permute-start = (bf16[144,384]{1,0:T(8,128)(2,1)S(1)}, bf16[144,384]{1,0:T(8,128)(2,1)S(1)}, u32[]{:S(2)}, u32[]{:S(2)}) collective-permute-start(bf16[144,384]{1,0:T(8,128)(2,1)S(1)} %get-tuple-element.17), channel_id=1, source_target_pairs={{0,6},{2,4},{4,2},{6,0},{1,7},{3,5},{5,3},{7,1},{8,14},{10,12},{12... | collective-permute-start | bytes 331784 | tf_op jit(solution)/shard_map/ppermute | solution.py:320
  16.6 10.2 %collective-permute-start.1 = (bf16[144,384]{1,0:T(8,128)(2,1)S(1)}, bf16[144,384]{1,0:T(8,128)(2,1)S(1)}, u32[]{:S(2)}, u32[]{:S(2)}) collective-permute-start(bf16[144,384]{1,0:T(8,128)(2,1)S(1)} %get-tuple-element.18), channel_id=1, source_target_pairs={{0,4},{2,6},{4,0},{6,2},{1,5},{3,7},{5,1},{7,3},{8,12},{10,14},{12... | collective-permute-start | bytes 331784 | tf_op jit(solution)/shard_map/ppermute | solution.py:320
  16.6 10.2 %collective-permute-start.2 = (bf16[144,384]{1,0:T(8,128)(2,1)S(1)}, bf16[144,384]{1,0:T(8,128)(2,1)S(1)}, u32[]{:S(2)}, u32[]{:S(2)}) collective-permute-start(bf16[144,384]{1,0:T(8,128)(2,1)S(1)} %get-tuple-element.19), channel_id=1, source_target_pairs={{0,2},{2,0},{4,6},{6,4},{1,3},{3,1},{5,7},{7,5},{8,10},{10,8},{12,... | collective-permute-start | bytes 331784 | tf_op jit(solution)/shard_map/ppermute | solution.py:320
  27.3 6.4 %collective-permute-start.3 = (bf16[320,384]{1,0:T(8,128)(2,1)S(1)}, bf16[320,384]{1,0:T(8,128)(2,1)S(1)}, u32[]{:S(2)}, u32[]{:S(2)}) collective-permute-start(bf16[320,384]{1,0:T(8,128)(2,1)S(1)} %shard_map.66), channel_id=1, source_target_pairs={{0,1},{1,0},{2,3},{3,2},{4,5},{5,4},{6,7},{7,6},{8,9},{9,8},{10,11... | collective-permute-start | bytes 737288 | tf_op jit(solution)/shard_map/ppermute | solution.py:326
  27.4 6.3 %slice-start.2 = ((s8[7962624]{0:T(1024)(128)(4,1)}), s8[4194304]{0:T(1024)(128)(4,1)S(1)}, s32[]{:S(2)}) async-start(s8[7962624]{0:T(1024)(128)(4,1)} %bitcast.5), calls=%async_computation.2 | async-start | bytes 8388608
  27.9 5.8 %slice-start.3 = ((s8[7962624]{0:T(1024)(128)(4,1)}), s8[3768320]{0:T(1024)(128)(4,1)S(1)}, s32[]{:S(2)}) async-start(s8[7962624]{0:T(1024)(128)(4,1)} %bitcast.5), calls=%async_computation.3 | async-start | bytes 7536640

commit v6 on v5

--- a/solution.py
+++ b/solution.py
@@ -13,7 +13,7 @@
 VMEM = pl.BlockSpec(memory_space=pltpu.VMEM)
 SMEM = pl.BlockSpec(memory_space=pltpu.SMEM)
 LANES = 128
-EARLY, LATE = (0,), (1, 2)
+EARLY, LATE = (0, 1), (2,)
 STEPS = {4: (3, 2, 1)}
 
 
@@ -171,17 +171,16 @@
     return [me] + [source(me) for _, _, source in pairing(row_devs)]
 
 
-def spread(full, targets, cols, rows, frames):
+def spread(full, target, a, cols, rows, frames):
     size = cols * (rows + 2) * frames
     place = lax.rem(lax.broadcasted_iota(jnp.int32, (size, LANES), 0), frames)
-    for a, target in enumerate(targets):
-        for p in range(2):
-            count = size - p * frames
-            for at_lane, lane in lanes(target.shape[2]):
-                value = full[at_lane, pl.ds(a + p * frames, count), :]
-                if a:
-                    value = jnp.where(place[:count] < frames - a, value, 0.0)
-                target[p, 0:count, lane] = value.astype(BF16)
+    for p in range(2):
+        count = size - p * frames
+        for at_lane, lane in lanes(target.shape[2]):
+            value = full[at_lane, pl.ds(a + p * frames, count), :]
+            if a:
+                value = jnp.where(place[:count] < frames - a, value, 0.0)
+            target[p, 0:count, lane] = value.astype(BF16)
 
 
 def tap(shifts, r, c, cols, rows, frames):
@@ -207,7 +206,7 @@
 def first_kernel(dims, *refs):
     time_devs, row_devs, frame_dev, row_dev, col_dev = dims
     pieces, weight_ref = refs[:row_devs], refs[row_devs]
-    acc_ref, mid_ref, last_ref, full, shifts = refs[row_devs + 1 :]
+    acc_ref, mid_ref, last_ref, full, *shifts = refs[row_devs + 1 :]
     frames, rows = time_devs * frame_dev, row_devs * row_dev
     plane, pitch, tall = rows * frames, (rows + 2) * frames, row_dev * frames
     for w in range(col_dev + 4):
@@ -221,19 +220,18 @@
                     w * tall : (w + 1) * tall, lane
                 ].astype(F32)
     full[:, (col_dev + 4) * pitch :, :] = jnp.zeros((full.shape[0], frames, LANES), F32)
-    spread(full, [shifts.at[0], shifts.at[1], last_ref], col_dev + 4, rows, frames)
     for w in range(col_dev):
         start = (w + 2) * pitch + frames
         mid_ref[:, w * plane : (w + 1) * plane, :] = full[:, start : start + plane, :]
-    acc_ref[...] = jnp.zeros_like(acc_ref)
-
-    @pl.loop(0, 2)
-    def _(a):
-        moved, mixed = taps_of(shifts.at[a], weight_ref.at[2 - a], col_dev + 2, rows, frames)
-        acc_ref[...] += dot_last(moved, mixed)
-
-    moved, mixed = taps_of(last_ref, weight_ref.at[0], col_dev + 2, rows, frames, EARLY)
-    acc_ref[...] += dot_last(moved, mixed)
+    shifts.append(last_ref)
+    for a in range(3):
+        spread(full, shifts[a], a, col_dev + 4, rows, frames)
+        row_taps = (0, 1, 2) if a < 2 else EARLY
+        moved, mixed = taps_of(
+            shifts[a], weight_ref.at[2 - a], col_dev + 2, rows, frames, row_taps
+        )
+        part = dot_last(moved, mixed)
+        acc_ref[...] = acc_ref[...] + part if a else part
 
 
 def last_tap_kernel(dims, cols, acc_in, shifts, weight_ref, acc_ref):
@@ -246,7 +244,7 @@
 def second_kernel(dims, cols_all, *refs):
     time_devs, row_devs, frame_dev, row_dev, col_dev = dims
     pieces, acc_ref, mid_ref, weight_ref, out_ref = refs[:row_devs], *refs[row_devs : row_devs + 4]
-    slopes, full, shifts, grad = refs[row_devs + 4 :]
+    slopes, full, grad, *shifts = refs[row_devs + 4 :]
     frames, rows = time_devs * frame_dev, row_devs * row_dev
     plane, pitch, tall = rows * frames, (rows + 2) * frames, row_dev * frames
     sizes = window_rows((1, 0), tall, col_dev)
@@ -270,14 +268,11 @@
                 value = acc_ref[pl.ds(here, tall), lane] * slope(at, w * tall, lane)
                 full[at_lane, pl.ds(start, tall), :] = jnp.where(inside, value, 0.0)
     full[:, (col_dev + 2) * pitch :, :] = jnp.zeros((full.shape[0], frames, LANES), F32)
-    spread(full, [shifts.at[a] for a in range(3)], col_dev + 2, rows, frames)
-    grad[...] = jnp.zeros_like(grad)
-
-    @pl.loop(0, 3)
-    def _(a):
-        moved, mixed = taps_of(shifts.at[a], weight_ref.at[2 - a], col_dev, rows, frames)
-        grad[...] += dot_last(mixed, moved)
-
+    for a in range(3):
+        spread(full, shifts[a], a, col_dev + 2, rows, frames)
+        moved, mixed = taps_of(shifts[a], weight_ref.at[2 - a], col_dev, rows, frames)
+        part = dot_last(mixed, moved)
+        grad[...] = grad[...] + part if a else part
     for w in range(col_dev):
         for at, source in enumerate(sources):
             here = pl.multiple_of(w * plane + source * tall, frames)
@@ -352,7 +347,7 @@
         [VMEM] * (row_devs + 1),
         [
             part_rows((col_dev + 4) * pitch + frames),
-            pltpu.VMEM((2, 2, (col_dev + 4) * pitch, channels), BF16),
+            *[pltpu.VMEM((2, (col_dev + 4) * pitch, channels), BF16)] * 2,
         ],
         3 * mac * wide,
     )(*cot, conv_two)
@@ -370,8 +365,8 @@
         [
             part_rows(narrow),
             part_rows((col_dev + 2) * pitch + frames),
-            pltpu.VMEM((3, 2, (col_dev + 2) * pitch, channels), BF16),
             pltpu.VMEM((channels, narrow), F32),
+            *[pltpu.VMEM((2, (col_dev + 2) * pitch, channels), BF16)] * 3,
         ],
         3 * mac * narrow,
     )(*hid, acc, mid, conv_one)

time: 38.4 us -> 36.3 us (0.945)
  Pallas kernels: 12.2 us -> 10.2 us
    pallas_call x1, Pallas kernels: 4.49 us -> 3.52 us  [on_device(): kernel_call(functools.partial(second_kernel, dims, cols), jax.ShapeDtypeS...]
    pallas_call x1, Pallas kernels: 4.63 us -> 3.99 us  [on_device(): kernel_call(functools.partial(first_kernel, dims), [jax.ShapeDtypeStruct(...]
    pallas_call x1, Pallas kernels: 1.1 us -> 0.65 us  [on_device(): kernel_call(functools.partial(last_tap_kernel, dims, col_dev + 2), jax.Sh...]
  transfers between devices with their start and end apart: 8 -> 8, of which waited for: 4 -> 4; matrix products, arithmetic and copies ran while one was open for 0% -> 0% of each run, Pallas kernels for 19% -> 17%
where the time goes in v6:
time: 36.3 us; the launch traced here: 36.2 us
  waiting for transfers between devices  13.8 us (38%)
  starting transfers between devices  10.4 us (29%)
  Pallas kernels  10.2 us (28%)
  local copies, waits for them, and re-layouts  0.95 us (3%)
  between operations  0.84 us (2%)
    ppermute x6, waiting for transfers between devices, over_tm(): out.append(lax.ppermute(windows[step + 1], 'tm', pairs))  13.8 us
    ppermute x6, starting transfers between devices, over_tm(): out.append(lax.ppermute(windows[step + 1], 'tm', pairs))  10.2 us
    pallas_call x1, Pallas kernels, on_device(): kernel_call(functools.partial(first_kernel, dims), [jax.ShapeDtypeStruct(...  3.99 us
    pallas_call x1, Pallas kernels, on_device(): kernel_call(functools.partial(second_kernel, dims, cols), jax.ShapeDtypeS...  3.52 us
    pallas_call x4, Pallas kernels, share(): kernel_call(functools.partial(share_kernel, dims, halos, own), [shape] *...  1.63 us
    unnamed x14, local copies, waits for them, and re-layouts  0.95 us
  transfers between devices with their start and end apart: 8, of which 4 were waited for; matrix products, arithmetic and copies ran while one was open for 0% of the time, Pallas kernels for 17%

profile of v6, /device:TPU:0, one launch (start us, length us, event | category | flops | bytes accessed | tf_op | source)
XLA Modules:
  0.0 36.2 jit_solution(9159865801791115483)
XLA Ops:
  0.7 0.0 copy-start
  0.7 0.9 %copy-done = bf16[1,2,4,32,384]{4,3,2,1,0:T(8,128)(2,1)S(1)} copy-done((bf16[1,2,4,32,384]{4,3,2,1,0:T(8,128)(2,1)S(1)}, bf16[1,2,4,32,384]{4,3,2,1,0:T(8,128)(2,1)}, u32[]{:S(2)}) %copy-start) | copy-done | bytes 196632
  1.6 0.0 copy-start.1
  1.6 0.0 copy-start.2
  1.6 0.1 shard_map.67
  1.7 5.1 %collective-permute-start.4 = (bf16[96,384]{1,0:T(8,128)(2,1)S(1)}, bf16[96,384]{1,0:T(8,128)(2,1)S(1)}, u32[]{:S(2)}, u32[]{:S(2)}) collective-permute-start(bf16[96,384]{1,0:T(8,128)(2,1)S(1)} %get-tuple-element.21), channel_id=1, source_target_pairs={{0,6},{2,4},{4,2},{6,0},{1,7},{3,5},{5,3},{7,1},{8,14},{10,12},{12... | collective-permute-start | bytes 221192 | tf_op jit(solution)/shard_map/ppermute | solution.py:315
  6.9 0.0 collective-permute-start.5
  6.9 0.6 %collective-permute-start.6 = (bf16[96,384]{1,0:T(8,128)(2,1)S(1)}, bf16[96,384]{1,0:T(8,128)(2,1)S(1)}, u32[]{:S(2)}, u32[]{:S(2)}) collective-permute-start(bf16[96,384]{1,0:T(8,128)(2,1)S(1)} %get-tuple-element.23), channel_id=1, source_target_pairs={{0,2},{2,0},{4,6},{6,4},{1,3},{3,1},{5,7},{7,5},{8,10},{10,8},{12,... | collective-permute-start | bytes 221192 | tf_op jit(solution)/shard_map/ppermute | solution.py:315
  7.5 2.0 %collective-permute-done.4.refs_1_ = bf16[96,384]{1,0:T(8,128)(2,1)S(1)} collective-permute-done((bf16[96,384]{1,0:T(8,128)(2,1)S(1)}, bf16[96,384]{1,0:T(8,128)(2,1)S(1)}, u32[]{:S(2)}, u32[]{:S(2)}) %collective-permute-start.4) | collective-permute-done | bytes 73760 | tf_op jit(solution)/shard_map/ppermute | solution.py:315
  9.5 3.5 %collective-permute-done.5.refs_2_ = bf16[96,384]{1,0:T(8,128)(2,1)S(1)} collective-permute-done((bf16[96,384]{1,0:T(8,128)(2,1)S(1)}, bf16[96,384]{1,0:T(8,128)(2,1)S(1)}, u32[]{:S(2)}, u32[]{:S(2)}) %collective-permute-start.5) | collective-permute-done | bytes 73760 | tf_op jit(solution)/shard_map/ppermute | solution.py:315
  13.1 0.0 collective-permute-done.6.refs_3_
  13.1 0.0 slice-start
  13.1 0.4 %shard_map.69 = bf16[256,384]{1,0:T(8,128)(2,1)S(1)} custom-call(bf16[96,384]{1,0:T(8,128)(2,1)S(1)} %get-tuple-element.20.refs_0_, bf16[96,384]{1,0:T(8,128)(2,1)S(1)} %collective-permute-done.4.refs_1_, bf16[96,384]{1,0:T(8,128)(2,1)S(1)} %collective-permute-done.5.refs_2_, bf16[96,384]{1,0:T(8,128)(2,1)S(1)} %collective-permute-done.6.refs_3_), custom_call_target="tpu_custom_call" | custom-call | flops 100000000 | bytes 4194304 | tf_op jit(solution)/shard_map/pallas_call | solution.py:160
  13.5 0.1 collective-permute-start.7
  13.6 0.0 copy-done.1
  13.6 0.0 copy-done.2
  13.6 0.0 slice-start.1
  13.6 0.2 shard_map.64
  13.8 2.8 %collective-permute-start = (bf16[144,384]{1,0:T(8,128)(2,1)S(1)}, bf16[144,384]{1,0:T(8,128)(2,1)S(1)}, u32[]{:S(2)}, u32[]{:S(2)}) collective-permute-start(bf16[144,384]{1,0:T(8,128)(2,1)S(1)} %get-tuple-element.17), channel_id=1, source_target_pairs={{0,6},{2,4},{4,2},{6,0},{1,7},{3,5},{5,3},{7,1},{8,14},{10,12},{12... | collective-permute-start | bytes 331784 | tf_op jit(solution)/shard_map/ppermute | solution.py:315
  16.6 0.0 collective-permute-start.1
  16.6 1.7 %collective-permute-start.2 = (bf16[144,384]{1,0:T(8,128)(2,1)S(1)}, bf16[144,384]{1,0:T(8,128)(2,1)S(1)}, u32[]{:S(2)}, u32[]{:S(2)}) collective-permute-start(bf16[144,384]{1,0:T(8,128)(2,1)S(1)} %get-tuple-element.19), channel_id=1, source_target_pairs={{0,2},{2,0},{4,6},{6,4},{1,3},{3,1},{5,7},{7,5},{8,10},{10,8},{12,... | collective-permute-start | bytes 331784 | tf_op jit(solution)/shard_map/ppermute | solution.py:315
  18.3 0.3 shard_map.68.refs_0_
  18.7 3.1 %collective-permute-done.refs_1_ = bf16[144,384]{1,0:T(8,128)(2,1)S(1)} collective-permute-done((bf16[144,384]{1,0:T(8,128)(2,1)S(1)}, bf16[144,384]{1,0:T(8,128)(2,1)S(1)}, u32[]{:S(2)}, u32[]{:S(2)}) %collective-permute-start) | collective-permute-done | bytes 110624 | tf_op jit(solution)/shard_map/ppermute | solution.py:315
  21.7 5.1 %collective-permute-done.1.refs_2_ = bf16[144,384]{1,0:T(8,128)(2,1)S(1)} collective-permute-done((bf16[144,384]{1,0:T(8,128)(2,1)S(1)}, bf16[144,384]{1,0:T(8,128)(2,1)S(1)}, u32[]{:S(2)}, u32[]{:S(2)}) %collective-permute-start.1) | collective-permute-done | bytes 110624 | tf_op jit(solution)/shard_map/ppermute | solution.py:315
  26.9 0.0 collective-permute-done.2.refs_3_
  26.9 0.4 %shard_map.66 = bf16[320,384]{1,0:T(8,128)(2,1)S(1)} custom-call(bf16[144,384]{1,0:T(8,128)(2,1)S(1)} %get-tuple-element.16.refs_0_, bf16[144,384]{1,0:T(8,128)(2,1)S(1)} %collective-permute-done.refs_1_, bf16[144,384]{1,0:T(8,128)(2,1)S(1)} %collective-permute-done.1.refs_2_, bf16[144,384]{1,0:T(8,128)(2,1)S(1)} %collective-permute-done.2.refs_3_), custom_call_target="tpu_custom_call" | custom-call | flops 100000000 | bytes 4194304 | tf_op jit(solution)/shard_map/pallas_call | solution.py:160
  27.3 0.1 collective-permute-start.3
  27.4 0.0 slice-start.2
  27.4 0.5 %shard_map.65.refs_0_ = f32[320,384]{1,0:T(8,128)S(1)} custom-call(bf16[144,384]{1,0:T(8,128)(2,1)S(1)} %get-tuple-element.16.refs_0_, bf16[144,384]{1,0:T(8,128)(2,1)S(1)} %collective-permute-done.refs_1_, bf16[144,384]{1,0:T(8,128)(2,1)S(1)} %collective-permute-done.1.refs_2_, bf16[144,384]{1,0:T(8,128)(2,1)S(1)} %collective-permute-done.2.refs_3_), custom_call_target="tpu_custom_call" | custom-call | flops 100000000 | bytes 4194304 | tf_op jit(solution)/shard_map/pallas_call | solution.py:160
  27.9 0.0 slice-start.3
  27.9 0.0 collective-permute-done.7.refs_1_
  27.9 0.0 slice-done
  27.9 0.0 slice-done.1
  28.0 4.0 %shard_map.70 = (f32[384,384]{1,0:T(8,128)S(1)}, f32[3,256,128]{2,1,0:T(8,128)S(1)}, bf16[2,640,384]{2,1,0:T(8,128)(2,1)S(1)}) custom-call(bf16[256,384]{1,0:T(8,128)(2,1)S(1)} %shard_map.68.refs_0_, bf16[256,384]{1,0:T(8,128)(2,1)S(1)} %collective-permute-done.7.refs_1_, bf16[3,3,3,384,384]{4,3,2,1,0:T(8,128)(2,1)S(1)} %bitcast.4), custom_call_target="tpu_custom_call" | custom-call | flops 3057647616 | bytes 4194304 | tf_op jit(solution)/shard_map/pallas_call | solution.py:340
  32.0 0.7 %shard_map.71.refs_2_ = f32[384,384]{1,0:T(8,128)S(1)} custom-call(f32[384,384]{1,0:T(8,128)S(1)} %get-tuple-element.24.acc_in, bf16[2,640,384]{2,1,0:T(8,128)(2,1)S(1)} %get-tuple-element.25.shifts, bf16[3,3,3,384,384]{4,3,2,1,0:T(8,128)(2,1)S(1)} %bitcast.4), custom_call_target="tpu_custom_call" | custom-call | flops 1019215872 | bytes 4194304 | tf_op jit(solution)/shard_map/pallas_call | solution.py:354
  32.6 0.0 collective-permute-done.3.refs_1_
  32.6 0.0 slice-done.2
  32.6 0.0 slice-done.3
  32.7 3.5 %shard_map.72 = f32[1,8,8,4,384]{4,3,2,1,0:T(4,128)} custom-call(f32[320,384]{1,0:T(8,128)S(1)} %shard_map.65.refs_0_, bf16[320,384]{1,0:T(8,128)(2,1)S(1)} %collective-permute-done.3.refs_1_, f32[384,384]{1,0:T(8,128)S(1)} %shard_map.71.refs_2_, f32[3,256,128]{2,1,0:T(8,128)S(1)} %get-tuple-element.26.refs_3_, bf16[3,3,3,384,384]{4,3,2,1,0:T(8,128)(2,1)S(1)} %bitcast.6), custom_call_target="tpu_custom_call" | custom-call | flops 2038431744 | bytes 4194304 | tf_op jit(solution)/shard_map/pallas_call | solution.py:361
  (2 shorter events, 0.0 us)
Async XLA Ops:
  0.7 0.9 %copy-start = (bf16[1,2,4,32,384]{4,3,2,1,0:T(8,128)(2,1)S(1)}, bf16[1,2,4,32,384]{4,3,2,1,0:T(8,128)(2,1)}, u32[]{:S(2)}) copy-start(bf16[1,2,4,32,384]{4,3,2,1,0:T(8,128)(2,1)} %param.8) | copy-start | bytes 589828
  1.6 12.0 %copy-start.1 = (bf16[1,2,4,32,384]{4,3,2,1,0:T(8,128)(2,1)S(1)}, bf16[1,2,4,32,384]{4,3,2,1,0:T(8,128)(2,1)}, u32[]{:S(2)}) copy-start(bf16[1,2,4,32,384]{4,3,2,1,0:T(8,128)(2,1)} %param.7) | copy-start | bytes 589828
  1.6 12.0 %copy-start.2 = (bf16[1,2,4,32,384]{4,3,2,1,0:T(8,128)(2,1)S(1)}, bf16[1,2,4,32,384]{4,3,2,1,0:T(8,128)(2,1)}, u32[]{:S(2)}) copy-start(bf16[1,2,4,32,384]{4,3,2,1,0:T(8,128)(2,1)} %param.6) | copy-start | bytes 589828
  1.7 7.8 %collective-permute-start.4 = (bf16[96,384]{1,0:T(8,128)(2,1)S(1)}, bf16[96,384]{1,0:T(8,128)(2,1)S(1)}, u32[]{:S(2)}, u32[]{:S(2)}) collective-permute-start(bf16[96,384]{1,0:T(8,128)(2,1)S(1)} %get-tuple-element.21), channel_id=1, source_target_pairs={{0,6},{2,4},{4,2},{6,0},{1,7},{3,5},{5,3},{7,1},{8,14},{10,12},{12... | collective-permute-start | bytes 221192 | tf_op jit(solution)/shard_map/ppermute | solution.py:315
  6.9 6.2 %collective-permute-start.5 = (bf16[96,384]{1,0:T(8,128)(2,1)S(1)}, bf16[96,384]{1,0:T(8,128)(2,1)S(1)}, u32[]{:S(2)}, u32[]{:S(2)}) collective-permute-start(bf16[96,384]{1,0:T(8,128)(2,1)S(1)} %get-tuple-element.22), channel_id=1, source_target_pairs={{0,4},{2,6},{4,0},{6,2},{1,5},{3,7},{5,1},{7,3},{8,12},{10,14},{12... | collective-permute-start | bytes 221192 | tf_op jit(solution)/shard_map/ppermute | solution.py:315
  6.9 6.2 %collective-permute-start.6 = (bf16[96,384]{1,0:T(8,128)(2,1)S(1)}, bf16[96,384]{1,0:T(8,128)(2,1)S(1)}, u32[]{:S(2)}, u32[]{:S(2)}) collective-permute-start(bf16[96,384]{1,0:T(8,128)(2,1)S(1)} %get-tuple-element.23), channel_id=1, source_target_pairs={{0,2},{2,0},{4,6},{6,4},{1,3},{3,1},{5,7},{7,5},{8,10},{10,8},{12,... | collective-permute-start | bytes 221192 | tf_op jit(solution)/shard_map/ppermute | solution.py:315
  13.1 14.8 %slice-start = ((s8[7962624]{0:T(1024)(128)(4,1)}), s8[4194304]{0:T(1024)(128)(4,1)S(1)}, s32[]{:S(2)}) async-start(s8[7962624]{0:T(1024)(128)(4,1)} %bitcast.3), calls=%async_computation | async-start | bytes 8388608
  13.5 14.4 %collective-permute-start.7 = (bf16[256,384]{1,0:T(8,128)(2,1)S(1)}, bf16[256,384]{1,0:T(8,128)(2,1)S(1)}, u32[]{:S(2)}, u32[]{:S(2)}) collective-permute-start(bf16[256,384]{1,0:T(8,128)(2,1)S(1)} %shard_map.69), channel_id=1, source_target_pairs={{0,1},{1,0},{2,3},{3,2},{4,5},{5,4},{6,7},{7,6},{8,9},{9,8},{10,11... | collective-permute-start | bytes 589832 | tf_op jit(solution)/shard_map/ppermute | solution.py:321
  13.6 14.4 %slice-start.1 = ((s8[7962624]{0:T(1024)(128)(4,1)}), s8[3768320]{0:T(1024)(128)(4,1)S(1)}, s32[]{:S(2)}) async-start(s8[7962624]{0:T(1024)(128)(4,1)} %bitcast.3), calls=%async_computation.1 | async-start | bytes 7536640
  13.8 7.9 %collective-permute-start = (bf16[144,384]{1,0:T(8,128)(2,1)S(1)}, bf16[144,384]{1,0:T(8,128)(2,1)S(1)}, u32[]{:S(2)}, u32[]{:S(2)}) collective-permute-start(bf16[144,384]{1,0:T(8,128)(2,1)S(1)} %get-tuple-element.17), channel_id=1, source_target_pairs={{0,6},{2,4},{4,2},{6,0},{1,7},{3,5},{5,3},{7,1},{8,14},{10,12},{12... | collective-permute-start | bytes 331784 | tf_op jit(solution)/shard_map/ppermute | solution.py:315
  16.6 10.2 %collective-permute-start.1 = (bf16[144,384]{1,0:T(8,128)(2,1)S(1)}, bf16[144,384]{1,0:T(8,128)(2,1)S(1)}, u32[]{:S(2)}, u32[]{:S(2)}) collective-permute-start(bf16[144,384]{1,0:T(8,128)(2,1)S(1)} %get-tuple-element.18), channel_id=1, source_target_pairs={{0,4},{2,6},{4,0},{6,2},{1,5},{3,7},{5,1},{7,3},{8,12},{10,14},{12... | collective-permute-start | bytes 331784 | tf_op jit(solution)/shard_map/ppermute | solution.py:315
  16.6 10.2 %collective-permute-start.2 = (bf16[144,384]{1,0:T(8,128)(2,1)S(1)}, bf16[144,384]{1,0:T(8,128)(2,1)S(1)}, u32[]{:S(2)}, u32[]{:S(2)}) collective-permute-start(bf16[144,384]{1,0:T(8,128)(2,1)S(1)} %get-tuple-element.19), channel_id=1, source_target_pairs={{0,2},{2,0},{4,6},{6,4},{1,3},{3,1},{5,7},{7,5},{8,10},{10,8},{12,... | collective-permute-start | bytes 331784 | tf_op jit(solution)/shard_map/ppermute | solution.py:315
  27.3 5.3 %collective-permute-start.3 = (bf16[320,384]{1,0:T(8,128)(2,1)S(1)}, bf16[320,384]{1,0:T(8,128)(2,1)S(1)}, u32[]{:S(2)}, u32[]{:S(2)}) collective-permute-start(bf16[320,384]{1,0:T(8,128)(2,1)S(1)} %shard_map.66), channel_id=1, source_target_pairs={{0,1},{1,0},{2,3},{3,2},{4,5},{5,4},{6,7},{7,6},{8,9},{9,8},{10,11... | collective-permute-start | bytes 737288 | tf_op jit(solution)/shard_map/ppermute | solution.py:321
  27.4 5.2 %slice-start.2 = ((s8[7962624]{0:T(1024)(128)(4,1)}), s8[4194304]{0:T(1024)(128)(4,1)S(1)}, s32[]{:S(2)}) async-start(s8[7962624]{0:T(1024)(128)(4,1)} %bitcast.5), calls=%async_computation.2 | async-start | bytes 8388608
  27.9 4.7 %slice-start.3 = ((s8[7962624]{0:T(1024)(128)(4,1)}), s8[3768320]{0:T(1024)(128)(4,1)S(1)}, s32[]{:S(2)}) async-start(s8[7962624]{0:T(1024)(128)(4,1)} %bitcast.5), calls=%async_computation.3 | async-start | bytes 7536640

commit v7 on v6

--- a/solution.py
+++ b/solution.py
@@ -110,14 +110,20 @@
     tm = lax.axis_index("tm")
     from_tm = [tm] + [source(tm) for _, _, source in pairing(time_devs)]
     cols = col_dev + 2 * halo
-    first = pl.multiple_of(target * (col_dev * unit), unit)
+    first = pl.multiple_of(target * (col_dev * unit), col_dev * unit)
+    size = cols * unit
+    narrow = (col_dev * unit) % 16 == 0 and begin % 16 == 0 and size % 16 == 0
     for s in range(time_devs):
         for at_lane, lane in lanes(wins[s].shape[1]):
             slot = s * stage.shape[0] // time_devs + at_lane
-            stage[slot] = wins[s][begin : begin + stage.shape[1], lane].astype(F32)
+            if narrow:
+                stage[slot, 0:size, :] = wins[s][pl.ds(begin + first, size), lane].astype(F32)
+            else:
+                stage[slot] = wins[s][begin : begin + stage.shape[1], lane].astype(F32)
+            base = 0 if narrow else first
             for frame in range(frame_dev):
                 for row in range(row_dev):
-                    start = first + frame * row_dev + row
+                    start = base + frame * row_dev + row
                     place = row * frames + from_tm[s] * frame_dev + frame
                     dest[at_lane, pl.ds(place, cols, stride=row_dev * frames), :] = stage[
                         slot, pl.ds(start, cols, stride=unit), :
@@ -234,11 +240,15 @@
         acc_ref[...] = acc_ref[...] + part if a else part
 
 
-def last_tap_kernel(dims, cols, acc_in, shifts, weight_ref, acc_ref):
+def last_tap_kernel(dims, cols, acc_in, shifts, weight_ref, own_ref, acc_ref):
     time_devs, row_devs, frame_dev, row_dev, _ = dims
     frames, rows = time_devs * frame_dev, row_devs * row_dev
     moved, mixed = taps_of(shifts, weight_ref.at[0], cols, rows, frames, LATE)
     acc_ref[...] = acc_in[...] + dot_last(moved, mixed)
+    plane, tall = rows * frames, row_dev * frames
+    for w in range(cols):
+        here = pl.multiple_of(w * plane + lax.axis_index("rows") * tall, frames)
+        acc_ref[pl.ds(here, tall), :] *= own_ref[w * tall : (w + 1) * tall, :]
 
 
 def second_kernel(dims, cols_all, *refs):
@@ -265,19 +275,21 @@
             here = pl.multiple_of(w * plane + source * tall, frames)
             start = pl.multiple_of(w * pitch + frames + source * tall, frames)
             for at_lane, lane in lanes(acc_ref.shape[1]):
-                value = acc_ref[pl.ds(here, tall), lane] * slope(at, w * tall, lane)
+                value = acc_ref[pl.ds(here, tall), lane]
+                if at:
+                    value = value * slope(at, w * tall, lane)
                 full[at_lane, pl.ds(start, tall), :] = jnp.where(inside, value, 0.0)
     full[:, (col_dev + 2) * pitch :, :] = jnp.zeros((full.shape[0], frames, LANES), F32)
+    for w in range(col_dev):
+        for at, source in enumerate(sources):
+            here = pl.multiple_of(w * plane + source * tall, frames)
+            for at_lane, lane in lanes(acc_ref.shape[1]):
+                slopes[at_lane, pl.ds(here, tall), :] = slope(at, sizes[1] + w * tall, lane)
     for a in range(3):
         spread(full, shifts[a], a, col_dev + 2, rows, frames)
         moved, mixed = taps_of(shifts[a], weight_ref.at[2 - a], col_dev, rows, frames)
         part = dot_last(mixed, moved)
         grad[...] = grad[...] + part if a else part
-    for w in range(col_dev):
-        for at, source in enumerate(sources):
-            here = pl.multiple_of(w * plane + source * tall, frames)
-            for at_lane, lane in lanes(acc_ref.shape[1]):
-                slopes[at_lane, pl.ds(here, tall), :] = slope(at, sizes[1] + w * tall, lane)
     size = col_dev * plane
     for at_lane, lane in lanes(grad.shape[0]):
         full[at_lane, 0:size, :] = mid_ref[at_lane] + grad[lane, :].T * slopes[at_lane]
@@ -354,10 +366,10 @@
     acc = kernel_call(
         functools.partial(last_tap_kernel, dims, col_dev + 2),
         jax.ShapeDtypeStruct((wide, channels), F32),
-        [VMEM] * 3,
+        [VMEM] * 4,
         [],
         mac * wide,
-    )(acc, moved, conv_two)
+    )(acc, moved, conv_two, hid[0])
     return kernel_call(
         functools.partial(second_kernel, dims, cols),
         jax.ShapeDtypeStruct((1, frames, rows, col_dev, channels), F32),

time: 36.3 us -> 36.3 us (level)
  no operation moved by 1% of the time
where the time goes in v7:
time: 36.3 us; the launch traced here: 36.1 us
  waiting for transfers between devices  13.8 us (38%)
  starting transfers between devices  10.4 us (29%)
  Pallas kernels  10.1 us (28%)
  local copies, waits for them, and re-layouts  0.95 us (3%)
  between operations  0.84 us (2%)
    ppermute x6, waiting for transfers between devices, over_tm(): out.append(lax.ppermute(windows[step + 1], 'tm', pairs))  13.8 us
    ppermute x6, starting transfers between devices, over_tm(): out.append(lax.ppermute(windows[step + 1], 'tm', pairs))  10.2 us
    pallas_call x1, Pallas kernels, on_device(): kernel_call(functools.partial(first_kernel, dims), [jax.ShapeDtypeStruct(...  3.99 us
    pallas_call x1, Pallas kernels, on_device(): kernel_call(functools.partial(second_kernel, dims, cols), jax.ShapeDtypeS...  3.49 us
    pallas_call x4, Pallas kernels, share(): kernel_call(functools.partial(share_kernel, dims, halos, own), [shape] *...  1.53 us
    unnamed x14, local copies, waits for them, and re-layouts  0.95 us
    pallas_call x1, Pallas kernels, on_device(): kernel_call(functools.partial(last_tap_kernel, dims, col_dev + 2), jax.Sh...  0.73 us
  transfers between devices with their start and end apart: 8, of which 4 were waited for; matrix products, arithmetic and copies ran while one was open for 0% of the time, Pallas kernels for 17%

profile of v7, /device:TPU:0, one launch (start us, length us, event | category | flops | bytes accessed | tf_op | source)
XLA Modules:
  0.0 36.1 jit_solution(17798765669813136311)
XLA Ops:
  0.7 0.0 copy-start
  0.7 0.9 %copy-done = bf16[1,2,4,32,384]{4,3,2,1,0:T(8,128)(2,1)S(1)} copy-done((bf16[1,2,4,32,384]{4,3,2,1,0:T(8,128)(2,1)S(1)}, bf16[1,2,4,32,384]{4,3,2,1,0:T(8,128)(2,1)}, u32[]{:S(2)}) %copy-start) | copy-done | bytes 196632
  1.6 0.0 copy-start.1
  1.6 0.0 copy-start.2
  1.6 0.1 shard_map.67
  1.7 5.1 %collective-permute-start.4 = (bf16[96,384]{1,0:T(8,128)(2,1)S(1)}, bf16[96,384]{1,0:T(8,128)(2,1)S(1)}, u32[]{:S(2)}, u32[]{:S(2)}) collective-permute-start(bf16[96,384]{1,0:T(8,128)(2,1)S(1)} %get-tuple-element.21), channel_id=1, source_target_pairs={{0,6},{2,4},{4,2},{6,0},{1,7},{3,5},{5,3},{7,1},{8,14},{10,12},{12... | collective-permute-start | bytes 221192 | tf_op jit(solution)/shard_map/ppermute | solution.py:327
  6.9 0.0 collective-permute-start.5
  6.9 0.6 %collective-permute-start.6 = (bf16[96,384]{1,0:T(8,128)(2,1)S(1)}, bf16[96,384]{1,0:T(8,128)(2,1)S(1)}, u32[]{:S(2)}, u32[]{:S(2)}) collective-permute-start(bf16[96,384]{1,0:T(8,128)(2,1)S(1)} %get-tuple-element.23), channel_id=1, source_target_pairs={{0,2},{2,0},{4,6},{6,4},{1,3},{3,1},{5,7},{7,5},{8,10},{10,8},{12,... | collective-permute-start | bytes 221192 | tf_op jit(solution)/shard_map/ppermute | solution.py:327
  7.5 2.0 %collective-permute-done.4.refs_1_ = bf16[96,384]{1,0:T(8,128)(2,1)S(1)} collective-permute-done((bf16[96,384]{1,0:T(8,128)(2,1)S(1)}, bf16[96,384]{1,0:T(8,128)(2,1)S(1)}, u32[]{:S(2)}, u32[]{:S(2)}) %collective-permute-start.4) | collective-permute-done | bytes 73760 | tf_op jit(solution)/shard_map/ppermute | solution.py:327
  9.5 3.5 %collective-permute-done.5.refs_2_ = bf16[96,384]{1,0:T(8,128)(2,1)S(1)} collective-permute-done((bf16[96,384]{1,0:T(8,128)(2,1)S(1)}, bf16[96,384]{1,0:T(8,128)(2,1)S(1)}, u32[]{:S(2)}, u32[]{:S(2)}) %collective-permute-start.5) | collective-permute-done | bytes 73760 | tf_op jit(solution)/shard_map/ppermute | solution.py:327
  13.1 0.0 collective-permute-done.6.refs_3_
  13.1 0.0 slice-start
  13.1 0.3 shard_map.69
  13.4 0.1 collective-permute-start.7
  13.5 0.0 copy-done.1
  13.5 0.0 copy-done.2
  13.5 0.0 slice-start.1
  13.6 0.2 shard_map.64
  13.8 2.8 %collective-permute-start = (bf16[144,384]{1,0:T(8,128)(2,1)S(1)}, bf16[144,384]{1,0:T(8,128)(2,1)S(1)}, u32[]{:S(2)}, u32[]{:S(2)}) collective-permute-start(bf16[144,384]{1,0:T(8,128)(2,1)S(1)} %get-tuple-element.17), channel_id=1, source_target_pairs={{0,6},{2,4},{4,2},{6,0},{1,7},{3,5},{5,3},{7,1},{8,14},{10,12},{12... | collective-permute-start | bytes 331784 | tf_op jit(solution)/shard_map/ppermute | solution.py:327
  16.6 0.0 collective-permute-start.1
  16.6 1.7 %collective-permute-start.2 = (bf16[144,384]{1,0:T(8,128)(2,1)S(1)}, bf16[144,384]{1,0:T(8,128)(2,1)S(1)}, u32[]{:S(2)}, u32[]{:S(2)}) collective-permute-start(bf16[144,384]{1,0:T(8,128)(2,1)S(1)} %get-tuple-element.19), channel_id=1, source_target_pairs={{0,2},{2,0},{4,6},{6,4},{1,3},{3,1},{5,7},{7,5},{8,10},{10,8},{12,... | collective-permute-start | bytes 331784 | tf_op jit(solution)/shard_map/ppermute | solution.py:327
  18.3 0.3 shard_map.68.refs_0_
  18.6 3.1 %collective-permute-done.refs_1_ = bf16[144,384]{1,0:T(8,128)(2,1)S(1)} collective-permute-done((bf16[144,384]{1,0:T(8,128)(2,1)S(1)}, bf16[144,384]{1,0:T(8,128)(2,1)S(1)}, u32[]{:S(2)}, u32[]{:S(2)}) %collective-permute-start) | collective-permute-done | bytes 110624 | tf_op jit(solution)/shard_map/ppermute | solution.py:327
  21.7 5.1 %collective-permute-done.1.refs_2_ = bf16[144,384]{1,0:T(8,128)(2,1)S(1)} collective-permute-done((bf16[144,384]{1,0:T(8,128)(2,1)S(1)}, bf16[144,384]{1,0:T(8,128)(2,1)S(1)}, u32[]{:S(2)}, u32[]{:S(2)}) %collective-permute-start.1) | collective-permute-done | bytes 110624 | tf_op jit(solution)/shard_map/ppermute | solution.py:327
  26.9 0.0 collective-permute-done.2.refs_3_
  26.9 0.4 %shard_map.66 = bf16[320,384]{1,0:T(8,128)(2,1)S(1)} custom-call(bf16[144,384]{1,0:T(8,128)(2,1)S(1)} %get-tuple-element.16.refs_0_, bf16[144,384]{1,0:T(8,128)(2,1)S(1)} %collective-permute-done.refs_1_, bf16[144,384]{1,0:T(8,128)(2,1)S(1)} %collective-permute-done.1.refs_2_, bf16[144,384]{1,0:T(8,128)(2,1)S(1)} %collective-permute-done.2.refs_3_), custom_call_target="tpu_custom_call" | custom-call | flops 100000000 | bytes 4194304 | tf_op jit(solution)/shard_map/pallas_call | solution.py:166
  27.2 0.1 collective-permute-start.3
  27.3 0.0 slice-start.2
  27.3 0.5 %shard_map.65.own_ref.refs_0_ = f32[320,384]{1,0:T(8,128)S(1)} custom-call(bf16[144,384]{1,0:T(8,128)(2,1)S(1)} %get-tuple-element.16.refs_0_, bf16[144,384]{1,0:T(8,128)(2,1)S(1)} %collective-permute-done.refs_1_, bf16[144,384]{1,0:T(8,128)(2,1)S(1)} %collective-permute-done.1.refs_2_, bf16[144,384]{1,0:T(8,128)(2,1)S(1)} %collective-permute-done.2.refs_3_), custom_call_target="tpu_custom_call" | custom-call | flops 100000000 | bytes 4194304 | tf_op jit(solution)/shard_map/pallas_call | solution.py:166
  27.8 0.0 slice-start.3
  27.8 0.0 collective-permute-done.7.refs_1_
  27.8 0.0 slice-done
  27.9 0.0 slice-done.1
  27.9 4.0 %shard_map.70 = (f32[384,384]{1,0:T(8,128)S(1)}, f32[3,256,128]{2,1,0:T(8,128)S(1)}, bf16[2,640,384]{2,1,0:T(8,128)(2,1)S(1)}) custom-call(bf16[256,384]{1,0:T(8,128)(2,1)S(1)} %shard_map.68.refs_0_, bf16[256,384]{1,0:T(8,128)(2,1)S(1)} %collective-permute-done.7.refs_1_, bf16[3,3,3,384,384]{4,3,2,1,0:T(8,128)(2,1)S(1)} %bitcast.4), custom_call_target="tpu_custom_call" | custom-call | flops 3057647616 | bytes 4194304 | tf_op jit(solution)/shard_map/pallas_call | solution.py:352
  31.9 0.7 %shard_map.71.refs_2_ = f32[384,384]{1,0:T(8,128)S(1)} custom-call(f32[384,384]{1,0:T(8,128)S(1)} %get-tuple-element.24.acc_in, bf16[2,640,384]{2,1,0:T(8,128)(2,1)S(1)} %get-tuple-element.25.shifts, bf16[3,3,3,384,384]{4,3,2,1,0:T(8,128)(2,1)S(1)} %bitcast.4, f32[320,384]{1,0:T(8,128)S(1)} %shard_map.65.own_ref.refs_0_), custom_call_target="tpu_custom_call" | custom-call | flops 1019215872 | bytes 4194304 | tf_op jit(solution)/shard_map/pallas_call | solution.py:366
  32.6 0.0 collective-permute-done.3.refs_1_
  32.6 0.0 slice-done.2
  32.6 0.0 slice-done.3
  32.7 3.5 %shard_map.72 = f32[1,8,8,4,384]{4,3,2,1,0:T(4,128)} custom-call(f32[320,384]{1,0:T(8,128)S(1)} %shard_map.65.own_ref.refs_0_, bf16[320,384]{1,0:T(8,128)(2,1)S(1)} %collective-permute-done.3.refs_1_, f32[384,384]{1,0:T(8,128)S(1)} %shard_map.71.refs_2_, f32[3,256,128]{2,1,0:T(8,128)S(1)} %get-tuple-element.26.refs_3_, bf16[3,3,3,384,384]{4,3,2,1,0:T(8,128)(2,1)S(1)} %bitcast.6), custom_call_target="tpu_custom_call" | custom-call | flops 2038431744 | bytes 4194304 | tf_op jit(solution)/shard_map/pallas_call | solution.py:373
  (2 shorter events, 0.0 us)
Async XLA Ops:
  0.7 0.9 %copy-start = (bf16[1,2,4,32,384]{4,3,2,1,0:T(8,128)(2,1)S(1)}, bf16[1,2,4,32,384]{4,3,2,1,0:T(8,128)(2,1)}, u32[]{:S(2)}) copy-start(bf16[1,2,4,32,384]{4,3,2,1,0:T(8,128)(2,1)} %param.8) | copy-start | bytes 589828
  1.6 11.9 %copy-start.1 = (bf16[1,2,4,32,384]{4,3,2,1,0:T(8,128)(2,1)S(1)}, bf16[1,2,4,32,384]{4,3,2,1,0:T(8,128)(2,1)}, u32[]{:S(2)}) copy-start(bf16[1,2,4,32,384]{4,3,2,1,0:T(8,128)(2,1)} %param.7) | copy-start | bytes 589828
  1.6 12.0 %copy-start.2 = (bf16[1,2,4,32,384]{4,3,2,1,0:T(8,128)(2,1)S(1)}, bf16[1,2,4,32,384]{4,3,2,1,0:T(8,128)(2,1)}, u32[]{:S(2)}) copy-start(bf16[1,2,4,32,384]{4,3,2,1,0:T(8,128)(2,1)} %param.6) | copy-start | bytes 589828
  1.7 7.8 %collective-permute-start.4 = (bf16[96,384]{1,0:T(8,128)(2,1)S(1)}, bf16[96,384]{1,0:T(8,128)(2,1)S(1)}, u32[]{:S(2)}, u32[]{:S(2)}) collective-permute-start(bf16[96,384]{1,0:T(8,128)(2,1)S(1)} %get-tuple-element.21), channel_id=1, source_target_pairs={{0,6},{2,4},{4,2},{6,0},{1,7},{3,5},{5,3},{7,1},{8,14},{10,12},{12... | collective-permute-start | bytes 221192 | tf_op jit(solution)/shard_map/ppermute | solution.py:327
  6.9 6.2 %collective-permute-start.5 = (bf16[96,384]{1,0:T(8,128)(2,1)S(1)}, bf16[96,384]{1,0:T(8,128)(2,1)S(1)}, u32[]{:S(2)}, u32[]{:S(2)}) collective-permute-start(bf16[96,384]{1,0:T(8,128)(2,1)S(1)} %get-tuple-element.22), channel_id=1, source_target_pairs={{0,4},{2,6},{4,0},{6,2},{1,5},{3,7},{5,1},{7,3},{8,12},{10,14},{12... | collective-permute-start | bytes 221192 | tf_op jit(solution)/shard_map/ppermute | solution.py:327
  6.9 6.2 %collective-permute-start.6 = (bf16[96,384]{1,0:T(8,128)(2,1)S(1)}, bf16[96,384]{1,0:T(8,128)(2,1)S(1)}, u32[]{:S(2)}, u32[]{:S(2)}) collective-permute-start(bf16[96,384]{1,0:T(8,128)(2,1)S(1)} %get-tuple-element.23), channel_id=1, source_target_pairs={{0,2},{2,0},{4,6},{6,4},{1,3},{3,1},{5,7},{7,5},{8,10},{10,8},{12,... | collective-permute-start | bytes 221192 | tf_op jit(solution)/shard_map/ppermute | solution.py:327
  13.1 14.7 %slice-start = ((s8[7962624]{0:T(1024)(128)(4,1)}), s8[4194304]{0:T(1024)(128)(4,1)S(1)}, s32[]{:S(2)}) async-start(s8[7962624]{0:T(1024)(128)(4,1)} %bitcast.3), calls=%async_computation | async-start | bytes 8388608
  13.4 14.4 %collective-permute-start.7 = (bf16[256,384]{1,0:T(8,128)(2,1)S(1)}, bf16[256,384]{1,0:T(8,128)(2,1)S(1)}, u32[]{:S(2)}, u32[]{:S(2)}) collective-permute-start(bf16[256,384]{1,0:T(8,128)(2,1)S(1)} %shard_map.69), channel_id=1, source_target_pairs={{0,1},{1,0},{2,3},{3,2},{4,5},{5,4},{6,7},{7,6},{8,9},{9,8},{10,11... | collective-permute-start | bytes 589832 | tf_op jit(solution)/shard_map/ppermute | solution.py:333
  13.5 14.3 %slice-start.1 = ((s8[7962624]{0:T(1024)(128)(4,1)}), s8[3768320]{0:T(1024)(128)(4,1)S(1)}, s32[]{:S(2)}) async-start(s8[7962624]{0:T(1024)(128)(4,1)} %bitcast.3), calls=%async_computation.1 | async-start | bytes 7536640
  13.8 7.9 %collective-permute-start = (bf16[144,384]{1,0:T(8,128)(2,1)S(1)}, bf16[144,384]{1,0:T(8,128)(2,1)S(1)}, u32[]{:S(2)}, u32[]{:S(2)}) collective-permute-start(bf16[144,384]{1,0:T(8,128)(2,1)S(1)} %get-tuple-element.17), channel_id=1, source_target_pairs={{0,6},{2,4},{4,2},{6,0},{1,7},{3,5},{5,3},{7,1},{8,14},{10,12},{12... | collective-permute-start | bytes 331784 | tf_op jit(solution)/shard_map/ppermute | solution.py:327
  16.6 10.2 %collective-permute-start.1 = (bf16[144,384]{1,0:T(8,128)(2,1)S(1)}, bf16[144,384]{1,0:T(8,128)(2,1)S(1)}, u32[]{:S(2)}, u32[]{:S(2)}) collective-permute-start(bf16[144,384]{1,0:T(8,128)(2,1)S(1)} %get-tuple-element.18), channel_id=1, source_target_pairs={{0,4},{2,6},{4,0},{6,2},{1,5},{3,7},{5,1},{7,3},{8,12},{10,14},{12... | collective-permute-start | bytes 331784 | tf_op jit(solution)/shard_map/ppermute | solution.py:327
  16.6 10.2 %collective-permute-start.2 = (bf16[144,384]{1,0:T(8,128)(2,1)S(1)}, bf16[144,384]{1,0:T(8,128)(2,1)S(1)}, u32[]{:S(2)}, u32[]{:S(2)}) collective-permute-start(bf16[144,384]{1,0:T(8,128)(2,1)S(1)} %get-tuple-element.19), channel_id=1, source_target_pairs={{0,2},{2,0},{4,6},{6,4},{1,3},{3,1},{5,7},{7,5},{8,10},{10,8},{12,... | collective-permute-start | bytes 331784 | tf_op jit(solution)/shard_map/ppermute | solution.py:327
  27.2 5.4 %collective-permute-start.3 = (bf16[320,384]{1,0:T(8,128)(2,1)S(1)}, bf16[320,384]{1,0:T(8,128)(2,1)S(1)}, u32[]{:S(2)}, u32[]{:S(2)}) collective-permute-start(bf16[320,384]{1,0:T(8,128)(2,1)S(1)} %shard_map.66), channel_id=1, source_target_pairs={{0,1},{1,0},{2,3},{3,2},{4,5},{5,4},{6,7},{7,6},{8,9},{9,8},{10,11... | collective-permute-start | bytes 737288 | tf_op jit(solution)/shard_map/ppermute | solution.py:333
  27.3 5.3 %slice-start.2 = ((s8[7962624]{0:T(1024)(128)(4,1)}), s8[4194304]{0:T(1024)(128)(4,1)S(1)}, s32[]{:S(2)}) async-start(s8[7962624]{0:T(1024)(128)(4,1)} %bitcast.5), calls=%async_computation.2 | async-start | bytes 8388608
  27.8 4.8 %slice-start.3 = ((s8[7962624]{0:T(1024)(128)(4,1)}), s8[3768320]{0:T(1024)(128)(4,1)S(1)}, s32[]{:S(2)}) async-start(s8[7962624]{0:T(1024)(128)(4,1)} %bitcast.5), calls=%async_computation.3 | async-start | bytes 7536640
